TPU v7x, 512 devices: a whole 4x4x16 slice. The times are simulated.
512 devices in a mesh: blk: 64 (over z, x), scale: 8 (over y, core).
Axes of the slice: x: 4, y: 4, z: 16, core: 2. Of those that a mesh axis runs over, the one named last changes fastest.
Arguments:
- start_block: float32 [64, 524288], P(None, ('blk', 'scale')), may hold values from -90 to 90
- blocks: bfloat16 [16384, 128, 128], P(('blk', 'scale')), may hold values from -0.1875 to 0.1875
- block_column: int32 [16384], P(('blk', 'scale')), may hold values from 0 to 7
- block_target: int32 [16384], P(('blk', 'scale')), may hold values from 0 to 15, as said below
- block_count: int32 [512], P(('blk', 'scale')), may hold values from 2 to 32, as said below
- partner: int32 [524288], P(('blk', 'scale')), may hold values from 0 to 1023, as said below
- degree: int32 [524288], P(('blk', 'scale')), may hold values from 1 to 16
Outputs:
- subspace: float32 [64, 524288], P(None, ('blk', 'scale'))
- rayleigh: float32 [64, 64], replicated
Inputs may be any that keep to these rules, and one draw needn't show every extreme that they name: block_count[g] is the number of live slots of row group g; it is at least 2; some row group has all 32 slots live in every draw. In each row group, slots c < 2 have block_target of 8 or more, and all other slots have block_target below 8. Within each row group, partner is a permutation of 0 to 1023, and the pairing is mutual: if node i of group (b, s) has partner j, then node j of group (b, s xor 1) has partner i.
All inputs are finite; a program needn't handle non-finite values.
Results may differ from a plain program's by a relative error of at most 0.0011.
Values may be sent and summed in bfloat16 or wider, within the bound.
No kernel may reach another device: no remote copies, remote signals or barrier semaphores. Data moves between devices by JAX's collectives and lax.ppermute only.
A program may use at most 64 MiB of HBM per device.

v0:
```python
import jax
import jax.numpy as jnp
from jax import lax
from jax.sharding import PartitionSpec as P

ITERS = 2


FULL_PRECISION = lax.Precision.HIGHEST


def from_behind(block, axis, distance):
    devices = range(lax.axis_size(axis))
    route = [((i - distance) % len(devices), i) for i in devices]
    return lax.ppermute(block, axis, route)


def swapped(array, axis, apart):
    return lax.ppermute(array, axis, [(i, i ^ 1 << apart) for i in range(lax.axis_size(axis))])


def pick_rows(onehot, source):
    picked = jnp.einsum(
        "cr,krj->ckj", onehot.astype(jnp.bfloat16), source, preferred_element_type=jnp.float32
    )
    return picked.astype(jnp.bfloat16)


def place_rows(onehot, partial_terms):
    return jnp.einsum("cr,ckj->krj", onehot, partial_terms, precision=FULL_PRECISION)


def slot_masks(columns, targets, slot_count, row_blocks):
    live_mask = (jnp.arange(columns.shape[0]) < slot_count[0]).astype(jnp.float32)[:, None]
    onecol = (columns[:, None] == jnp.arange(row_blocks)[None, :]).astype(jnp.float32) * live_mask
    onetgt = (targets[:, None] == jnp.arange(2 * row_blocks)[None, :]).astype(
        jnp.float32
    ) * live_mask
    return (onecol, onetgt)


def forward_terms(source, weights, onecol):
    picked = pick_rows(onecol, source)
    return jnp.einsum("cki,cji->ckj", picked, weights, preferred_element_type=jnp.float32)


def backward_terms(stacked, weights, onetgt):
    picked = pick_rows(onetgt, stacked)
    return jnp.einsum("ckj,cji->cki", picked, weights, preferred_element_type=jnp.float32)


def over_slots(term_fn, slot_total, initial):
    return jax.tree.map(jnp.add, initial, term_fn(0, slot_total))


def apply_operator(
    vectors, inv_sqrt_degree, blocks, block_column, block_target, block_count, partner
):
    vector_count, node_rows = vectors.shape
    row_blocks = node_rows // 128
    scaled = (vectors * inv_sqrt_degree[None, :]).astype(jnp.bfloat16)
    own_vectors = scaled.reshape(vector_count, row_blocks, 128)
    next_vectors = from_behind(own_vectors, "blk", -1)
    stacked = jnp.concatenate([own_vectors, next_vectors], axis=1)
    onecol, onetgt = slot_masks(block_column, block_target, block_count, row_blocks)
    empty_sum = jnp.zeros((vector_count, row_blocks, 128), jnp.float32)

    def local_terms(first_slot, slot_width):
        forward = forward_terms(own_vectors, blocks, onecol)
        backward = backward_terms(stacked, blocks, onetgt)
        nearby = place_rows(onetgt[:, :row_blocks], forward) + place_rows(onecol, backward)
        return (nearby, place_rows(onetgt[:, row_blocks:], forward))

    nearby, ahead_sum = over_slots(local_terms, blocks.shape[0], (empty_sum, empty_sum))
    surface = nearby + from_behind(ahead_sum.astype(jnp.bfloat16), "blk", 1).astype(ahead_sum.dtype)
    partner_vectors = swapped(scaled, "scale", 0)
    crossed = jnp.take(partner_vectors, partner, axis=1).astype(jnp.float32)
    return vectors + inv_sqrt_degree[None, :] * (surface.reshape(vector_count, node_rows) + crossed)


def shards(start_block, blocks, block_column, block_target, block_count, partner, degree):
    inv_sqrt_degree = 1.0 / jnp.sqrt(degree.astype(jnp.float32))
    vector_count = start_block.shape[0]
    node_total = start_block.shape[1] * lax.axis_size("blk") * lax.axis_size("scale")

    def operate(vectors):
        return apply_operator(
            vectors, inv_sqrt_degree, blocks, block_column, block_target, block_count, partner
        )

    subspace = start_block
    for sweep_index in range(ITERS):
        orthonormal_images = operate(subspace)
        local_gram = jnp.dot(orthonormal_images, orthonormal_images.T, precision=FULL_PRECISION)
        gram_matrix = lax.psum(local_gram, ("blk", "scale")) / node_total
        factor = jnp.linalg.cholesky(gram_matrix)
        factor_inverse = jax.scipy.linalg.solve_triangular(
            factor, jnp.eye(vector_count, dtype=jnp.float32), lower=True
        )
        subspace = jnp.dot(factor_inverse, orthonormal_images, precision=FULL_PRECISION)
    images = operate(subspace)
    local_projection = jnp.dot(subspace, images.T, precision=FULL_PRECISION)
    rayleigh = lax.psum(local_projection, ("blk", "scale")) / node_total
    return (subspace, rayleigh)


def solution(mesh):
    return jax.shard_map(
        shards,
        mesh=mesh,
        in_specs=(
            P(None, ("blk", "scale")),
            P(("blk", "scale"), None, None),
            P(("blk", "scale")),
            P(("blk", "scale")),
            P(("blk", "scale")),
            P(("blk", "scale")),
            P(("blk", "scale")),
        ),
        out_specs=(P(None, ("blk", "scale")), P()),
        check_vma=False,
    )
```

profile of v0, /device:TPU:1, one launch (start us, length us, event | category | flops | bytes accessed | tf_op | source)
XLA Modules:
  0.0 408.4 jit_solution(9733213956229735695)
XLA Ops:
  0.6 0.8 convert_rsqrt_fusion
  1.4 1.0 fusion.136
  2.4 14.1 %collective-permute-start = (bf16[64,8,128]{2,1,0:T(8,128)(2,1)S(1)}, bf16[64,8,128]{2,1,0:T(8,128)(2,1)S(1)}, u32[]{:S(2)}, u32[]{:S(2)}) collective-permute-start(bf16[64,8,128]{2,1,0:T(8,128)(2,1)S(1)} %bitcast.141), channel_id=1, source_target_pairs={{8,0},{16,8},{24,16},{32,24},{40,32},{48,40},{56,48},{64,56},{72,6... | collective-permute-start | bytes 393224 | tf_op jit(solution)/shard_map/ppermute | solution.py:15
  17.2 0.6 copy-done.10
  17.9 0.3 fusion.83
  18.2 0.3 copy-done.15
  18.6 0.8 fusion.18
  19.4 1.2 fusion.3
  20.6 1.9 collective-permute-start.1
  22.6 2.9 collective-permute-start.2
  25.5 1.2 fusion.16
  26.8 0.6 compare_and_fusion
  27.3 0.3 fusion.33
  27.7 0.4 fusion.19
  28.2 3.2 gather_fusion
  31.6 1.9 convert_add_fusion.2
  33.5 0.7 copy-done.7
  34.2 0.4 fusion.118
  34.6 103.9 %psum.21 = f32[64,64]{0,1:T(8,128)S(1)} all-reduce(f32[64,64]{0,1:T(8,128)S(1)} %fusion.118), channel_id=1, replica_groups=mesh['blk'=64,'scale'=8] {'blk','scale'}, use_global_device_ids=true, to_apply=%region_0.0 | all-reduce | flops 4096 | bytes 32768 | tf_op jit(solution)/shard_map/psum | solution.py:95
  138.7 5.8 %cholesky.44 = f32[64,64]{1,0:T(8,128)S(1)} custom-call(f32[64,64]{1,0:T(8,128)S(1)} %fusion.60), custom_call_target="Cholesky" | custom-call | tf_op jit(solution)/shard_map/jit(cholesky)/cholesky | solution.py:96
  144.6 0.6 compare_reduce_fusion.1
  145.2 0.7 fusion.55
  145.9 4.9 %custom-call.6 = f32[1,64,64]{1,2,0:T(8,128)S(1)} custom-call(f32[1,64,64]{2,1,0:T(8,128)S(1)} %fusion.55), custom_call_target="InvertDiagBlocksLowerTriangular" | custom-call | tf_op jit(solution)/shard_map/jit(_solve_triangular)/triangular_solve | solution.py:97
  150.8 0.3 fusion.53
  151.0 0.4 multiply_convert_fusion.1
  151.5 0.6 copy-done.4
  152.1 0.3 fusion.81
  152.5 1.9 collective-permute-start.3
  154.4 2.9 collective-permute-start.5
  157.3 0.8 fusion.20
  158.1 1.2 fusion.4
  159.4 3.8 collective-permute-start.4
  163.2 1.2 fusion.13
  164.5 0.3 fusion.37
  164.8 0.4 fusion.21
  165.4 3.2 gather_fusion.1
  168.7 0.9 collective-permute-done.4
  169.6 1.9 convert_add_fusion.1
  171.5 0.7 copy-done.8
  172.2 0.4 fusion.122
  172.6 99.6 %psum.22 = f32[64,64]{0,1:T(8,128)S(1)} all-reduce(f32[64,64]{0,1:T(8,128)S(1)} %fusion.122), channel_id=1, replica_groups=mesh['blk'=64,'scale'=8] {'blk','scale'}, use_global_device_ids=true, to_apply=%region_3.7 | all-reduce | flops 4096 | bytes 32768 | tf_op jit(solution)/shard_map/psum | solution.py:95
  272.4 5.8 %cholesky.55 = f32[64,64]{1,0:T(8,128)S(1)} custom-call(f32[64,64]{1,0:T(8,128)S(1)} %fusion.58), custom_call_target="Cholesky" | custom-call | tf_op jit(solution)/shard_map/jit(cholesky)/cholesky | solution.py:96
  278.3 0.6 compare_reduce_fusion
  278.9 0.7 fusion.56
  279.6 4.9 %custom-call.7 = f32[1,64,64]{1,2,0:T(8,128)S(1)} custom-call(f32[1,64,64]{2,1,0:T(8,128)S(1)} %fusion.56), custom_call_target="InvertDiagBlocksLowerTriangular" | custom-call | tf_op jit(solution)/shard_map/jit(_solve_triangular)/triangular_solve | solution.py:97
  284.5 0.3 fusion.51
  284.7 0.4 multiply_convert_fusion
  285.2 0.7 copy-done.5
  285.9 0.3 fusion.79
  286.2 4.8 %collective-permute-start.6 = (bf16[64,8,128]{2,1,0:T(8,128)(2,1)S(1)}, bf16[64,8,128]{2,1,0:T(8,128)(2,1)S(1)}, u32[]{:S(2)}, u32[]{:S(2)}) collective-permute-start(bf16[64,8,128]{2,1,0:T(8,128)(2,1)S(1)} %bitcast.145), channel_id=1, source_target_pairs={{8,0},{16,8},{24,16},{32,24},{40,32},{48,40},{56,48},{64,56},{72,6... | collective-permute-start | bytes 393224 | tf_op jit(solution)/shard_map/ppermute | solution.py:15
  291.0 2.9 collective-permute-start.8
  293.9 0.8 fusion.22
  294.7 1.3 fusion.5
  296.0 2.1 collective-permute-start.7
  298.1 1.2 fusion.10
  299.4 0.3 fusion.41
  299.7 0.4 fusion.23
  300.3 3.2 gather_fusion.2
  303.7 2.6 collective-permute-done.7
  306.3 1.2 convert_add_fusion
  307.5 0.7 copy-done.9
  308.2 0.4 fusion.24
  308.6 99.2 %psum.23 = f32[64,64]{0,1:T(8,128)S(1)} all-reduce(f32[64,64]{0,1:T(8,128)S(1)} %fusion.24), channel_id=1, replica_groups=mesh['blk'=64,'scale'=8] {'blk','scale'}, use_global_device_ids=true, to_apply=%region_4.8 | all-reduce | flops 4096 | bytes 32768 | tf_op jit(solution)/shard_map/psum | solution.py:103
  407.7 0.7 copy.26
  (58 shorter events, 1.4 us)
Async XLA Ops:
  0.6 17.9 %copy-start = (bf16[32,128,128]{2,1,0:T(8,128)(2,1)S(1)}, bf16[32,128,128]{2,1,0:T(8,128)(2,1)}, u32[]{:S(2)}) copy-start(bf16[32,128,128]{2,1,0:T(8,128)(2,1)} %param.13) | copy-start | bytes 3145732
  2.4 24.9 %collective-permute-start = (bf16[64,8,128]{2,1,0:T(8,128)(2,1)S(1)}, bf16[64,8,128]{2,1,0:T(8,128)(2,1)S(1)}, u32[]{:S(2)}, u32[]{:S(2)}) collective-permute-start(bf16[64,8,128]{2,1,0:T(8,128)(2,1)S(1)} %bitcast.141), channel_id=1, source_target_pairs={{8,0},{16,8},{24,16},{32,24},{40,32},{48,40},{56,48},{64,56},{72,6... | collective-permute-start | bytes 393224 | tf_op jit(solution)/shard_map/ppermute | solution.py:15
  17.2 0.7 copy-start.10
  17.9 9.5 %copy-start.3 = (f32[32]{0:T(128)}, f32[32]{0:T(128)S(1)}, u32[]{:S(2)}) copy-start(f32[32]{0:T(128)S(1)} %compare_convert_fusion) | copy-start | bytes 388
  17.9 0.7 copy-start.15
  19.4 3.2 copy-start.1
  20.6 11.0 %collective-permute-start.1 = (bf16[64,8,128]{2,1,0:T(8,128)(2,1)S(1)}, bf16[64,8,128]{2,1,0:T(8,128)(2,1)S(1)}, u32[]{:S(2)}, u32[]{:S(2)}) collective-permute-start(bf16[64,8,128]{2,1,0:T(8,128)(2,1)S(1)} %fusion.3), channel_id=1, source_target_pairs={{504,0},{0,8},{8,16},{16,24},{24,32},{32,40},{40,48},{48,56},{56,6... | collective-permute-start | bytes 393224 | tf_op jit(solution)/shard_map/ppermute | solution.py:15
  22.6 4.1 %copy-start.14 = (s32[1024]{0:T(1024)S(1)}, s32[1024]{0:T(1024)}, u32[]{:S(2)}) copy-start(s32[1024]{0:T(1024)} %param.17) | copy-start | bytes 12292
  22.6 5.4 %collective-permute-start.2 = (bf16[64,1024]{1,0:T(8,128)(2,1)S(1)}, bf16[64,1024]{1,0:T(8,128)(2,1)S(1)}, u32[]{:S(2)}, u32[]{:S(2)}) collective-permute-start(bf16[64,1024]{1,0:T(8,128)(2,1)S(1)} %multiply_convert_fusion.2), channel_id=1, source_target_pairs={{0,1},{1,0},{2,3},{3,2},{4,5},{5,4},{6,7},{7,6},{8,9},{9,8},{10,11... | collective-permute-start | bytes 393224 | tf_op jit(solution)/shard_map/ppermute | solution.py:19
  33.5 0.7 copy-start.7
  151.5 0.7 copy-start.4
  151.5 0.7 copy-start.11
  152.5 12.0 %collective-permute-start.3 = (bf16[64,8,128]{2,1,0:T(8,128)(2,1)S(1)}, bf16[64,8,128]{2,1,0:T(8,128)(2,1)S(1)}, u32[]{:S(2)}, u32[]{:S(2)}) collective-permute-start(bf16[64,8,128]{2,1,0:T(8,128)(2,1)S(1)} %bitcast.148), channel_id=1, source_target_pairs={{8,0},{16,8},{24,16},{32,24},{40,32},{48,40},{56,48},{64,56},{72,6... | collective-permute-start | bytes 393224 | tf_op jit(solution)/shard_map/ppermute | solution.py:15
  154.4 10.8 %collective-permute-start.5 = (bf16[64,1024]{1,0:T(8,128)(2,1)S(1)}, bf16[64,1024]{1,0:T(8,128)(2,1)S(1)}, u32[]{:S(2)}, u32[]{:S(2)}) collective-permute-start(bf16[64,1024]{1,0:T(8,128)(2,1)S(1)} %get-tuple-element.7), channel_id=1, source_target_pairs={{0,1},{1,0},{2,3},{3,2},{4,5},{5,4},{6,7},{7,6},{8,9},{9,8},{10,11... | collective-permute-start | bytes 393224 | tf_op jit(solution)/shard_map/ppermute | solution.py:19
  159.4 5.1 %copy-start.16 = (s32[32]{0:T(128)S(1)}, s32[32]{0:T(128)}, u32[]{:S(2)}) copy-start(s32[32]{0:T(128)} %param.15) | copy-start | bytes 388
  159.4 10.3 %collective-permute-start.4 = (bf16[64,8,128]{2,1,0:T(8,128)(2,1)S(1)}, bf16[64,8,128]{2,1,0:T(8,128)(2,1)S(1)}, u32[]{:S(2)}, u32[]{:S(2)}) collective-permute-start(bf16[64,8,128]{2,1,0:T(8,128)(2,1)S(1)} %fusion.4), channel_id=1, source_target_pairs={{504,0},{0,8},{8,16},{16,24},{24,32},{32,40},{40,48},{48,56},{56,6... | collective-permute-start | bytes 393224 | tf_op jit(solution)/shard_map/ppermute | solution.py:15
  171.5 0.7 copy-start.8
  285.1 22.4 %copy-start.2 = (f32[64,1024]{1,0:T(8,128)}, f32[64,1024]{1,0:T(8,128)S(1)}, u32[]{:S(2)}) copy-start(f32[64,1024]{1,0:T(8,128)S(1)} %get-tuple-element.10) | copy-start | bytes 786436
  285.2 0.7 copy-start.5
  285.2 0.7 copy-start.12
  286.2 13.2 %collective-permute-start.6 = (bf16[64,8,128]{2,1,0:T(8,128)(2,1)S(1)}, bf16[64,8,128]{2,1,0:T(8,128)(2,1)S(1)}, u32[]{:S(2)}, u32[]{:S(2)}) collective-permute-start(bf16[64,8,128]{2,1,0:T(8,128)(2,1)S(1)} %bitcast.145), channel_id=1, source_target_pairs={{8,0},{16,8},{24,16},{32,24},{40,32},{48,40},{56,48},{64,56},{72,6... | collective-permute-start | bytes 393224 | tf_op jit(solution)/shard_map/ppermute | solution.py:15
  291.0 9.1 %collective-permute-start.8 = (bf16[64,1024]{1,0:T(8,128)(2,1)S(1)}, bf16[64,1024]{1,0:T(8,128)(2,1)S(1)}, u32[]{:S(2)}, u32[]{:S(2)}) collective-permute-start(bf16[64,1024]{1,0:T(8,128)(2,1)S(1)} %get-tuple-element.9), channel_id=1, source_target_pairs={{0,1},{1,0},{2,3},{3,2},{4,5},{5,4},{6,7},{7,6},{8,9},{9,8},{10,11... | collective-permute-start | bytes 393224 | tf_op jit(solution)/shard_map/ppermute | solution.py:19
  296.0 3.4 copy-start.17
  296.0 10.3 %collective-permute-start.7 = (bf16[64,8,128]{2,1,0:T(8,128)(2,1)S(1)}, bf16[64,8,128]{2,1,0:T(8,128)(2,1)S(1)}, u32[]{:S(2)}, u32[]{:S(2)}) collective-permute-start(bf16[64,8,128]{2,1,0:T(8,128)(2,1)S(1)} %fusion.5), channel_id=1, source_target_pairs={{504,0},{0,8},{8,16},{16,24},{24,32},{32,40},{40,48},{48,56},{56,6... | collective-permute-start | bytes 393224 | tf_op jit(solution)/shard_map/ppermute | solution.py:15
  303.5 2.7 copy-start.6
  303.5 2.7 copy-start.13
  307.5 0.7 copy-start.9
where the time goes:
time: 409 us; the launch traced here: 408 us
  blocking collectives  303 us (74%)
  starting transfers between devices  37.3 us (9%)
  other arithmetic  26.5 us (6%)
  matrix products  20.7 us (5%)
  local copies, waits for them, and re-layouts  15.8 us (4%)
    psum x2, blocking collectives, shards(): gram_matrix = lax.psum(local_gram, ('blk', 'scale')) / node_total  204 us
    psum x1, blocking collectives, shards(): rayleigh = lax.psum(local_projection, ('blk', 'scale')) / node_total  99.2 us
    ppermute x6, starting transfers between devices, from_behind(): return lax.ppermute(block, axis, route)  28.7 us
    another operation x6, other arithmetic, shards(): factor = jnp.linalg.cholesky(gram_matrix)  13 us
    dot_general x9, matrix products, place_rows(): jnp.einsum('cr,ckj->krj', onehot, partial_terms, precision=FULL_PRECISION)  12.5 us
    another operation x4, other arithmetic, shards(): jax.scipy.linalg.solve_triangular(factor, jnp.eye(vector_count, dtype=jnp...  11.1 us
    gather x6, local copies, waits for them, and re-layouts, apply_operator(): crossed = jnp.take(partner_vectors, partner, axis=1).astype(jnp.float32)  10 us
    ppermute x3, starting transfers between devices, swapped(): lax.ppermute(array, axis, [(i, i ^ 1 << apart) for i in range(lax.axis_si...  8.6 us
  transfers between devices with their start and end apart: 9, of which 2 were waited for; matrix products, arithmetic and copies ran while one was open for 6% of the time, Pallas kernels for 0%

commit v1 on v0

v1 whole, which is shorter than its diff:
```python
import functools

import jax
import jax.numpy as jnp
from jax import lax
from jax.experimental import pallas as pl
from jax.experimental.pallas import tpu as pltpu
from jax.sharding import PartitionSpec as P

BLOCK = 128
CROSS = 2
ALONG_X = 4
BOTH = ("blk", "scale")
FULL = lax.Precision.HIGHEST
F32 = jnp.float32
BF16 = jnp.bfloat16

VMEM = pl.BlockSpec(memory_space=pltpu.VMEM)
SMEM = pl.BlockSpec(memory_space=pltpu.SMEM)


def lanes(j):
    return slice(j * BLOCK, (j + 1) * BLOCK)


def times(left, right):
    return jnp.dot(left, right, preferred_element_type=F32)


def times_t(left, right, precision=None):
    return lax.dot_general(
        left, right, (((1,), (1,)), ((), ())), precision=precision, preferred_element_type=F32
    )


def fold(product, k):
    return product if product.shape[0] == k else product[:k] + product[k:]


def split(value):
    high = value.astype(BF16)
    return jnp.concatenate([high, (value - high.astype(F32)).astype(BF16)], axis=0)


def first_kernel(x_ref, degree_ref, far_ref, col_ref, tgt_ref, dinv_ref, scaled_ref, ahead_ref, s3):
    k = x_ref.shape[0]
    dinv = 1.0 / jnp.sqrt(degree_ref[...].astype(F32))
    dinv_ref[...] = dinv
    scaled = (x_ref[...] * dinv).astype(BF16)
    scaled_ref[...] = scaled
    for j in range(s3.shape[0]):
        s3[j] = scaled[:, lanes(j)]
    for c in range(CROSS):
        ahead_ref[c * BLOCK : (c + 1) * BLOCK] = far_ref[c]
        at = CROSS * BLOCK + c * k
        ahead_ref[at : at + k] = s3[col_ref[c]]
        at = CROSS * (BLOCK + k) + c * 16
        row = jnp.full((16, BLOCK), tgt_ref[c] - s3.shape[0], jnp.int32)
        ahead_ref[at : at + 16] = row.astype(F32).astype(BF16)


def near_kernel(z_ref, blocks_ref, col_ref, tgt_ref, count_ref, out_ref, s3, acc):
    rb = s3.shape[0]
    k = out_ref.shape[0]
    for j in range(rb):
        s3[j] = z_ref[:, lanes(j)]
    acc[...] = jnp.zeros_like(acc)
    count = count_ref[0]
    for c in range(CROSS, blocks_ref.shape[0]):
        live = c < count
        column, target = col_ref[c], tgt_ref[c]
        weights = blocks_ref[c]
        forward = fold(times_t(s3[column], weights), k)
        backward = fold(times(s3[target], weights), k)
        acc[jnp.where(live, target, rb)] += forward
        acc[jnp.where(live, column, rb)] += backward
    for j in range(rb):
        out_ref[:, lanes(j)] = acc[j]


def crossed_block(part_ref, partner_ref, j, k):
    nodes = partner_ref.shape[1]
    ids = lax.broadcasted_iota(jnp.int32, (nodes, BLOCK), 0)
    onehot = jnp.where(ids == partner_ref[:, lanes(j)], 1.0, 0.0).astype(BF16)
    return fold(times(part_ref[...], onehot), k)


def finish_kernel(
    first,
    near_ref,
    v_ref,
    dinv_ref,
    next_ref,
    prev_ref,
    pay_ref,
    part_ref,
    partner_ref,
    far_ref,
    col_ref,
    tgt_ref,
    y_ref,
    z_ref,
    *rest,
):
    k = v_ref.shape[0]
    rb = v_ref.shape[1] // BLOCK
    back_ref, tot, z3 = rest[-3:]
    for j in range(rb):
        tot[j] = near_ref[:, lanes(j)] + crossed_block(part_ref, partner_ref, j, k)
    places = []
    for c in range(CROSS):
        at = CROSS * (BLOCK + k) + c * 16
        place = pay_ref[at : at + 16, :].astype(F32)[0:1]
        places.append(place)
        if first:
            theirs = next_ref[:, pl.ds(pl.multiple_of((tgt_ref[c] - rb) * BLOCK, BLOCK), BLOCK)]
            at = CROSS * BLOCK + c * k
            behind = pay_ref[at : at + k]
        else:
            theirs = next_ref[:, lanes(c)]
            behind = prev_ref[:, lanes(c)]
        tot[col_ref[c]] += fold(times(theirs, far_ref[c]), k)
        landed = fold(times_t(behind, pay_ref[c * BLOCK : (c + 1) * BLOCK]), k)
        for j in range(rb):
            tot[j] += jnp.where(place == j, landed, 0.0)
    for j in range(rb):
        dinv = dinv_ref[:, lanes(j)]
        y = v_ref[:, lanes(j)] + dinv * tot[j]
        z = split(y * dinv)
        y_ref[:, lanes(j)] = y
        z_ref[:, lanes(j)] = z
        z3[j] = z
    for c in range(CROSS):
        if first:
            rest[0][:, lanes(c)] = z3[col_ref[c]]
        wanted = jnp.zeros(z3.shape[1:], F32)
        for j in range(rb):
            wanted = jnp.where(places[c] == j, z3[j].astype(F32), wanted)
        back_ref[:, lanes(c)] = wanted.astype(BF16)


def form_kernel(
    y_ref, z_ref, blocks_ref, col_ref, tgt_ref, count_ref, u_ref, ufar_ref, gram_ref, s3, acc
):
    rb = s3.shape[0]
    k = u_ref.shape[0]
    for j in range(rb):
        s3[j] = z_ref[:, lanes(j)]
    acc[...] = jnp.zeros_like(acc)
    count = count_ref[0]
    for c in range(blocks_ref.shape[0]):
        forward = fold(times_t(s3[col_ref[c]], blocks_ref[c]), k)
        if c < CROSS:
            ufar_ref[:, lanes(c)] = forward
        else:
            acc[jnp.where(c < count, tgt_ref[c], rb)] += forward
    for j in range(rb):
        u_ref[:, lanes(j)] = acc[j]
    y = y_ref[...]
    gram_ref[...] = times_t(y, y, FULL)


def pair_kernel(u_ref, ufar_ref, gram_ref, y_ref, dinv_ref, next_ref, part_ref, partner_ref, out_ref):
    k = u_ref.shape[0]
    rb = u_ref.shape[1] // BLOCK
    left = [
        u_ref[:, lanes(j)] + 0.5 * crossed_block(part_ref, partner_ref, j, k) for j in range(rb)
    ]
    left.append(ufar_ref[...])
    theirs = next_ref[...].astype(F32)
    right = [y_ref[...] * dinv_ref[...], theirs[:k] + theirs[k:]]
    form = times_t(jnp.concatenate(left, axis=1), jnp.concatenate(right, axis=1), FULL)
    both = jnp.concatenate([gram_ref[...], form], axis=1)
    rows = out_ref.shape[1]
    for g in range(out_ref.shape[0]):
        out_ref[g] = both[g * rows : (g + 1) * rows]


def solve_kernel(nodes, both_ref, y_ref, sub_ref, ray_ref):
    k = y_ref.shape[0]
    pieces, rows, _ = both_ref.shape
    both = jnp.concatenate([both_ref[g] for g in range(pieces)], axis=0) * (1.0 / nodes)
    gram = both[:, :k]
    form = both[:, k:]
    projected = gram + form + form.T
    ids = lax.broadcasted_iota(jnp.int32, (k, 2 * k), 0)
    lane = lax.broadcasted_iota(jnp.int32, (k, 2 * k), 1)
    work = jnp.concatenate([gram, jnp.zeros((k, k), F32)], axis=1)
    work = jnp.where(lane == ids + k, 1.0, work)
    for i in range(k):
        row = work[i : i + 1]
        pivot = lax.rsqrt(work[i : i + 1, i : i + 1])
        row = row * pivot
        column = work[:, i : i + 1] * pivot
        work = jnp.where(ids > i, work - column * row, jnp.where(ids == i, row, work))
    inverse = work[:, k:]
    sub_ref[...] = jnp.dot(inverse, y_ref[...], precision=FULL, preferred_element_type=F32)
    half = jnp.dot(inverse, projected, precision=FULL, preferred_element_type=F32)
    ray_ref[...] = times_t(half, inverse, FULL)


def call(kernel, ins, outs, scratch, *args):
    return pl.pallas_call(
        kernel,
        out_shape=[jax.ShapeDtypeStruct(shape, dtype) for shape, dtype in outs],
        in_specs=ins,
        out_specs=[VMEM] * len(outs),
        scratch_shapes=scratch,
        compiler_params=pltpu.CompilerParams(vmem_limit_bytes=24 * 1024 * 1024),
    )(*args)


def shards(start_block, blocks, block_column, block_target, block_count, partner, degree):
    k, nodes = start_block.shape
    rb = nodes // BLOCK
    blk, scale = lax.axis_size("blk"), lax.axis_size("scale")
    total = blk * scale
    node_total = nodes * total
    degree = degree.reshape(1, nodes)
    partner = partner.reshape(1, nodes)

    def shifted(array, distance):
        return lax.ppermute(array, "blk", [(i, (i + distance) % blk) for i in range(blk)])

    def swapped(array):
        return lax.ppermute(array, "scale", [(i, i ^ 1) for i in range(scale)])

    far = blocks[:CROSS]
    pay_rows = CROSS * (BLOCK + k + 16)
    dinv, scaled, ahead = call(
        first_kernel,
        [VMEM, VMEM, VMEM, SMEM, SMEM],
        [((1, nodes), F32), ((k, nodes), BF16), ((pay_rows, BLOCK), BF16)],
        [pltpu.VMEM((rb, k, BLOCK), BF16)],
        start_block,
        degree,
        far,
        block_column,
        block_target,
    )

    def near(z):
        return call(
            near_kernel,
            [VMEM, VMEM, SMEM, SMEM, SMEM],
            [((k, nodes), F32)],
            [pltpu.VMEM((rb, z.shape[0], BLOCK), BF16), pltpu.VMEM((rb + 1, k, BLOCK), F32)],
            z,
            blocks,
            block_column,
            block_target,
            block_count,
        )[0]

    def finish(first, near_sum, v, from_next, from_prev, part):
        outs = [((k, nodes), F32), ((2 * k, nodes), BF16)]
        outs += [((2 * k, CROSS * BLOCK), BF16)] * (2 if first else 1)
        return call(
            functools.partial(finish_kernel, first),
            [VMEM] * 9 + [SMEM, SMEM],
            outs,
            [pltpu.VMEM((rb, k, BLOCK), F32), pltpu.VMEM((rb, 2 * k, BLOCK), BF16)],
            near_sum,
            v,
            dinv,
            from_next,
            from_prev,
            pay,
            part,
            partner,
            far,
            block_column,
            block_target,
        )

    pay = shifted(ahead, 1)
    from_next = shifted(scaled, -1)
    part = swapped(scaled)
    first_image, z, ahead, back = finish(True, near(scaled), start_block, from_next, pay, part)

    from_prev = shifted(ahead, 1)
    from_next = shifted(back, -1)
    part = swapped(z)
    images, z, back = finish(False, near(z), first_image, from_next, from_prev, part)

    from_next = shifted(back, -1)
    part = swapped(z)
    u, ufar, gram = call(
        form_kernel,
        [VMEM, VMEM, VMEM, SMEM, SMEM, SMEM],
        [((k, nodes), F32), ((k, CROSS * BLOCK), F32), ((k, k), F32)],
        [pltpu.VMEM((rb, 2 * k, BLOCK), BF16), pltpu.VMEM((rb + 1, k, BLOCK), F32)],
        images,
        z,
        blocks,
        block_column,
        block_target,
        block_count,
    )
    plane = ALONG_X * scale
    depth = blk // ALONG_X
    rows = k // plane
    (mine,) = call(
        pair_kernel,
        [VMEM] * 8,
        [((plane, rows, 2 * k), F32)],
        [],
        u,
        ufar,
        gram,
        images,
        dinv,
        from_next,
        part,
        partner,
    )

    planes = [[z_at * plane + i for i in range(plane)] for z_at in range(depth)]
    columns = [[z_at * ALONG_X + x_at for z_at in range(depth)] for x_at in range(ALONG_X)]
    piece = lax.all_to_all(mine, BOTH, 0, 0, axis_index_groups=planes).sum(0)
    piece = jnp.broadcast_to(piece[None], (depth, rows, 2 * k))
    piece = lax.all_to_all(piece, "blk", 0, 0, axis_index_groups=columns).sum(0)
    piece = jnp.broadcast_to(piece[None], (plane, rows, 2 * k))
    both = lax.all_to_all(piece, BOTH, 0, 0, axis_index_groups=planes)

    return call(
        functools.partial(solve_kernel, node_total),
        [VMEM, VMEM],
        [((k, nodes), F32), ((k, k), F32)],
        [],
        both,
        images,
    )


def solution(mesh):
    return jax.shard_map(
        shards,
        mesh=mesh,
        in_specs=(
            P(None, BOTH),
            P(BOTH, None, None),
            P(BOTH),
            P(BOTH),
            P(BOTH),
            P(BOTH),
            P(BOTH),
        ),
        out_specs=(P(None, BOTH), P()),
        check_vma=False,
    )
```

time: 409 us -> 107 us (0.26)
  blocking collectives: 303 us -> 43.6 us
  other arithmetic: 26.5 us -> 0.07 us
  matrix products: 20.7 us -> 0 us
  Pallas kernels: 0 us -> 16 us
  local copies, waits for them, and re-layouts: 15.8 us -> 3.71 us
  waiting for transfers between devices: 3.48 us -> 9.53 us
  starting transfers between devices: 37.3 us -> 32.3 us
    psum x3 -> x0, blocking collectives: 303 us -> none  [the longest x2 204 us: shards(): gram_matrix = lax.psum(local_gram, ('blk', 'scale')) / node_total]
    all_to_all x0 -> x3, blocking collectives: none -> 43.6 us  [the longest x1 18.9 us: shards(): piece = lax.all_to_all(piece, 'blk', 0, 0, axis_index_groups=columns).sum(0)]
    another operation x10 -> x0, other arithmetic: 24.1 us -> none  [the longest x6 13 us: shards(): factor = jnp.linalg.cholesky(gram_matrix)]
    dot_general x26 -> x0, matrix products: 20.2 us -> none  [the longest x9 12.5 us: place_rows(): jnp.einsum('cr,ckj->krj', onehot, partial_terms, precision=FULL_PRECISION)]
    pallas_call x0 -> x8, Pallas kernels: none -> 16 us  [call(): pl.pallas_call(kernel, out_shape=[jax.ShapeDtypeStruct(shape, dtype) for...]
    gather x6 -> x0, local copies, waits for them, and re-layouts: 10 us -> none  [apply_operator(): crossed = jnp.take(partner_vectors, partner, axis=1).astype(jnp.float32)]
    ppermute x9 -> x8, waiting for transfers between devices: 3.48 us -> 9.53 us  [the longest x5 9.53 us: shifted(): lax.ppermute(array, 'blk', [(i, (i + distance) % blk) for i in range(blk)])]
    ppermute x9 -> x8, starting transfers between devices: 37.3 us -> 32.3 us  [the longest x5 17.1 us: shifted(): lax.ppermute(array, 'blk', [(i, (i + distance) % blk) for i in range(blk)])]
  transfers between devices with their start and end apart: 9 -> 8, of which waited for: 2 -> 3; matrix products, arithmetic and copies ran while one was open for 6% -> 0% of each run, Pallas kernels for 0% -> 4%
where the time goes in v1:
time: 107 us
  blocking collectives  43.6 us (41%)
  starting transfers between devices  32.3 us (30%)
  Pallas kernels  16 us (15%)
  waiting for transfers between devices  9.53 us (9%)
  local copies, waits for them, and re-layouts  3.71 us (3%)
  between operations  1.46 us (1%)
    all_to_all x1, blocking collectives, shards(): piece = lax.all_to_all(piece, 'blk', 0, 0, axis_index_groups=columns).sum(0)  18.9 us
    ppermute x5, starting transfers between devices, shifted(): lax.ppermute(array, 'blk', [(i, (i + distance) % blk) for i in range(blk)])  17.1 us
    pallas_call x8, Pallas kernels, call(): pl.pallas_call(kernel, out_shape=[jax.ShapeDtypeStruct(shape, dtype) for...  16 us
    ppermute x3, starting transfers between devices, swapped(): return lax.ppermute(array, 'scale', [(i, i ^ 1) for i in range(scale)])  15.2 us
    all_to_all x1, blocking collectives, shards(): piece = lax.all_to_all(mine, BOTH, 0, 0, axis_index_groups=planes).sum(0)  12.6 us
    all_to_all x1, blocking collectives, shards(): both = lax.all_to_all(piece, BOTH, 0, 0, axis_index_groups=planes)  12.1 us
    ppermute x5, waiting for transfers between devices, shifted(): lax.ppermute(array, 'blk', [(i, (i + distance) % blk) for i in range(blk)])  9.53 us
    unnamed x16, local copies, waits for them, and re-layouts  2.84 us
  transfers between devices with their start and end apart: 8, of which 3 were waited for; matrix products, arithmetic and copies ran while one was open for 0% of the time, Pallas kernels for 4%

profile of v1, /device:TPU:1, one launch (start us, length us, event | category | flops | bytes accessed | tf_op | source)
XLA Modules:
  0.0 106.7 jit_solution(10652211619718733182)
XLA Ops:
  0.6 0.0 copy-start.7
  0.6 0.9 slice.3.far_ref
  1.5 0.0 copy-start.5
  1.5 0.0 copy-start.6
  1.5 0.0 copy-done.7
  1.5 0.6 copy-done.5
  2.1 0.0 copy-done.6
  2.2 0.0 copy-start.2
  2.2 0.9 copy-done.2
  3.1 0.6 shard_map.86
  3.7 8.7 %collective-permute-start.2 = (bf16[64,1024]{1,0:T(8,128)(2,1)S(1)}, bf16[64,1024]{1,0:T(8,128)(2,1)S(1)}, u32[]{:S(2)}, u32[]{:S(2)}) collective-permute-start(bf16[64,1024]{1,0:T(8,128)(2,1)S(1)} %get-tuple-element.15.z_ref), channel_id=1, source_target_pairs={{0,1},{1,0},{2,3},{3,2},{4,5},{5,4},{6,7},{7,6},{8,9},{9,8},{10,11... | collective-permute-start | bytes 393224 | tf_op jit(solution)/shard_map/ppermute | solution.py:226
  12.5 8.0 %collective-permute-start = (bf16[64,1024]{1,0:T(8,128)(2,1)S(1)}, bf16[64,1024]{1,0:T(8,128)(2,1)S(1)}, u32[]{:S(2)}, u32[]{:S(2)}) collective-permute-start(bf16[64,1024]{1,0:T(8,128)(2,1)S(1)} %get-tuple-element.15.z_ref), channel_id=1, source_target_pairs={{0,504},{8,0},{16,8},{24,16},{32,24},{40,32},{48,40},{56,48},{64,5... | collective-permute-start | bytes 393224 | tf_op jit(solution)/shard_map/ppermute | solution.py:223
  20.4 1.9 %collective-permute-start.1 = (bf16[416,128]{1,0:T(8,128)(2,1)S(1)}, bf16[416,128]{1,0:T(8,128)(2,1)S(1)}, u32[]{:S(2)}, u32[]{:S(2)}) collective-permute-start(bf16[416,128]{1,0:T(8,128)(2,1)S(1)} %get-tuple-element.17), channel_id=1, source_target_pairs={{0,8},{8,16},{16,24},{24,32},{32,40},{40,48},{48,56},{56,64},{64,7... | collective-permute-start | bytes 319496 | tf_op jit(solution)/shard_map/ppermute | solution.py:223
  23.0 0.0 copy-start
  23.0 1.2 %copy-done = bf16[32,128,128]{2,1,0:T(8,128)(2,1)S(1)} copy-done((bf16[32,128,128]{2,1,0:T(8,128)(2,1)S(1)}, bf16[32,128,128]{2,1,0:T(8,128)(2,1)}, u32[]{:S(2)}) %copy-start) | copy-done | bytes 1048600
  24.2 0.0 copy-start.3
  24.3 0.0 copy-start.4
  24.3 0.0 copy-start.1
  24.3 1.5 %shard_map.87.near_ref = f32[64,1024]{1,0:T(8,128)S(1)} custom-call(bf16[64,1024]{1,0:T(8,128)(2,1)S(1)} %get-tuple-element.15.z_ref, bf16[32,128,128]{2,1,0:T(8,128)(2,1)S(1)} %copy-done, s32[32]{0:T(128)S(1)} %copy-done.5, s32[32]{0:T(128)S(1)} %copy-done.6, s32[1]{0:T(128)S(6)} %copy.11.count_ref), custom_call_target="tpu_custom_call" | custom-call | tf_op jit(solution)/shard_map/pallas_call | solution.py:203
  25.8 4.1 %collective-permute-done.1.prev_ref.pay_ref = bf16[416,128]{1,0:T(8,128)(2,1)S(1)} collective-permute-done((bf16[416,128]{1,0:T(8,128)(2,1)S(1)}, bf16[416,128]{1,0:T(8,128)(2,1)S(1)}, u32[]{:S(2)}, u32[]{:S(2)}) %collective-permute-start.1) | collective-permute-done | bytes 106528 | tf_op jit(solution)/shard_map/ppermute | solution.py:223
  29.9 0.0 collective-permute-done.2.part_ref
  29.9 0.0 collective-permute-done.next_ref
  29.9 0.0 copy-done.3
  29.9 0.0 copy-done.4
  29.9 1.2 %shard_map.88 = (f32[64,1024]{1,0:T(8,128)S(1)}, bf16[128,1024]{1,0:T(8,128)(2,1)S(1)}, bf16[128,256]{1,0:T(8,128)(2,1)S(1)}, bf16[128,256]{1,0:T(8,128)(2,1)S(1)}) custom-call(f32[64,1024]{1,0:T(8,128)S(1)} %shard_map.87.near_ref, f32[64,1024]{1,0:T(8,128)S(1)} %copy-done.3, f32[1,1024]{1,0:T(1,128)S(1)} %get-tuple-element.16.dinv_ref, ...), custom_call_target="tpu_custom_call" | custom-call | tf_op jit(solution)/shard_map/pallas_call | solution.py:203
  31.2 3.1 %collective-permute-start.5 = (bf16[128,1024]{1,0:T(8,128)(2,1)S(1)}, bf16[128,1024]{1,0:T(8,128)(2,1)S(1)}, u32[]{:S(2)}, u32[]{:S(2)}) collective-permute-start(bf16[128,1024]{1,0:T(8,128)(2,1)S(1)} %get-tuple-element.18.z_ref), channel_id=1, source_target_pairs={{0,1},{1,0},{2,3},{3,2},{4,5},{5,4},{6,7},{7,6},{8,9},{9,8},{10,11... | collective-permute-start | bytes 786440 | tf_op jit(solution)/shard_map/ppermute | solution.py:226
  34.2 2.0 %collective-permute-start.3 = (bf16[128,256]{1,0:T(8,128)(2,1)S(1)}, bf16[128,256]{1,0:T(8,128)(2,1)S(1)}, u32[]{:S(2)}, u32[]{:S(2)}) collective-permute-start(bf16[128,256]{1,0:T(8,128)(2,1)S(1)} %get-tuple-element.20), channel_id=1, source_target_pairs={{0,504},{8,0},{16,8},{24,16},{32,24},{40,32},{48,40},{56,48},{64,5... | collective-permute-start | bytes 196616 | tf_op jit(solution)/shard_map/ppermute | solution.py:223
  36.3 3.3 %collective-permute-start.4 = (bf16[128,256]{1,0:T(8,128)(2,1)S(1)}, bf16[128,256]{1,0:T(8,128)(2,1)S(1)}, u32[]{:S(2)}, u32[]{:S(2)}) collective-permute-start(bf16[128,256]{1,0:T(8,128)(2,1)S(1)} %get-tuple-element.21), channel_id=1, source_target_pairs={{0,8},{8,16},{16,24},{24,32},{32,40},{40,48},{48,56},{56,64},{64,7... | collective-permute-start | bytes 196616 | tf_op jit(solution)/shard_map/ppermute | solution.py:223
  39.5 0.0 copy-done.1
  39.5 1.6 %shard_map.89.near_ref = f32[64,1024]{1,0:T(8,128)S(1)} custom-call(bf16[128,1024]{1,0:T(8,128)(2,1)S(1)} %get-tuple-element.18.z_ref, bf16[32,128,128]{2,1,0:T(8,128)(2,1)S(1)} %copy-done.1, s32[32]{0:T(128)S(1)} %copy-done.5, s32[32]{0:T(128)S(1)} %copy-done.6, s32[1]{0:T(128)S(6)} %copy.11.count_ref), custom_call_target="tpu_custom_call" | custom-call | tf_op jit(solution)/shard_map/pallas_call | solution.py:203
  41.1 0.0 collective-permute-done.3.next_ref
  41.1 3.5 %collective-permute-done.4.prev_ref = bf16[128,256]{1,0:T(8,128)(2,1)S(1)} collective-permute-done((bf16[128,256]{1,0:T(8,128)(2,1)S(1)}, bf16[128,256]{1,0:T(8,128)(2,1)S(1)}, u32[]{:S(2)}, u32[]{:S(2)}) %collective-permute-start.4) | collective-permute-done | bytes 65568 | tf_op jit(solution)/shard_map/ppermute | solution.py:223
  44.6 0.0 collective-permute-done.5.part_ref
  44.6 1.5 %shard_map.90 = (f32[64,1024]{1,0:T(8,128)S(1)}, bf16[128,1024]{1,0:T(8,128)(2,1)S(1)}, bf16[128,256]{1,0:T(8,128)(2,1)S(1)}) custom-call(f32[64,1024]{1,0:T(8,128)S(1)} %shard_map.89.near_ref, f32[64,1024]{1,0:T(8,128)S(1)} %get-tuple-element.19.v_ref, f32[1,1024]{1,0:T(1,128)S(1)} %get-tuple-element.16.dinv_ref, ...), custom_call_target="tpu_custom_call" | custom-call | tf_op jit(solution)/shard_map/pallas_call | solution.py:203
  46.1 3.4 %collective-permute-start.7 = (bf16[128,1024]{1,0:T(8,128)(2,1)S(1)}, bf16[128,1024]{1,0:T(8,128)(2,1)S(1)}, u32[]{:S(2)}, u32[]{:S(2)}) collective-permute-start(bf16[128,1024]{1,0:T(8,128)(2,1)S(1)} %get-tuple-element.23.z_ref), channel_id=1, source_target_pairs={{0,1},{1,0},{2,3},{3,2},{4,5},{5,4},{6,7},{7,6},{8,9},{9,8},{10,11... | collective-permute-start | bytes 786440 | tf_op jit(solution)/shard_map/ppermute | solution.py:226
  49.5 1.9 %collective-permute-start.6 = (bf16[128,256]{1,0:T(8,128)(2,1)S(1)}, bf16[128,256]{1,0:T(8,128)(2,1)S(1)}, u32[]{:S(2)}, u32[]{:S(2)}) collective-permute-start(bf16[128,256]{1,0:T(8,128)(2,1)S(1)} %get-tuple-element.27), channel_id=1, source_target_pairs={{0,504},{8,0},{16,8},{24,16},{32,24},{40,32},{48,40},{56,48},{64,5... | collective-permute-start | bytes 196616 | tf_op jit(solution)/shard_map/ppermute | solution.py:223
  51.4 1.6 %shard_map.91 = (f32[64,1024]{1,0:T(8,128)S(1)}, f32[64,256]{1,0:T(8,128)S(1)}, f32[64,64]{1,0:T(8,128)S(1)}) custom-call(f32[64,1024]{1,0:T(8,128)S(1)} %get-tuple-element.22.y_ref, bf16[128,1024]{1,0:T(8,128)(2,1)S(1)} %get-tuple-element.23.z_ref, bf16[32,128,128]{2,1,0:T(8,128)(2,1)S(1)} %copy-done.1, s32[32]{0:T(128)S(1)} %copy-done.5, s32[32]{0:T(128)S(1)} %copy-done.6, ...), custom_call_target="tpu_custom_call" | custom-call | tf_op jit(solution)/shard_map/pallas_call | solution.py:203
  53.1 2.0 %collective-permute-done.6.next_ref = bf16[128,256]{1,0:T(8,128)(2,1)S(1)} collective-permute-done((bf16[128,256]{1,0:T(8,128)(2,1)S(1)}, bf16[128,256]{1,0:T(8,128)(2,1)S(1)}, u32[]{:S(2)}, u32[]{:S(2)}) %collective-permute-start.6) | collective-permute-done | bytes 65568 | tf_op jit(solution)/shard_map/ppermute | solution.py:223
  55.0 0.0 collective-permute-done.7.part_ref
  55.0 1.3 %shard_map.92 = f32[32,2,128]{2,1,0:T(2,128)S(1)} custom-call(f32[64,1024]{1,0:T(8,128)S(1)} %get-tuple-element.24.u_ref, f32[64,256]{1,0:T(8,128)S(1)} %get-tuple-element.25.ufar_ref, f32[64,64]{1,0:T(8,128)S(1)} %get-tuple-element.26.gram_ref, f32[64,1024]{1,0:T(8,128)S(1)} %get-tuple-element.22.y_ref, f32[1,1024]{1,0:T(1,128)S(1)} %get-tuple-element.16.dinv_ref, ...), custom_call_target="tpu_custom_call" | custom-call | tf_op jit(solution)/shard_map/pallas_call | solution.py:203
  56.4 12.6 %all_to_all.15 = f32[32,2,128]{2,1,0:T(2,128)S(1)} all-to-all(f32[32,2,128]{2,1,0:T(2,128)S(1)} %shard_map.92), channel_id=1, replica_groups={{0,1,2,3,4,5,6,7,8,9,10,11,12,13,14,15,16,17,18,19,20,21,22,23,24,25,26..., dimensions={0} | all-to-all | bytes 65536 | tf_op jit(solution)/shard_map/all_to_all | solution.py:320
  69.0 18.9 %all_to_all.16 = f32[16,2,128]{2,1,0:T(2,128)S(1)} all-to-all(f32[16,2,128]{2,1,0:T(2,128)S(1)} %broadcast_in_dim.4), channel_id=1, replica_groups={{0,32,64,96,128,160,192,224,256,288,320,352,384,416,448,480},{8,40,72,1..., dimensions={0} | all-to-all | bytes 32768 | tf_op jit(solution)/shard_map/all_to_all | solution.py:322
  87.9 12.1 %all_to_all.17.both_ref = f32[32,2,128]{2,1,0:T(2,128)S(1)} all-to-all(f32[32,2,128]{2,1,0:T(2,128)S(1)} %broadcast_in_dim.5), channel_id=1, replica_groups={{0,1,2,3,4,5,6,7,8,9,10,11,12,13,14,15,16,17,18,19,20,21,22,23,24,25,26..., dimensions={0} | all-to-all | bytes 65536 | tf_op jit(solution)/shard_map/all_to_all | solution.py:324
  100.1 6.6 %shard_map.93 = (f32[64,1024]{1,0:T(8,128)}, f32[64,64]{1,0:T(8,128)}) custom-call(f32[32,2,128]{2,1,0:T(2,128)S(1)} %all_to_all.17.both_ref, f32[64,1024]{1,0:T(8,128)S(1)} %get-tuple-element.22.y_ref), custom_call_target="tpu_custom_call" | custom-call | tf_op jit(solution)/shard_map/pallas_call | solution.py:203
  (4 shorter events, 0.1 us)
Async XLA Ops:
  0.6 0.9 copy-start.7
  1.5 0.7 copy-start.5
  1.5 0.7 copy-start.6
  2.2 0.9 copy-start.2
  3.7 26.2 %collective-permute-start.2 = (bf16[64,1024]{1,0:T(8,128)(2,1)S(1)}, bf16[64,1024]{1,0:T(8,128)(2,1)S(1)}, u32[]{:S(2)}, u32[]{:S(2)}) collective-permute-start(bf16[64,1024]{1,0:T(8,128)(2,1)S(1)} %get-tuple-element.15.z_ref), channel_id=1, source_target_pairs={{0,1},{1,0},{2,3},{3,2},{4,5},{5,4},{6,7},{7,6},{8,9},{9,8},{10,11... | collective-permute-start | bytes 393224 | tf_op jit(solution)/shard_map/ppermute | solution.py:226
  12.5 17.4 %collective-permute-start = (bf16[64,1024]{1,0:T(8,128)(2,1)S(1)}, bf16[64,1024]{1,0:T(8,128)(2,1)S(1)}, u32[]{:S(2)}, u32[]{:S(2)}) collective-permute-start(bf16[64,1024]{1,0:T(8,128)(2,1)S(1)} %get-tuple-element.15.z_ref), channel_id=1, source_target_pairs={{0,504},{8,0},{16,8},{24,16},{32,24},{40,32},{48,40},{56,48},{64,5... | collective-permute-start | bytes 393224 | tf_op jit(solution)/shard_map/ppermute | solution.py:223
  20.4 9.4 %collective-permute-start.1 = (bf16[416,128]{1,0:T(8,128)(2,1)S(1)}, bf16[416,128]{1,0:T(8,128)(2,1)S(1)}, u32[]{:S(2)}, u32[]{:S(2)}) collective-permute-start(bf16[416,128]{1,0:T(8,128)(2,1)S(1)} %get-tuple-element.17), channel_id=1, source_target_pairs={{0,8},{8,16},{16,24},{24,32},{32,40},{40,48},{48,56},{56,64},{64,7... | collective-permute-start | bytes 319496 | tf_op jit(solution)/shard_map/ppermute | solution.py:223
  23.0 1.2 %copy-start = (bf16[32,128,128]{2,1,0:T(8,128)(2,1)S(1)}, bf16[32,128,128]{2,1,0:T(8,128)(2,1)}, u32[]{:S(2)}) copy-start(bf16[32,128,128]{2,1,0:T(8,128)(2,1)} %blocks_ref.5) | copy-start | bytes 3145732
  24.2 5.7 %copy-start.3 = (f32[64,1024]{1,0:T(8,128)S(1)}, f32[64,1024]{1,0:T(8,128)}, u32[]{:S(2)}) copy-start(f32[64,1024]{1,0:T(8,128)} %v_ref.1) | copy-start | bytes 786436
  24.3 5.7 %copy-start.4 = (s32[1024]{0:T(1024)S(1)}, s32[1024]{0:T(1024)}, u32[]{:S(2)}) copy-start(s32[1024]{0:T(1024)} %param.12) | copy-start | bytes 12292
  24.3 15.3 %copy-start.1 = (bf16[32,128,128]{2,1,0:T(8,128)(2,1)S(1)}, bf16[32,128,128]{2,1,0:T(8,128)(2,1)}, u32[]{:S(2)}) copy-start(bf16[32,128,128]{2,1,0:T(8,128)(2,1)} %blocks_ref.5) | copy-start | bytes 3145732
  31.2 13.4 %collective-permute-start.5 = (bf16[128,1024]{1,0:T(8,128)(2,1)S(1)}, bf16[128,1024]{1,0:T(8,128)(2,1)S(1)}, u32[]{:S(2)}, u32[]{:S(2)}) collective-permute-start(bf16[128,1024]{1,0:T(8,128)(2,1)S(1)} %get-tuple-element.18.z_ref), channel_id=1, source_target_pairs={{0,1},{1,0},{2,3},{3,2},{4,5},{5,4},{6,7},{7,6},{8,9},{9,8},{10,11... | collective-permute-start | bytes 786440 | tf_op jit(solution)/shard_map/ppermute | solution.py:226
  34.2 6.9 %collective-permute-start.3 = (bf16[128,256]{1,0:T(8,128)(2,1)S(1)}, bf16[128,256]{1,0:T(8,128)(2,1)S(1)}, u32[]{:S(2)}, u32[]{:S(2)}) collective-permute-start(bf16[128,256]{1,0:T(8,128)(2,1)S(1)} %get-tuple-element.20), channel_id=1, source_target_pairs={{0,504},{8,0},{16,8},{24,16},{32,24},{40,32},{48,40},{56,48},{64,5... | collective-permute-start | bytes 196616 | tf_op jit(solution)/shard_map/ppermute | solution.py:223
  36.3 8.3 %collective-permute-start.4 = (bf16[128,256]{1,0:T(8,128)(2,1)S(1)}, bf16[128,256]{1,0:T(8,128)(2,1)S(1)}, u32[]{:S(2)}, u32[]{:S(2)}) collective-permute-start(bf16[128,256]{1,0:T(8,128)(2,1)S(1)} %get-tuple-element.21), channel_id=1, source_target_pairs={{0,8},{8,16},{16,24},{24,32},{32,40},{40,48},{48,56},{56,64},{64,7... | collective-permute-start | bytes 196616 | tf_op jit(solution)/shard_map/ppermute | solution.py:223
  46.1 8.9 %collective-permute-start.7 = (bf16[128,1024]{1,0:T(8,128)(2,1)S(1)}, bf16[128,1024]{1,0:T(8,128)(2,1)S(1)}, u32[]{:S(2)}, u32[]{:S(2)}) collective-permute-start(bf16[128,1024]{1,0:T(8,128)(2,1)S(1)} %get-tuple-element.23.z_ref), channel_id=1, source_target_pairs={{0,1},{1,0},{2,3},{3,2},{4,5},{5,4},{6,7},{7,6},{8,9},{9,8},{10,11... | collective-permute-start | bytes 786440 | tf_op jit(solution)/shard_map/ppermute | solution.py:226
  49.5 5.5 %collective-permute-start.6 = (bf16[128,256]{1,0:T(8,128)(2,1)S(1)}, bf16[128,256]{1,0:T(8,128)(2,1)S(1)}, u32[]{:S(2)}, u32[]{:S(2)}) collective-permute-start(bf16[128,256]{1,0:T(8,128)(2,1)S(1)} %get-tuple-element.27), channel_id=1, source_target_pairs={{0,504},{8,0},{16,8},{24,16},{32,24},{40,32},{48,40},{56,48},{64,5... | collective-permute-start | bytes 196616 | tf_op jit(solution)/shard_map/ppermute | solution.py:223

commit v2 on v1

--- a/solution.py
+++ b/solution.py
@@ -7,9 +7,12 @@
 from jax.experimental.pallas import tpu as pltpu
 from jax.sharding import PartitionSpec as P
 
+
 BLOCK = 128
 CROSS = 2
 ALONG_X = 4
+SUBLANES = 8
+PANEL = 8
 BOTH = ("blk", "scale")
 FULL = lax.Precision.HIGHEST
 F32 = jnp.float32
@@ -42,8 +45,38 @@
     return jnp.concatenate([high, (value - high.astype(F32)).astype(BF16)], axis=0)
 
 
-def first_kernel(x_ref, degree_ref, far_ref, col_ref, tgt_ref, dinv_ref, scaled_ref, ahead_ref, s3):
+def first_kernel(
+    x_hbm,
+    degree_hbm,
+    blocks_hbm,
+    col_hbm,
+    tgt_hbm,
+    dinv_ref,
+    scaled_ref,
+    ahead_ref,
+    blocks_ref,
+    col_ref,
+    tgt_ref,
+    x_ref,
+    degree_ref,
+    s3,
+    sems,
+):
     k = x_ref.shape[0]
+    far, near = pl.ds(0, CROSS), pl.ds(CROSS, blocks_ref.shape[0] - CROSS)
+    moves = [
+        (degree_hbm, degree_ref),
+        (x_hbm, x_ref),
+        (col_hbm, col_ref),
+        (tgt_hbm, tgt_ref),
+        (blocks_hbm.at[far], blocks_ref.at[far]),
+        (blocks_hbm.at[near], blocks_ref.at[near]),
+    ]
+    copies = [pltpu.make_async_copy(src, dst, sems.at[i]) for i, (src, dst) in enumerate(moves)]
+    for copy in copies:
+        copy.start()
+    for copy in copies[:5]:
+        copy.wait()
     dinv = 1.0 / jnp.sqrt(degree_ref[...].astype(F32))
     dinv_ref[...] = dinv
     scaled = (x_ref[...] * dinv).astype(BF16)
@@ -51,12 +84,13 @@
     for j in range(s3.shape[0]):
         s3[j] = scaled[:, lanes(j)]
     for c in range(CROSS):
-        ahead_ref[c * BLOCK : (c + 1) * BLOCK] = far_ref[c]
+        ahead_ref[c * BLOCK : (c + 1) * BLOCK] = blocks_ref[c]
         at = CROSS * BLOCK + c * k
         ahead_ref[at : at + k] = s3[col_ref[c]]
         at = CROSS * (BLOCK + k) + c * 16
         row = jnp.full((16, BLOCK), tgt_ref[c] - s3.shape[0], jnp.int32)
         ahead_ref[at : at + 16] = row.astype(F32).astype(BF16)
+    copies[5].wait()
 
 
 def near_kernel(z_ref, blocks_ref, col_ref, tgt_ref, count_ref, out_ref, s3, acc):
@@ -140,10 +174,10 @@
 
 
 def form_kernel(
-    y_ref, z_ref, blocks_ref, col_ref, tgt_ref, count_ref, u_ref, ufar_ref, gram_ref, s3, acc
+    y_ref, z_ref, dinv_ref, blocks_ref, partner_ref, col_ref, tgt_ref, count_ref, right_ref, out_ref, s3, acc
 ):
     rb = s3.shape[0]
-    k = u_ref.shape[0]
+    k = y_ref.shape[0]
     for j in range(rb):
         s3[j] = z_ref[:, lanes(j)]
     acc[...] = jnp.zeros_like(acc)
@@ -151,60 +185,91 @@
     for c in range(blocks_ref.shape[0]):
         forward = fold(times_t(s3[col_ref[c]], blocks_ref[c]), k)
         if c < CROSS:
-            ufar_ref[:, lanes(c)] = forward
+            right_ref[:, lanes(rb + c)] = forward
         else:
             acc[jnp.where(c < count, tgt_ref[c], rb)] += forward
-    for j in range(rb):
-        u_ref[:, lanes(j)] = acc[j]
+    nodes = y_ref.shape[1]
+    for j in range(rb):
+        ids = lax.broadcasted_iota(jnp.int32, (BLOCK, nodes), 0) + j * BLOCK
+        onehot = jnp.where(ids == partner_ref[...], 0.5, 0.0).astype(BF16)
+        right_ref[:, lanes(j)] = fold(times_t(z_ref[...], onehot), k)
     y = y_ref[...]
-    gram_ref[...] = times_t(y, y, FULL)
-
-
-def pair_kernel(u_ref, ufar_ref, gram_ref, y_ref, dinv_ref, next_ref, part_ref, partner_ref, out_ref):
-    k = u_ref.shape[0]
-    rb = u_ref.shape[1] // BLOCK
-    left = [
-        u_ref[:, lanes(j)] + 0.5 * crossed_block(part_ref, partner_ref, j, k) for j in range(rb)
-    ]
-    left.append(ufar_ref[...])
-    theirs = next_ref[...].astype(F32)
-    right = [y_ref[...] * dinv_ref[...], theirs[:k] + theirs[k:]]
-    form = times_t(jnp.concatenate(left, axis=1), jnp.concatenate(right, axis=1), FULL)
-    both = jnp.concatenate([gram_ref[...], form], axis=1)
+    z = y * dinv_ref[...]
+    near = jnp.concatenate([acc[j] for j in range(rb)], axis=1)
+    out_ref[:, :k] = times_t(y, y, FULL)
+    out_ref[:, k:] = times_t(near, z, FULL)
+
+
+def pair_kernel(right_ref, sums_ref, next_ref, part_ref, out_ref):
+    k = right_ref.shape[0]
+    theirs = jnp.concatenate([part_ref[...], next_ref[...]], axis=1).astype(F32)
+    form = times_t(theirs[:k] + theirs[k:], right_ref[...], FULL)
+    both = sums_ref[...] + jnp.concatenate([jnp.zeros((k, k), F32), form], axis=1)
     rows = out_ref.shape[1]
     for g in range(out_ref.shape[0]):
         out_ref[g] = both[g * rows : (g + 1) * rows]
 
 
+def inverse_factor(gram):
+    k = gram.shape[0]
+    row_ids = lax.broadcasted_iota(jnp.int32, (SUBLANES, 2 * k), 0)
+    lane = lax.broadcasted_iota(jnp.int32, (SUBLANES, 2 * k), 1)
+    padded = jnp.concatenate([gram, jnp.zeros((k, k), F32)], axis=1)
+    tiles = []
+    for t in range(k // SUBLANES):
+        tile = padded[t * SUBLANES : (t + 1) * SUBLANES]
+        tiles.append(jnp.where(lane == row_ids + (k + t * SUBLANES), 1.0, tile))
+    for start in range(0, k, PANEL):
+        top, offset = divmod(start, SUBLANES)
+        below = range(top, len(tiles))
+        columns, rows = [], []
+        for j in range(PANEL):
+            at = start + j
+            columns.append(
+                {t: jnp.broadcast_to(tiles[t][:, at : at + 1], (SUBLANES, 2 * k)) for t in below}
+            )
+            rows.append(tiles[top][offset + j : offset + j + 1])
+        for j in range(PANEL):
+            pivot = lax.rsqrt(columns[j][top][offset + j : offset + j + 1])
+            rows[j] = rows[j] * pivot
+            columns[j] = {t: c * pivot for t, c in columns[j].items()}
+            for m in range(j + 1, PANEL):
+                factor = columns[j][top][offset + m : offset + m + 1]
+                rows[m] = rows[m] - rows[j] * factor
+                columns[m] = {t: c - columns[j][t] * factor for t, c in columns[m].items()}
+        for t in below:
+            if t == top and offset + PANEL == SUBLANES:
+                continue
+            tile = tiles[t]
+            for j in range(PANEL):
+                tile = tile - columns[j][t] * rows[j]
+            if t == top:
+                tile = jnp.where(row_ids >= offset + PANEL, tile, tiles[t])
+            tiles[t] = tile
+        for j in range(PANEL):
+            tiles[top] = jnp.where(row_ids == offset + j, rows[j], tiles[top])
+    return jnp.concatenate([tile[:, k:] for tile in tiles], axis=0)
+
+
 def solve_kernel(nodes, both_ref, y_ref, sub_ref, ray_ref):
     k = y_ref.shape[0]
-    pieces, rows, _ = both_ref.shape
+    pieces, _, _ = both_ref.shape
     both = jnp.concatenate([both_ref[g] for g in range(pieces)], axis=0) * (1.0 / nodes)
     gram = both[:, :k]
     form = both[:, k:]
     projected = gram + form + form.T
-    ids = lax.broadcasted_iota(jnp.int32, (k, 2 * k), 0)
-    lane = lax.broadcasted_iota(jnp.int32, (k, 2 * k), 1)
-    work = jnp.concatenate([gram, jnp.zeros((k, k), F32)], axis=1)
-    work = jnp.where(lane == ids + k, 1.0, work)
-    for i in range(k):
-        row = work[i : i + 1]
-        pivot = lax.rsqrt(work[i : i + 1, i : i + 1])
-        row = row * pivot
-        column = work[:, i : i + 1] * pivot
-        work = jnp.where(ids > i, work - column * row, jnp.where(ids == i, row, work))
-    inverse = work[:, k:]
+    inverse = inverse_factor(gram)
     sub_ref[...] = jnp.dot(inverse, y_ref[...], precision=FULL, preferred_element_type=F32)
     half = jnp.dot(inverse, projected, precision=FULL, preferred_element_type=F32)
     ray_ref[...] = times_t(half, inverse, FULL)
 
 
-def call(kernel, ins, outs, scratch, *args):
+def call(kernel, ins, outs, scratch, *args, out_specs=None):
     return pl.pallas_call(
         kernel,
         out_shape=[jax.ShapeDtypeStruct(shape, dtype) for shape, dtype in outs],
         in_specs=ins,
-        out_specs=[VMEM] * len(outs),
+        out_specs=[VMEM] * len(outs) if out_specs is None else out_specs,
         scratch_shapes=scratch,
         compiler_params=pltpu.CompilerParams(vmem_limit_bytes=24 * 1024 * 1024),
     )(*args)
@@ -214,8 +279,7 @@
     k, nodes = start_block.shape
     rb = nodes // BLOCK
     blk, scale = lax.axis_size("blk"), lax.axis_size("scale")
-    total = blk * scale
-    node_total = nodes * total
+    node_total = nodes * blk * scale
     degree = degree.reshape(1, nodes)
     partner = partner.reshape(1, nodes)
 
@@ -225,18 +289,29 @@
     def swapped(array):
         return lax.ppermute(array, "scale", [(i, i ^ 1) for i in range(scale)])
 
-    far = blocks[:CROSS]
     pay_rows = CROSS * (BLOCK + k + 16)
-    dinv, scaled, ahead = call(
+    dinv, scaled, ahead, blocks, column, target = call(
         first_kernel,
-        [VMEM, VMEM, VMEM, SMEM, SMEM],
-        [((1, nodes), F32), ((k, nodes), BF16), ((pay_rows, BLOCK), BF16)],
-        [pltpu.VMEM((rb, k, BLOCK), BF16)],
-        start_block,
-        degree,
-        far,
-        block_column,
-        block_target,
+        [pl.BlockSpec(memory_space=pltpu.HBM)] * 5,
+        [
+            ((1, nodes), F32),
+            ((k, nodes), BF16),
+            ((pay_rows, BLOCK), BF16),
+            (blocks.shape, BF16),
+            (block_column.shape, jnp.int32),
+            (block_target.shape, jnp.int32),
+        ],
+        [
+            pltpu.VMEM((k, nodes), F32),
+            pltpu.VMEM((1, nodes), jnp.int32),
+            pltpu.VMEM((rb, k, BLOCK), BF16),
+            pltpu.SemaphoreType.DMA((6,)),
+        ],
+        *[
+            pltpu.with_memory_space_constraint(array, pltpu.HBM)
+            for array in (start_block, degree, blocks, block_column, block_target)
+        ],
+        out_specs=[VMEM] * 4 + [SMEM] * 2,
     )
 
     def near(z):
@@ -247,8 +322,8 @@
             [pltpu.VMEM((rb, z.shape[0], BLOCK), BF16), pltpu.VMEM((rb + 1, k, BLOCK), F32)],
             z,
             blocks,
-            block_column,
-            block_target,
+            column,
+            target,
             block_count,
         )[0]
 
@@ -268,9 +343,9 @@
             pay,
             part,
             partner,
-            far,
-            block_column,
-            block_target,
+            blocks,
+            column,
+            target,
         )
 
     pay = shifted(ahead, 1)
@@ -285,16 +360,18 @@
 
     from_next = shifted(back, -1)
     part = swapped(z)
-    u, ufar, gram = call(
+    right, sums = call(
         form_kernel,
-        [VMEM, VMEM, VMEM, SMEM, SMEM, SMEM],
-        [((k, nodes), F32), ((k, CROSS * BLOCK), F32), ((k, k), F32)],
+        [VMEM] * 5 + [SMEM] * 3,
+        [((k, nodes + CROSS * BLOCK), F32), ((k, 2 * k), F32)],
         [pltpu.VMEM((rb, 2 * k, BLOCK), BF16), pltpu.VMEM((rb + 1, k, BLOCK), F32)],
         images,
         z,
+        dinv,
         blocks,
-        block_column,
-        block_target,
+        partner,
+        column,
+        target,
         block_count,
     )
     plane = ALONG_X * scale
@@ -302,17 +379,13 @@
     rows = k // plane
     (mine,) = call(
         pair_kernel,
-        [VMEM] * 8,
+        [VMEM] * 4,
         [((plane, rows, 2 * k), F32)],
         [],
-        u,
-        ufar,
-        gram,
-        images,
-        dinv,
+        right,
+        sums,
         from_next,
         part,
-        partner,
     )
 
     planes = [[z_at * plane + i for i in range(plane)] for z_at in range(depth)]
@@ -333,9 +406,13 @@
     )
 
 
+def layered(*args):
+    return tuple(shards(*args))
+
+
 def solution(mesh):
     return jax.shard_map(
-        shards,
+        layered,
         mesh=mesh,
         in_specs=(
             P(None, BOTH),

time: 107 us -> 101 us (0.944)
  local copies, waits for them, and re-layouts: 3.71 us -> 0.03 us
  Pallas kernels: 16 us -> 13.8 us
    unnamed x16 -> x4, local copies, waits for them, and re-layouts: 2.84 us -> 0.01 us
    pallas_call x8, Pallas kernels: 16 us -> 13.8 us  [call(): pl.pallas_call(kernel, out_shape=[jax.ShapeDtypeStruct(shape, dtype) for...]
  transfers between devices with their start and end apart: 8 -> 8, of which waited for: 3 -> 3; matrix products, arithmetic and copies ran while one was open for 0% -> 0% of each run, Pallas kernels for 4% -> 6%
where the time goes in v2:
time: 101 us
  blocking collectives  43.6 us (43%)
  starting transfers between devices  31.7 us (31%)
  Pallas kernels  13.8 us (14%)
  waiting for transfers between devices  10.4 us (10%)
  between operations  1.43 us (1%)
    all_to_all x1, blocking collectives, shards(): piece = lax.all_to_all(piece, 'blk', 0, 0, axis_index_groups=columns).sum(0)  18.9 us
    ppermute x5, starting transfers between devices, shifted(): lax.ppermute(array, 'blk', [(i, (i + distance) % blk) for i in range(blk)])  17.1 us
    ppermute x3, starting transfers between devices, swapped(): return lax.ppermute(array, 'scale', [(i, i ^ 1) for i in range(scale)])  14.6 us
    pallas_call x8, Pallas kernels, call(): pl.pallas_call(kernel, out_shape=[jax.ShapeDtypeStruct(shape, dtype) for...  13.8 us
    all_to_all x1, blocking collectives, shards(): piece = lax.all_to_all(mine, BOTH, 0, 0, axis_index_groups=planes).sum(0)  12.6 us
    all_to_all x1, blocking collectives, shards(): both = lax.all_to_all(piece, BOTH, 0, 0, axis_index_groups=planes)  12.1 us
    ppermute x5, waiting for transfers between devices, shifted(): lax.ppermute(array, 'blk', [(i, (i + distance) % blk) for i in range(blk)])  10.4 us
  transfers between devices with their start and end apart: 8, of which 3 were waited for; matrix products, arithmetic and copies ran while one was open for 0% of the time, Pallas kernels for 6%

profile of v2, /device:TPU:1, one launch (start us, length us, event | category | flops | bytes accessed | tf_op | source)
XLA Modules:
  0.0 100.9 jit_solution(8569351795858220913)
XLA Ops:
  0.6 2.0 %shard_map.86 = (f32[1,1024]{1,0:T(1,128)S(1)}, bf16[64,1024]{1,0:T(8,128)(2,1)S(1)}, bf16[416,128]{1,0:T(8,128)(2,1)S(1)}, bf16[32,128,128]{2,1,0:T(8,128)(2,1)S(1)}, s32[32]{0:T(128)S(1)}, /*index=5*/s32[32]{0:T(128)S(1)}) custom-call(f32[64,1024]{1,0:T(8,128)} %v_ref.1, s32[1,1024]{1,0:T(1,128)} %bitcast.5, bf16[32,128,128]{2,1,0:T(8,128)(2,1)} %blocks_hbm.1, ...), custom_call_target="tpu_custom_call" | custom-call | tf_op jit(solution)/shard_map/pallas_call | solution.py:268
  2.6 8.7 %collective-permute-start.2 = (bf16[64,1024]{1,0:T(8,128)(2,1)S(1)}, bf16[64,1024]{1,0:T(8,128)(2,1)S(1)}, u32[]{:S(2)}, u32[]{:S(2)}) collective-permute-start(bf16[64,1024]{1,0:T(8,128)(2,1)S(1)} %get-tuple-element.17.z_ref), channel_id=1, source_target_pairs={{0,1},{1,0},{2,3},{3,2},{4,5},{5,4},{6,7},{7,6},{8,9},{9,8},{10,11... | collective-permute-start | bytes 393224 | tf_op jit(solution)/shard_map/ppermute | solution.py:290
  11.4 8.0 %collective-permute-start = (bf16[64,1024]{1,0:T(8,128)(2,1)S(1)}, bf16[64,1024]{1,0:T(8,128)(2,1)S(1)}, u32[]{:S(2)}, u32[]{:S(2)}) collective-permute-start(bf16[64,1024]{1,0:T(8,128)(2,1)S(1)} %get-tuple-element.17.z_ref), channel_id=1, source_target_pairs={{0,504},{8,0},{16,8},{24,16},{32,24},{40,32},{48,40},{56,48},{64,5... | collective-permute-start | bytes 393224 | tf_op jit(solution)/shard_map/ppermute | solution.py:287
  19.4 1.9 %collective-permute-start.1 = (bf16[416,128]{1,0:T(8,128)(2,1)S(1)}, bf16[416,128]{1,0:T(8,128)(2,1)S(1)}, u32[]{:S(2)}, u32[]{:S(2)}) collective-permute-start(bf16[416,128]{1,0:T(8,128)(2,1)S(1)} %get-tuple-element.22), channel_id=1, source_target_pairs={{0,8},{8,16},{16,24},{24,32},{32,40},{40,48},{48,56},{56,64},{64,7... | collective-permute-start | bytes 319496 | tf_op jit(solution)/shard_map/ppermute | solution.py:287
  21.9 0.0 copy-start
  22.0 0.0 copy-start.1
  22.0 1.5 %shard_map.87.near_ref = f32[64,1024]{1,0:T(8,128)S(1)} custom-call(bf16[64,1024]{1,0:T(8,128)(2,1)S(1)} %get-tuple-element.17.z_ref, bf16[32,128,128]{2,1,0:T(8,128)(2,1)S(1)} %get-tuple-element.18.blocks_ref.far_ref, s32[32]{0:T(128)S(1)} %get-tuple-element.19.col_ref, s32[32]{0:T(128)S(1)} %get-tuple-element.20.tgt_ref, s32[1]{0:T(128)S(6)} %copy.11.count_ref), custom_call_target="tpu_custom_call" | custom-call | tf_op jit(solution)/shard_map/pallas_call | solution.py:268
  23.5 5.3 %collective-permute-done.1.prev_ref.pay_ref = bf16[416,128]{1,0:T(8,128)(2,1)S(1)} collective-permute-done((bf16[416,128]{1,0:T(8,128)(2,1)S(1)}, bf16[416,128]{1,0:T(8,128)(2,1)S(1)}, u32[]{:S(2)}, u32[]{:S(2)}) %collective-permute-start.1) | collective-permute-done | bytes 106528 | tf_op jit(solution)/shard_map/ppermute | solution.py:287
  28.8 0.0 collective-permute-done.2.part_ref
  28.8 0.0 collective-permute-done.next_ref
  28.8 0.0 copy-done
  28.8 0.0 copy-done.1
  28.8 1.3 %shard_map.88 = (f32[64,1024]{1,0:T(8,128)S(1)}, bf16[128,1024]{1,0:T(8,128)(2,1)S(1)}, bf16[128,256]{1,0:T(8,128)(2,1)S(1)}, bf16[128,256]{1,0:T(8,128)(2,1)S(1)}) custom-call(f32[64,1024]{1,0:T(8,128)S(1)} %shard_map.87.near_ref, f32[64,1024]{1,0:T(8,128)S(1)} %copy-done, f32[1,1024]{1,0:T(1,128)S(1)} %get-tuple-element.21.dinv_ref, ...), custom_call_target="tpu_custom_call" | custom-call | tf_op jit(solution)/shard_map/pallas_call | solution.py:268
  30.1 3.1 %collective-permute-start.5 = (bf16[128,1024]{1,0:T(8,128)(2,1)S(1)}, bf16[128,1024]{1,0:T(8,128)(2,1)S(1)}, u32[]{:S(2)}, u32[]{:S(2)}) collective-permute-start(bf16[128,1024]{1,0:T(8,128)(2,1)S(1)} %get-tuple-element.23.z_ref), channel_id=1, source_target_pairs={{0,1},{1,0},{2,3},{3,2},{4,5},{5,4},{6,7},{7,6},{8,9},{9,8},{10,11... | collective-permute-start | bytes 786440 | tf_op jit(solution)/shard_map/ppermute | solution.py:290
  33.2 1.9 %collective-permute-start.3 = (bf16[128,256]{1,0:T(8,128)(2,1)S(1)}, bf16[128,256]{1,0:T(8,128)(2,1)S(1)}, u32[]{:S(2)}, u32[]{:S(2)}) collective-permute-start(bf16[128,256]{1,0:T(8,128)(2,1)S(1)} %get-tuple-element.25), channel_id=1, source_target_pairs={{0,504},{8,0},{16,8},{24,16},{32,24},{40,32},{48,40},{56,48},{64,5... | collective-permute-start | bytes 196616 | tf_op jit(solution)/shard_map/ppermute | solution.py:287
  35.1 3.4 %collective-permute-start.4 = (bf16[128,256]{1,0:T(8,128)(2,1)S(1)}, bf16[128,256]{1,0:T(8,128)(2,1)S(1)}, u32[]{:S(2)}, u32[]{:S(2)}) collective-permute-start(bf16[128,256]{1,0:T(8,128)(2,1)S(1)} %get-tuple-element.26), channel_id=1, source_target_pairs={{0,8},{8,16},{16,24},{24,32},{32,40},{40,48},{48,56},{56,64},{64,7... | collective-permute-start | bytes 196616 | tf_op jit(solution)/shard_map/ppermute | solution.py:287
  38.5 1.6 %shard_map.89.near_ref = f32[64,1024]{1,0:T(8,128)S(1)} custom-call(bf16[128,1024]{1,0:T(8,128)(2,1)S(1)} %get-tuple-element.23.z_ref, bf16[32,128,128]{2,1,0:T(8,128)(2,1)S(1)} %get-tuple-element.18.blocks_ref.far_ref, s32[32]{0:T(128)S(1)} %get-tuple-element.19.col_ref, s32[32]{0:T(128)S(1)} %get-tuple-element.20.tgt_ref, s32[1]{0:T(128)S(6)} %copy.11.count_ref), custom_call_target="tpu_custom_call" | custom-call | tf_op jit(solution)/shard_map/pallas_call | solution.py:268
  40.0 0.0 collective-permute-done.3.next_ref
  40.0 3.9 %collective-permute-done.4.prev_ref = bf16[128,256]{1,0:T(8,128)(2,1)S(1)} collective-permute-done((bf16[128,256]{1,0:T(8,128)(2,1)S(1)}, bf16[128,256]{1,0:T(8,128)(2,1)S(1)}, u32[]{:S(2)}, u32[]{:S(2)}) %collective-permute-start.4) | collective-permute-done | bytes 65568 | tf_op jit(solution)/shard_map/ppermute | solution.py:287
  43.9 0.0 collective-permute-done.5.part_ref
  43.9 1.5 %shard_map.90 = (f32[64,1024]{1,0:T(8,128)S(1)}, bf16[128,1024]{1,0:T(8,128)(2,1)S(1)}, bf16[128,256]{1,0:T(8,128)(2,1)S(1)}) custom-call(f32[64,1024]{1,0:T(8,128)S(1)} %shard_map.89.near_ref, f32[64,1024]{1,0:T(8,128)S(1)} %get-tuple-element.24.v_ref, f32[1,1024]{1,0:T(1,128)S(1)} %get-tuple-element.21.dinv_ref, ...), custom_call_target="tpu_custom_call" | custom-call | tf_op jit(solution)/shard_map/pallas_call | solution.py:268
  45.5 2.8 %collective-permute-start.7 = (bf16[128,1024]{1,0:T(8,128)(2,1)S(1)}, bf16[128,1024]{1,0:T(8,128)(2,1)S(1)}, u32[]{:S(2)}, u32[]{:S(2)}) collective-permute-start(bf16[128,1024]{1,0:T(8,128)(2,1)S(1)} %get-tuple-element.28.z_ref), channel_id=1, source_target_pairs={{0,1},{1,0},{2,3},{3,2},{4,5},{5,4},{6,7},{7,6},{8,9},{9,8},{10,11... | collective-permute-start | bytes 786440 | tf_op jit(solution)/shard_map/ppermute | solution.py:290
  48.3 1.9 %collective-permute-start.6 = (bf16[128,256]{1,0:T(8,128)(2,1)S(1)}, bf16[128,256]{1,0:T(8,128)(2,1)S(1)}, u32[]{:S(2)}, u32[]{:S(2)}) collective-permute-start(bf16[128,256]{1,0:T(8,128)(2,1)S(1)} %get-tuple-element.31), channel_id=1, source_target_pairs={{0,504},{8,0},{16,8},{24,16},{32,24},{40,32},{48,40},{56,48},{64,5... | collective-permute-start | bytes 196616 | tf_op jit(solution)/shard_map/ppermute | solution.py:287
  50.2 2.5 %shard_map.91 = (f32[64,1280]{1,0:T(8,128)S(1)}, f32[64,128]{1,0:T(8,128)S(1)}) custom-call(f32[64,1024]{1,0:T(8,128)S(1)} %get-tuple-element.27.y_ref, bf16[128,1024]{1,0:T(8,128)(2,1)S(1)} %get-tuple-element.28.z_ref, f32[1,1024]{1,0:T(1,128)S(1)} %get-tuple-element.21.dinv_ref, bf16[32,128,128]{2,1,0:T(8,128)(2,1)S(1)} %get-tuple-element.18.blocks_ref.far_ref, ...), custom_call_target="tpu_custom_call" | custom-call | tf_op jit(solution)/shard_map/pallas_call | solution.py:268
  52.7 1.1 %collective-permute-done.6.next_ref = bf16[128,256]{1,0:T(8,128)(2,1)S(1)} collective-permute-done((bf16[128,256]{1,0:T(8,128)(2,1)S(1)}, bf16[128,256]{1,0:T(8,128)(2,1)S(1)}, u32[]{:S(2)}, u32[]{:S(2)}) %collective-permute-start.6) | collective-permute-done | bytes 65568 | tf_op jit(solution)/shard_map/ppermute | solution.py:287
  53.8 0.0 collective-permute-done.7.part_ref
  53.8 0.5 shard_map.92
  54.3 12.6 %all_to_all.15 = f32[32,2,128]{2,1,0:T(2,128)S(1)} all-to-all(f32[32,2,128]{2,1,0:T(2,128)S(1)} %shard_map.92), channel_id=1, replica_groups={{0,1,2,3,4,5,6,7,8,9,10,11,12,13,14,15,16,17,18,19,20,21,22,23,24,25,26..., dimensions={0} | all-to-all | bytes 65536 | tf_op jit(solution)/shard_map/all_to_all | solution.py:393
  66.9 18.9 %all_to_all.16 = f32[16,2,128]{2,1,0:T(2,128)S(1)} all-to-all(f32[16,2,128]{2,1,0:T(2,128)S(1)} %broadcast_in_dim.4), channel_id=1, replica_groups={{0,32,64,96,128,160,192,224,256,288,320,352,384,416,448,480},{8,40,72,1..., dimensions={0} | all-to-all | bytes 32768 | tf_op jit(solution)/shard_map/all_to_all | solution.py:395
  85.9 12.1 %all_to_all.17.both_ref = f32[32,2,128]{2,1,0:T(2,128)S(1)} all-to-all(f32[32,2,128]{2,1,0:T(2,128)S(1)} %broadcast_in_dim.5), channel_id=1, replica_groups={{0,1,2,3,4,5,6,7,8,9,10,11,12,13,14,15,16,17,18,19,20,21,22,23,24,25,26..., dimensions={0} | all-to-all | bytes 65536 | tf_op jit(solution)/shard_map/all_to_all | solution.py:397
  98.0 2.9 %shard_map.93 = (f32[64,1024]{1,0:T(8,128)}, f32[64,64]{1,0:T(8,128)}) custom-call(f32[32,2,128]{2,1,0:T(2,128)S(1)} %all_to_all.17.both_ref, f32[64,1024]{1,0:T(8,128)S(1)} %get-tuple-element.27.y_ref), custom_call_target="tpu_custom_call" | custom-call | tf_op jit(solution)/shard_map/pallas_call | solution.py:268
  (4 shorter events, 0.1 us)
Async XLA Ops:
  2.6 26.2 %collective-permute-start.2 = (bf16[64,1024]{1,0:T(8,128)(2,1)S(1)}, bf16[64,1024]{1,0:T(8,128)(2,1)S(1)}, u32[]{:S(2)}, u32[]{:S(2)}) collective-permute-start(bf16[64,1024]{1,0:T(8,128)(2,1)S(1)} %get-tuple-element.17.z_ref), channel_id=1, source_target_pairs={{0,1},{1,0},{2,3},{3,2},{4,5},{5,4},{6,7},{7,6},{8,9},{9,8},{10,11... | collective-permute-start | bytes 393224 | tf_op jit(solution)/shard_map/ppermute | solution.py:290
  11.4 17.4 %collective-permute-start = (bf16[64,1024]{1,0:T(8,128)(2,1)S(1)}, bf16[64,1024]{1,0:T(8,128)(2,1)S(1)}, u32[]{:S(2)}, u32[]{:S(2)}) collective-permute-start(bf16[64,1024]{1,0:T(8,128)(2,1)S(1)} %get-tuple-element.17.z_ref), channel_id=1, source_target_pairs={{0,504},{8,0},{16,8},{24,16},{32,24},{40,32},{48,40},{56,48},{64,5... | collective-permute-start | bytes 393224 | tf_op jit(solution)/shard_map/ppermute | solution.py:287
  19.4 9.4 %collective-permute-start.1 = (bf16[416,128]{1,0:T(8,128)(2,1)S(1)}, bf16[416,128]{1,0:T(8,128)(2,1)S(1)}, u32[]{:S(2)}, u32[]{:S(2)}) collective-permute-start(bf16[416,128]{1,0:T(8,128)(2,1)S(1)} %get-tuple-element.22), channel_id=1, source_target_pairs={{0,8},{8,16},{16,24},{24,32},{32,40},{40,48},{48,56},{56,64},{64,7... | collective-permute-start | bytes 319496 | tf_op jit(solution)/shard_map/ppermute | solution.py:287
  21.9 6.9 %copy-start = (f32[64,1024]{1,0:T(8,128)S(1)}, f32[64,1024]{1,0:T(8,128)}, u32[]{:S(2)}) copy-start(f32[64,1024]{1,0:T(8,128)} %v_ref.1) | copy-start | bytes 786436
  22.0 6.9 %copy-start.1 = (s32[1024]{0:T(1024)S(1)}, s32[1024]{0:T(1024)}, u32[]{:S(2)}) copy-start(s32[1024]{0:T(1024)} %param.12) | copy-start | bytes 12292
  30.1 13.8 %collective-permute-start.5 = (bf16[128,1024]{1,0:T(8,128)(2,1)S(1)}, bf16[128,1024]{1,0:T(8,128)(2,1)S(1)}, u32[]{:S(2)}, u32[]{:S(2)}) collective-permute-start(bf16[128,1024]{1,0:T(8,128)(2,1)S(1)} %get-tuple-element.23.z_ref), channel_id=1, source_target_pairs={{0,1},{1,0},{2,3},{3,2},{4,5},{5,4},{6,7},{7,6},{8,9},{9,8},{10,11... | collective-permute-start | bytes 786440 | tf_op jit(solution)/shard_map/ppermute | solution.py:290
  33.2 6.9 %collective-permute-start.3 = (bf16[128,256]{1,0:T(8,128)(2,1)S(1)}, bf16[128,256]{1,0:T(8,128)(2,1)S(1)}, u32[]{:S(2)}, u32[]{:S(2)}) collective-permute-start(bf16[128,256]{1,0:T(8,128)(2,1)S(1)} %get-tuple-element.25), channel_id=1, source_target_pairs={{0,504},{8,0},{16,8},{24,16},{32,24},{40,32},{48,40},{56,48},{64,5... | collective-permute-start | bytes 196616 | tf_op jit(solution)/shard_map/ppermute | solution.py:287
  35.1 8.8 %collective-permute-start.4 = (bf16[128,256]{1,0:T(8,128)(2,1)S(1)}, bf16[128,256]{1,0:T(8,128)(2,1)S(1)}, u32[]{:S(2)}, u32[]{:S(2)}) collective-permute-start(bf16[128,256]{1,0:T(8,128)(2,1)S(1)} %get-tuple-element.26), channel_id=1, source_target_pairs={{0,8},{8,16},{16,24},{24,32},{32,40},{40,48},{48,56},{56,64},{64,7... | collective-permute-start | bytes 196616 | tf_op jit(solution)/shard_map/ppermute | solution.py:287
  45.5 8.3 %collective-permute-start.7 = (bf16[128,1024]{1,0:T(8,128)(2,1)S(1)}, bf16[128,1024]{1,0:T(8,128)(2,1)S(1)}, u32[]{:S(2)}, u32[]{:S(2)}) collective-permute-start(bf16[128,1024]{1,0:T(8,128)(2,1)S(1)} %get-tuple-element.28.z_ref), channel_id=1, source_target_pairs={{0,1},{1,0},{2,3},{3,2},{4,5},{5,4},{6,7},{7,6},{8,9},{9,8},{10,11... | collective-permute-start | bytes 786440 | tf_op jit(solution)/shard_map/ppermute | solution.py:290
  48.3 5.5 %collective-permute-start.6 = (bf16[128,256]{1,0:T(8,128)(2,1)S(1)}, bf16[128,256]{1,0:T(8,128)(2,1)S(1)}, u32[]{:S(2)}, u32[]{:S(2)}) collective-permute-start(bf16[128,256]{1,0:T(8,128)(2,1)S(1)} %get-tuple-element.31), channel_id=1, source_target_pairs={{0,504},{8,0},{16,8},{24,16},{32,24},{40,32},{48,40},{56,48},{64,5... | collective-permute-start | bytes 196616 | tf_op jit(solution)/shard_map/ppermute | solution.py:287

commit v3 on v2

--- a/solution.py
+++ b/solution.py
@@ -12,6 +12,7 @@
 CROSS = 2
 ALONG_X = 4
 SUBLANES = 8
+TILE_ROWS = 16
 PANEL = 8
 BOTH = ("blk", "scale")
 FULL = lax.Precision.HIGHEST
@@ -43,6 +44,10 @@
 def split(value):
     high = value.astype(BF16)
     return jnp.concatenate([high, (value - high.astype(F32)).astype(BF16)], axis=0)
+
+
+def even_group():
+    return lax.rem(lax.axis_index("blk"), 2) == 0
 
 
 def first_kernel(
@@ -53,16 +58,17 @@
     tgt_hbm,
     dinv_ref,
     scaled_ref,
-    ahead_ref,
+    inner_ref,
+    outer_ref,
     blocks_ref,
     col_ref,
     tgt_ref,
     x_ref,
     degree_ref,
-    s3,
+    ahead_ref,
     sems,
 ):
-    k = x_ref.shape[0]
+    rb, k, _ = scaled_ref.shape
     far, near = pl.ds(0, CROSS), pl.ds(CROSS, blocks_ref.shape[0] - CROSS)
     moves = [
         (degree_hbm, degree_ref),
@@ -79,44 +85,55 @@
         copy.wait()
     dinv = 1.0 / jnp.sqrt(degree_ref[...].astype(F32))
     dinv_ref[...] = dinv
-    scaled = (x_ref[...] * dinv).astype(BF16)
-    scaled_ref[...] = scaled
-    for j in range(s3.shape[0]):
-        s3[j] = scaled[:, lanes(j)]
+    for j in range(rb):
+        scaled_ref[j] = (x_ref[:, lanes(j)] * dinv[:, lanes(j)]).astype(BF16)
+    rows, picks, places = payload_rows(k)
+    ahead_ref[...] = jnp.zeros_like(ahead_ref)
     for c in range(CROSS):
-        ahead_ref[c * BLOCK : (c + 1) * BLOCK] = blocks_ref[c]
-        at = CROSS * BLOCK + c * k
-        ahead_ref[at : at + k] = s3[col_ref[c]]
-        at = CROSS * (BLOCK + k) + c * 16
-        row = jnp.full((16, BLOCK), tgt_ref[c] - s3.shape[0], jnp.int32)
-        ahead_ref[at : at + 16] = row.astype(F32).astype(BF16)
+        ahead_ref[rows[c]] = blocks_ref[c]
+        ahead_ref[picks[c]] = scaled_ref[col_ref[c]]
+        place = jnp.full((TILE_ROWS, BLOCK), tgt_ref[c] - rb, jnp.int32)
+        ahead_ref[places[c]] = place.astype(F32).astype(BF16)
+    even = even_group()
+    ahead = ahead_ref[...]
+    back = jnp.concatenate([scaled_ref[j] for j in range(rb)], axis=0)
+    inner_ref[...] = jnp.where(even, ahead, back)
+    outer_ref[...] = jnp.where(even, back, ahead)
     copies[5].wait()
 
 
-def near_kernel(z_ref, blocks_ref, col_ref, tgt_ref, count_ref, out_ref, s3, acc):
-    rb = s3.shape[0]
-    k = out_ref.shape[0]
-    for j in range(rb):
-        s3[j] = z_ref[:, lanes(j)]
+def payload_rows(k):
+    sizes = [BLOCK] * CROSS + [k] * CROSS + [TILE_ROWS] * CROSS
+    starts = [sum(sizes[:i]) for i in range(len(sizes))]
+    spans = [slice(at, at + size) for at, size in zip(starts, sizes)]
+    return spans[:CROSS], spans[CROSS : 2 * CROSS], spans[2 * CROSS :]
+
+
+def near_kernel(z_ref, blocks_ref, col_ref, tgt_ref, count_ref, out_ref, acc):
+    rb, k, _ = out_ref.shape
     acc[...] = jnp.zeros_like(acc)
     count = count_ref[0]
     for c in range(CROSS, blocks_ref.shape[0]):
         live = c < count
         column, target = col_ref[c], tgt_ref[c]
         weights = blocks_ref[c]
-        forward = fold(times_t(s3[column], weights), k)
-        backward = fold(times(s3[target], weights), k)
+        forward = fold(times_t(z_ref[column], weights), k)
+        backward = fold(times(z_ref[target], weights), k)
         acc[jnp.where(live, target, rb)] += forward
         acc[jnp.where(live, column, rb)] += backward
     for j in range(rb):
-        out_ref[:, lanes(j)] = acc[j]
+        out_ref[j] = acc[j]
+
+
+def side_by_side(ref):
+    return jnp.concatenate([ref[j] for j in range(ref.shape[0])], axis=1)
 
 
 def crossed_block(part_ref, partner_ref, j, k):
     nodes = partner_ref.shape[1]
     ids = lax.broadcasted_iota(jnp.int32, (nodes, BLOCK), 0)
     onehot = jnp.where(ids == partner_ref[:, lanes(j)], 1.0, 0.0).astype(BF16)
-    return fold(times(part_ref[...], onehot), k)
+    return fold(times(side_by_side(part_ref), onehot), k)
 
 
 def finish_kernel(
@@ -124,75 +141,88 @@
     near_ref,
     v_ref,
     dinv_ref,
-    next_ref,
-    prev_ref,
-    pay_ref,
+    inner_ref,
+    outer_ref,
+    pay_inner_ref,
+    pay_outer_ref,
     part_ref,
     partner_ref,
-    far_ref,
+    blocks_ref,
     col_ref,
     tgt_ref,
     y_ref,
     z_ref,
     *rest,
 ):
+    sends, (tot,) = rest[:-1], rest[-1:]
     k = v_ref.shape[0]
     rb = v_ref.shape[1] // BLOCK
-    back_ref, tot, z3 = rest[-3:]
+    even = even_group()
     for j in range(rb):
-        tot[j] = near_ref[:, lanes(j)] + crossed_block(part_ref, partner_ref, j, k)
+        tot[j] = near_ref[j] + crossed_block(part_ref, partner_ref, j, k)
+    rows, picks, spots = payload_rows(k)
     places = []
     for c in range(CROSS):
-        at = CROSS * (BLOCK + k) + c * 16
-        place = pay_ref[at : at + 16, :].astype(F32)[0:1]
-        places.append(place)
+        sent = jnp.where(even, pay_outer_ref[spots[c]], pay_inner_ref[spots[c]])
+        places.append(sent.astype(F32)[0:1])
         if first:
-            theirs = next_ref[:, pl.ds(pl.multiple_of((tgt_ref[c] - rb) * BLOCK, BLOCK), BLOCK)]
-            at = CROSS * BLOCK + c * k
-            behind = pay_ref[at : at + k]
+            at = pl.ds(pl.multiple_of((tgt_ref[c] - rb) * k, k), k)
+            theirs = jnp.where(even, inner_ref[at], outer_ref[at])
+            behind = jnp.where(even, pay_outer_ref[picks[c]], pay_inner_ref[picks[c]])
         else:
-            theirs = next_ref[:, lanes(c)]
-            behind = prev_ref[:, lanes(c)]
-        tot[col_ref[c]] += fold(times(theirs, far_ref[c]), k)
-        landed = fold(times_t(behind, pay_ref[c * BLOCK : (c + 1) * BLOCK]), k)
+            theirs = jnp.where(even, inner_ref[:, lanes(c)], outer_ref[:, lanes(c)])
+            behind = jnp.where(even, outer_ref[:, lanes(c)], inner_ref[:, lanes(c)])
+        weights = jnp.where(even, pay_outer_ref[rows[c]], pay_inner_ref[rows[c]])
+        tot[col_ref[c]] += fold(times(theirs, blocks_ref[c]), k)
+        landed = fold(times_t(behind, weights), k)
         for j in range(rb):
-            tot[j] += jnp.where(place == j, landed, 0.0)
+            tot[j] += jnp.where(places[c] == j, landed, 0.0)
     for j in range(rb):
         dinv = dinv_ref[:, lanes(j)]
         y = v_ref[:, lanes(j)] + dinv * tot[j]
-        z = split(y * dinv)
         y_ref[:, lanes(j)] = y
-        z_ref[:, lanes(j)] = z
-        z3[j] = z
+        z_ref[j] = split(y * dinv)
     for c in range(CROSS):
+        wanted = jnp.zeros(z_ref.shape[1:], F32)
+        for j in range(rb):
+            wanted = jnp.where(places[c] == j, z_ref[j].astype(F32), wanted)
+        back = wanted.astype(BF16)
         if first:
-            rest[0][:, lanes(c)] = z3[col_ref[c]]
-        wanted = jnp.zeros(z3.shape[1:], F32)
-        for j in range(rb):
-            wanted = jnp.where(places[c] == j, z3[j].astype(F32), wanted)
-        back_ref[:, lanes(c)] = wanted.astype(BF16)
+            ahead = z_ref[col_ref[c]]
+            sends[0][:, lanes(c)] = jnp.where(even, ahead, back)
+            sends[1][:, lanes(c)] = jnp.where(even, back, ahead)
+        else:
+            sends[0][:, lanes(c)] = back
 
 
 def form_kernel(
-    y_ref, z_ref, dinv_ref, blocks_ref, partner_ref, col_ref, tgt_ref, count_ref, right_ref, out_ref, s3, acc
+    y_ref,
+    z_ref,
+    dinv_ref,
+    blocks_ref,
+    partner_ref,
+    col_ref,
+    tgt_ref,
+    count_ref,
+    right_ref,
+    out_ref,
+    acc,
 ):
-    rb = s3.shape[0]
-    k = y_ref.shape[0]
-    for j in range(rb):
-        s3[j] = z_ref[:, lanes(j)]
+    rb = z_ref.shape[0]
+    k, nodes = y_ref.shape
     acc[...] = jnp.zeros_like(acc)
     count = count_ref[0]
     for c in range(blocks_ref.shape[0]):
-        forward = fold(times_t(s3[col_ref[c]], blocks_ref[c]), k)
+        forward = fold(times_t(z_ref[col_ref[c]], blocks_ref[c]), k)
         if c < CROSS:
             right_ref[:, lanes(rb + c)] = forward
         else:
             acc[jnp.where(c < count, tgt_ref[c], rb)] += forward
-    nodes = y_ref.shape[1]
+    mine = side_by_side(z_ref)
     for j in range(rb):
         ids = lax.broadcasted_iota(jnp.int32, (BLOCK, nodes), 0) + j * BLOCK
         onehot = jnp.where(ids == partner_ref[...], 0.5, 0.0).astype(BF16)
-        right_ref[:, lanes(j)] = fold(times_t(z_ref[...], onehot), k)
+        right_ref[:, lanes(j)] = fold(times_t(mine, onehot), k)
     y = y_ref[...]
     z = y * dinv_ref[...]
     near = jnp.concatenate([acc[j] for j in range(rb)], axis=1)
@@ -202,7 +232,7 @@
 
 def pair_kernel(right_ref, sums_ref, next_ref, part_ref, out_ref):
     k = right_ref.shape[0]
-    theirs = jnp.concatenate([part_ref[...], next_ref[...]], axis=1).astype(F32)
+    theirs = jnp.concatenate([side_by_side(part_ref), next_ref[...]], axis=1).astype(F32)
     form = times_t(theirs[:k] + theirs[k:], right_ref[...], FULL)
     both = sums_ref[...] + jnp.concatenate([jnp.zeros((k, k), F32), form], axis=1)
     rows = out_ref.shape[1]
@@ -283,20 +313,26 @@
     degree = degree.reshape(1, nodes)
     partner = partner.reshape(1, nodes)
 
-    def shifted(array, distance):
-        return lax.ppermute(array, "blk", [(i, (i + distance) % blk) for i in range(blk)])
+    def moved(array, target):
+        return lax.ppermute(array, "blk", [(i, target(i) % blk) for i in range(blk)])
 
     def swapped(array):
         return lax.ppermute(array, "scale", [(i, i ^ 1) for i in range(scale)])
 
-    pay_rows = CROSS * (BLOCK + k + 16)
-    dinv, scaled, ahead, blocks, column, target = call(
+    def inner(i):
+        return i + 1 - 2 * (i % 2)
+
+    def outer(i):
+        return i - 1 + 2 * (i % 2)
+
+    dinv, scaled, to_inner, to_outer, blocks, column, target = call(
         first_kernel,
         [pl.BlockSpec(memory_space=pltpu.HBM)] * 5,
         [
             ((1, nodes), F32),
-            ((k, nodes), BF16),
-            ((pay_rows, BLOCK), BF16),
+            ((rb, k, BLOCK), BF16),
+            ((rb * k, BLOCK), BF16),
+            ((rb * k, BLOCK), BF16),
             (blocks.shape, BF16),
             (block_column.shape, jnp.int32),
             (block_target.shape, jnp.int32),
@@ -304,22 +340,22 @@
         [
             pltpu.VMEM((k, nodes), F32),
             pltpu.VMEM((1, nodes), jnp.int32),
-            pltpu.VMEM((rb, k, BLOCK), BF16),
+            pltpu.VMEM((rb * k, BLOCK), BF16),
             pltpu.SemaphoreType.DMA((6,)),
         ],
         *[
             pltpu.with_memory_space_constraint(array, pltpu.HBM)
             for array in (start_block, degree, blocks, block_column, block_target)
         ],
-        out_specs=[VMEM] * 4 + [SMEM] * 2,
+        out_specs=[VMEM] * 5 + [SMEM] * 2,
     )
 
     def near(z):
         return call(
             near_kernel,
             [VMEM, VMEM, SMEM, SMEM, SMEM],
-            [((k, nodes), F32)],
-            [pltpu.VMEM((rb, z.shape[0], BLOCK), BF16), pltpu.VMEM((rb + 1, k, BLOCK), F32)],
+            [((rb, k, BLOCK), F32)],
+            [pltpu.VMEM((rb + 1, k, BLOCK), F32)],
             z,
             blocks,
             column,
@@ -327,20 +363,21 @@
             block_count,
         )[0]
 
-    def finish(first, near_sum, v, from_next, from_prev, part):
-        outs = [((k, nodes), F32), ((2 * k, nodes), BF16)]
+    def finish(first, near_sum, v, from_inner, from_outer, part):
+        outs = [((k, nodes), F32), ((rb, 2 * k, BLOCK), BF16)]
         outs += [((2 * k, CROSS * BLOCK), BF16)] * (2 if first else 1)
         return call(
             functools.partial(finish_kernel, first),
-            [VMEM] * 9 + [SMEM, SMEM],
+            [VMEM] * 10 + [SMEM, SMEM],
             outs,
-            [pltpu.VMEM((rb, k, BLOCK), F32), pltpu.VMEM((rb, 2 * k, BLOCK), BF16)],
+            [pltpu.VMEM((rb, k, BLOCK), F32)],
             near_sum,
             v,
             dinv,
-            from_next,
-            from_prev,
-            pay,
+            from_inner,
+            from_outer,
+            pay_inner,
+            pay_outer,
             part,
             partner,
             blocks,
@@ -348,23 +385,25 @@
             target,
         )
 
-    pay = shifted(ahead, 1)
-    from_next = shifted(scaled, -1)
+    pay_outer = moved(to_outer, outer)
+    pay_inner = moved(to_inner, inner)
     part = swapped(scaled)
-    first_image, z, ahead, back = finish(True, near(scaled), start_block, from_next, pay, part)
-
-    from_prev = shifted(ahead, 1)
-    from_next = shifted(back, -1)
+    first_image, z, to_inner, to_outer = finish(
+        True, near(scaled), start_block, pay_inner, pay_outer, part
+    )
+
+    from_outer = moved(to_outer, outer)
+    from_inner = moved(to_inner, inner)
     part = swapped(z)
-    images, z, back = finish(False, near(z), first_image, from_next, from_prev, part)
-
-    from_next = shifted(back, -1)
+    images, z, back = finish(False, near(z), first_image, from_inner, from_outer, part)
+
+    from_next = moved(back, lambda i: i - 1)
     part = swapped(z)
     right, sums = call(
         form_kernel,
         [VMEM] * 5 + [SMEM] * 3,
         [((k, nodes + CROSS * BLOCK), F32), ((k, 2 * k), F32)],
-        [pltpu.VMEM((rb, 2 * k, BLOCK), BF16), pltpu.VMEM((rb + 1, k, BLOCK), F32)],
+        [pltpu.VMEM((rb + 1, k, BLOCK), F32)],
         images,
         z,
         dinv,

time: 101 us -> 99.8 us (0.988)
  waiting for transfers between devices: 10.4 us -> 1.05 us
  starting transfers between devices: 31.7 us -> 38.4 us
  blocking collectives: 43.6 us -> 44.7 us
    ppermute x5, starting transfers between devices: 17.1 us -> 29.8 us  [moved(): lax.ppermute(array, 'blk', [(i, target(i) % blk) for i in range(blk)])]
    ppermute x5, waiting for transfers between devices: 10.4 us -> 1.05 us  [moved(): lax.ppermute(array, 'blk', [(i, target(i) % blk) for i in range(blk)])]
    ppermute x3, starting transfers between devices: 14.6 us -> 8.62 us  [swapped(): return lax.ppermute(array, 'scale', [(i, i ^ 1) for i in range(scale)])]
    all_to_all x1, blocking collectives: 18.9 us -> 20.6 us  [shards(): piece = lax.all_to_all(piece, 'blk', 0, 0, axis_index_groups=columns).sum(0)]
  transfers between devices with their start and end apart: 8 -> 8, of which waited for: 3 -> 1; matrix products, arithmetic and copies ran while one was open for 0% -> 0% of each run, Pallas kernels for 6% -> 6%
where the time goes in v3:
time: 99.8 us; the launch traced here: 99.3 us
  blocking collectives  44.7 us (45%)
  starting transfers between devices  38.4 us (38%)
  Pallas kernels  13.6 us (14%)
  between operations  1.48 us (1%)
  waiting for transfers between devices  1.05 us (1%)
    ppermute x5, starting transfers between devices, moved(): lax.ppermute(array, 'blk', [(i, target(i) % blk) for i in range(blk)])  29.8 us
    all_to_all x1, blocking collectives, shards(): piece = lax.all_to_all(piece, 'blk', 0, 0, axis_index_groups=columns).sum(0)  20.6 us
    pallas_call x8, Pallas kernels, call(): pl.pallas_call(kernel, out_shape=[jax.ShapeDtypeStruct(shape, dtype) for...  13.6 us
    all_to_all x1, blocking collectives, shards(): both = lax.all_to_all(piece, BOTH, 0, 0, axis_index_groups=planes)  12.1 us
    all_to_all x1, blocking collectives, shards(): piece = lax.all_to_all(mine, BOTH, 0, 0, axis_index_groups=planes).sum(0)  12 us
    ppermute x3, starting transfers between devices, swapped(): return lax.ppermute(array, 'scale', [(i, i ^ 1) for i in range(scale)])  8.62 us
  transfers between devices with their start and end apart: 8, of which 1 were waited for; matrix products, arithmetic and copies ran while one was open for 0% of the time, Pallas kernels for 6%

profile of v3, /device:TPU:1, one launch (start us, length us, event | category | flops | bytes accessed | tf_op | source)
XLA Modules:
  0.0 99.3 jit_solution(16583873983712872016)
XLA Ops:
  0.6 2.0 %shard_map.86 = (f32[1,1024]{1,0:T(1,128)S(1)}, bf16[8,64,128]{2,1,0:T(8,128)(2,1)S(1)}, bf16[512,128]{1,0:T(8,128)(2,1)S(1)}, bf16[512,128]{1,0:T(8,128)(2,1)S(...) custom-call(f32[64,1024]{1,0:T(8,128)} %v_ref.1, s32[1,1024]{1,0:T(1,128)} %bitcast.5, ...), custom_call_target="tpu_custom_call" | custom-call | tf_op jit(solution)/shard_map/pallas_call | solution.py:298
  2.6 3.9 %collective-permute-start = (bf16[512,128]{1,0:T(8,128)(2,1)S(1)}, bf16[512,128]{1,0:T(8,128)(2,1)S(1)}, u32[]{:S(2)}, u32[]{:S(2)}) collective-permute-start(bf16[512,128]{1,0:T(8,128)(2,1)S(1)} %get-tuple-element.23), channel_id=1, source_target_pairs={{0,8},{8,0},{16,24},{24,16},{32,40},{40,32},{48,56},{56,48},{64,72... | collective-permute-start | bytes 393224 | tf_op jit(solution)/shard_map/ppermute | solution.py:317
  6.6 12.7 %collective-permute-start.1 = (bf16[512,128]{1,0:T(8,128)(2,1)S(1)}, bf16[512,128]{1,0:T(8,128)(2,1)S(1)}, u32[]{:S(2)}, u32[]{:S(2)}) collective-permute-start(bf16[512,128]{1,0:T(8,128)(2,1)S(1)} %get-tuple-element.24), channel_id=1, source_target_pairs={{0,504},{8,16},{16,8},{24,32},{32,24},{40,48},{48,40},{56,64},{64,... | collective-permute-start | bytes 393224 | tf_op jit(solution)/shard_map/ppermute | solution.py:317
  19.2 3.1 %collective-permute-start.2 = (bf16[8,64,128]{2,1,0:T(8,128)(2,1)S(1)}, bf16[8,64,128]{2,1,0:T(8,128)(2,1)S(1)}, u32[]{:S(2)}, u32[]{:S(2)}) collective-permute-start(bf16[8,64,128]{2,1,0:T(8,128)(2,1)S(1)} %get-tuple-element.18.z_ref), channel_id=1, source_target_pairs={{0,1},{1,0},{2,3},{3,2},{4,5},{5,4},{6,7},{7,6},{8,9},{9,8},{10,11... | collective-permute-start | bytes 393224 | tf_op jit(solution)/shard_map/ppermute | solution.py:320
  23.0 0.0 copy-start
  23.0 0.0 copy-start.1
  23.1 1.5 %shard_map.87.near_ref = f32[8,64,128]{2,1,0:T(8,128)S(1)} custom-call(bf16[8,64,128]{2,1,0:T(8,128)(2,1)S(1)} %get-tuple-element.18.z_ref, bf16[32,128,128]{2,1,0:T(8,128)(2,1)S(1)} %get-tuple-element.19.blocks_ref, s32[32]{0:T(128)S(1)} %get-tuple-element.20.col_ref, s32[32]{0:T(128)S(1)} %get-tuple-element.21.tgt_ref, s32[1]{0:T(128)S(6)} %copy.11.count_ref), custom_call_target="tpu_custom_call" | custom-call | tf_op jit(solution)/shard_map/pallas_call | solution.py:298
  24.6 0.0 collective-permute-done.inner_ref.pay_inner_ref
  24.6 0.0 collective-permute-done.1.outer_ref.pay_outer_ref
  24.6 0.0 collective-permute-done.2.part_ref
  24.6 0.0 copy-done
  24.6 0.0 copy-done.1
  24.6 1.2 %shard_map.88 = (f32[64,1024]{1,0:T(8,128)S(1)}, bf16[8,128,128]{2,1,0:T(8,128)(2,1)S(1)}, bf16[128,256]{1,0:T(8,128)(2,1)S(1)}, bf16[128,256]{1,0:T(8,128)(2,1)S(1)}) custom-call(f32[8,64,128]{2,1,0:T(8,128)S(1)} %shard_map.87.near_ref, f32[64,1024]{1,0:T(8,128)S(1)} %copy-done, f32[1,1024]{1,0:T(1,128)S(1)} %get-tuple-element.22.dinv_ref, ...), custom_call_target="tpu_custom_call" | custom-call | tf_op jit(solution)/shard_map/pallas_call | solution.py:298
  25.9 1.9 %collective-permute-start.5 = (bf16[8,128,128]{2,1,0:T(8,128)(2,1)S(1)}, bf16[8,128,128]{2,1,0:T(8,128)(2,1)S(1)}, u32[]{:S(2)}, u32[]{:S(2)}) collective-permute-start(bf16[8,128,128]{2,1,0:T(8,128)(2,1)S(1)} %get-tuple-element.25.z_ref), channel_id=1, source_target_pairs={{0,1},{1,0},{2,3},{3,2},{4,5},{5,4},{6,7},{7,6},{8,9},{9,8},{10,11... | collective-permute-start | bytes 786440 | tf_op jit(solution)/shard_map/ppermute | solution.py:320
  27.8 1.9 %collective-permute-start.3 = (bf16[128,256]{1,0:T(8,128)(2,1)S(1)}, bf16[128,256]{1,0:T(8,128)(2,1)S(1)}, u32[]{:S(2)}, u32[]{:S(2)}) collective-permute-start(bf16[128,256]{1,0:T(8,128)(2,1)S(1)} %get-tuple-element.27), channel_id=1, source_target_pairs={{0,8},{8,0},{16,24},{24,16},{32,40},{40,32},{48,56},{56,48},{64,72... | collective-permute-start | bytes 196616 | tf_op jit(solution)/shard_map/ppermute | solution.py:317
  29.7 5.7 %collective-permute-start.4 = (bf16[128,256]{1,0:T(8,128)(2,1)S(1)}, bf16[128,256]{1,0:T(8,128)(2,1)S(1)}, u32[]{:S(2)}, u32[]{:S(2)}) collective-permute-start(bf16[128,256]{1,0:T(8,128)(2,1)S(1)} %get-tuple-element.28), channel_id=1, source_target_pairs={{0,504},{8,16},{16,8},{24,32},{32,24},{40,48},{48,40},{56,64},{64,... | collective-permute-start | bytes 196616 | tf_op jit(solution)/shard_map/ppermute | solution.py:317
  35.5 1.5 %shard_map.89.near_ref = f32[8,64,128]{2,1,0:T(8,128)S(1)} custom-call(bf16[8,128,128]{2,1,0:T(8,128)(2,1)S(1)} %get-tuple-element.25.z_ref, bf16[32,128,128]{2,1,0:T(8,128)(2,1)S(1)} %get-tuple-element.19.blocks_ref, s32[32]{0:T(128)S(1)} %get-tuple-element.20.col_ref, s32[32]{0:T(128)S(1)} %get-tuple-element.21.tgt_ref, s32[1]{0:T(128)S(6)} %copy.11.count_ref), custom_call_target="tpu_custom_call" | custom-call | tf_op jit(solution)/shard_map/pallas_call | solution.py:298
  37.0 0.0 collective-permute-done.3.inner_ref
  37.0 1.0 %collective-permute-done.4.outer_ref = bf16[128,256]{1,0:T(8,128)(2,1)S(1)} collective-permute-done((bf16[128,256]{1,0:T(8,128)(2,1)S(1)}, bf16[128,256]{1,0:T(8,128)(2,1)S(1)}, u32[]{:S(2)}, u32[]{:S(2)}) %collective-permute-start.4) | collective-permute-done | bytes 65568 | tf_op jit(solution)/shard_map/ppermute | solution.py:317
  38.0 0.0 collective-permute-done.5.part_ref
  38.0 1.4 %shard_map.90 = (f32[64,1024]{1,0:T(8,128)S(1)}, bf16[8,128,128]{2,1,0:T(8,128)(2,1)S(1)}, bf16[128,256]{1,0:T(8,128)(2,1)S(1)}) custom-call(f32[8,64,128]{2,1,0:T(8,128)S(1)} %shard_map.89.near_ref, f32[64,1024]{1,0:T(8,128)S(1)} %get-tuple-element.26.v_ref, f32[1,1024]{1,0:T(1,128)S(1)} %get-tuple-element.22.dinv_ref, ...), custom_call_target="tpu_custom_call" | custom-call | tf_op jit(solution)/shard_map/pallas_call | solution.py:298
  39.5 3.6 %collective-permute-start.7 = (bf16[8,128,128]{2,1,0:T(8,128)(2,1)S(1)}, bf16[8,128,128]{2,1,0:T(8,128)(2,1)S(1)}, u32[]{:S(2)}, u32[]{:S(2)}) collective-permute-start(bf16[8,128,128]{2,1,0:T(8,128)(2,1)S(1)} %get-tuple-element.30.z_ref), channel_id=1, source_target_pairs={{0,1},{1,0},{2,3},{3,2},{4,5},{5,4},{6,7},{7,6},{8,9},{9,8},{10,11... | collective-permute-start | bytes 786440 | tf_op jit(solution)/shard_map/ppermute | solution.py:320
  43.1 5.5 %collective-permute-start.6 = (bf16[128,256]{1,0:T(8,128)(2,1)S(1)}, bf16[128,256]{1,0:T(8,128)(2,1)S(1)}, u32[]{:S(2)}, u32[]{:S(2)}) collective-permute-start(bf16[128,256]{1,0:T(8,128)(2,1)S(1)} %get-tuple-element.33), channel_id=1, source_target_pairs={{0,504},{8,0},{16,8},{24,16},{32,24},{40,32},{48,40},{56,48},{64,5... | collective-permute-start | bytes 196616 | tf_op jit(solution)/shard_map/ppermute | solution.py:317
  48.6 2.4 %shard_map.91 = (f32[64,1280]{1,0:T(8,128)S(1)}, f32[64,128]{1,0:T(8,128)S(1)}) custom-call(f32[64,1024]{1,0:T(8,128)S(1)} %get-tuple-element.29.y_ref, bf16[8,128,128]{2,1,0:T(8,128)(2,1)S(1)} %get-tuple-element.30.z_ref, f32[1,1024]{1,0:T(1,128)S(1)} %get-tuple-element.22.dinv_ref, bf16[32,128,128]{2,1,0:T(8,128)(2,1)S(1)} %get-tuple-element.19.blocks_ref, ...), custom_call_target="tpu_custom_call" | custom-call | tf_op jit(solution)/shard_map/pallas_call | solution.py:298
  51.0 0.0 collective-permute-done.6.next_ref
  51.0 0.0 collective-permute-done.7.part_ref
  51.0 0.5 shard_map.92
  51.5 12.0 %all_to_all.15 = f32[32,2,128]{2,1,0:T(2,128)S(1)} all-to-all(f32[32,2,128]{2,1,0:T(2,128)S(1)} %shard_map.92), channel_id=1, replica_groups={{0,1,2,3,4,5,6,7,8,9,10,11,12,13,14,15,16,17,18,19,20,21,22,23,24,25,26..., dimensions={0} | all-to-all | bytes 65536 | tf_op jit(solution)/shard_map/all_to_all | solution.py:432
  63.6 20.6 %all_to_all.16 = f32[16,2,128]{2,1,0:T(2,128)S(1)} all-to-all(f32[16,2,128]{2,1,0:T(2,128)S(1)} %broadcast_in_dim.4), channel_id=1, replica_groups={{0,32,64,96,128,160,192,224,256,288,320,352,384,416,448,480},{8,40,72,1..., dimensions={0} | all-to-all | bytes 32768 | tf_op jit(solution)/shard_map/all_to_all | solution.py:434
  84.2 12.1 %all_to_all.17.both_ref = f32[32,2,128]{2,1,0:T(2,128)S(1)} all-to-all(f32[32,2,128]{2,1,0:T(2,128)S(1)} %broadcast_in_dim.5), channel_id=1, replica_groups={{0,1,2,3,4,5,6,7,8,9,10,11,12,13,14,15,16,17,18,19,20,21,22,23,24,25,26..., dimensions={0} | all-to-all | bytes 65536 | tf_op jit(solution)/shard_map/all_to_all | solution.py:436
  96.4 2.9 %shard_map.93 = (f32[64,1024]{1,0:T(8,128)}, f32[64,64]{1,0:T(8,128)}) custom-call(f32[32,2,128]{2,1,0:T(2,128)S(1)} %all_to_all.17.both_ref, f32[64,1024]{1,0:T(8,128)S(1)} %get-tuple-element.29.y_ref), custom_call_target="tpu_custom_call" | custom-call | tf_op jit(solution)/shard_map/pallas_call | solution.py:298
  (4 shorter events, 0.1 us)
Async XLA Ops:
  2.6 21.9 %collective-permute-start = (bf16[512,128]{1,0:T(8,128)(2,1)S(1)}, bf16[512,128]{1,0:T(8,128)(2,1)S(1)}, u32[]{:S(2)}, u32[]{:S(2)}) collective-permute-start(bf16[512,128]{1,0:T(8,128)(2,1)S(1)} %get-tuple-element.23), channel_id=1, source_target_pairs={{0,8},{8,0},{16,24},{24,16},{32,40},{40,32},{48,56},{56,48},{64,72... | collective-permute-start | bytes 393224 | tf_op jit(solution)/shard_map/ppermute | solution.py:317
  6.6 18.0 %collective-permute-start.1 = (bf16[512,128]{1,0:T(8,128)(2,1)S(1)}, bf16[512,128]{1,0:T(8,128)(2,1)S(1)}, u32[]{:S(2)}, u32[]{:S(2)}) collective-permute-start(bf16[512,128]{1,0:T(8,128)(2,1)S(1)} %get-tuple-element.24), channel_id=1, source_target_pairs={{0,504},{8,16},{16,8},{24,32},{32,24},{40,48},{48,40},{56,64},{64,... | collective-permute-start | bytes 393224 | tf_op jit(solution)/shard_map/ppermute | solution.py:317
  19.2 5.4 %collective-permute-start.2 = (bf16[8,64,128]{2,1,0:T(8,128)(2,1)S(1)}, bf16[8,64,128]{2,1,0:T(8,128)(2,1)S(1)}, u32[]{:S(2)}, u32[]{:S(2)}) collective-permute-start(bf16[8,64,128]{2,1,0:T(8,128)(2,1)S(1)} %get-tuple-element.18.z_ref), channel_id=1, source_target_pairs={{0,1},{1,0},{2,3},{3,2},{4,5},{5,4},{6,7},{7,6},{8,9},{9,8},{10,11... | collective-permute-start | bytes 393224 | tf_op jit(solution)/shard_map/ppermute | solution.py:320
  23.0 1.6 %copy-start = (f32[64,1024]{1,0:T(8,128)S(1)}, f32[64,1024]{1,0:T(8,128)}, u32[]{:S(2)}) copy-start(f32[64,1024]{1,0:T(8,128)} %v_ref.1) | copy-start | bytes 786436
  23.0 1.6 %copy-start.1 = (s32[1024]{0:T(1024)S(1)}, s32[1024]{0:T(1024)}, u32[]{:S(2)}) copy-start(s32[1024]{0:T(1024)} %param.12) | copy-start | bytes 12292
  25.9 12.2 %collective-permute-start.5 = (bf16[8,128,128]{2,1,0:T(8,128)(2,1)S(1)}, bf16[8,128,128]{2,1,0:T(8,128)(2,1)S(1)}, u32[]{:S(2)}, u32[]{:S(2)}) collective-permute-start(bf16[8,128,128]{2,1,0:T(8,128)(2,1)S(1)} %get-tuple-element.25.z_ref), channel_id=1, source_target_pairs={{0,1},{1,0},{2,3},{3,2},{4,5},{5,4},{6,7},{7,6},{8,9},{9,8},{10,11... | collective-permute-start | bytes 786440 | tf_op jit(solution)/shard_map/ppermute | solution.py:320
  27.8 9.2 %collective-permute-start.3 = (bf16[128,256]{1,0:T(8,128)(2,1)S(1)}, bf16[128,256]{1,0:T(8,128)(2,1)S(1)}, u32[]{:S(2)}, u32[]{:S(2)}) collective-permute-start(bf16[128,256]{1,0:T(8,128)(2,1)S(1)} %get-tuple-element.27), channel_id=1, source_target_pairs={{0,8},{8,0},{16,24},{24,16},{32,40},{40,32},{48,56},{56,48},{64,72... | collective-permute-start | bytes 196616 | tf_op jit(solution)/shard_map/ppermute | solution.py:317
  29.7 8.3 %collective-permute-start.4 = (bf16[128,256]{1,0:T(8,128)(2,1)S(1)}, bf16[128,256]{1,0:T(8,128)(2,1)S(1)}, u32[]{:S(2)}, u32[]{:S(2)}) collective-permute-start(bf16[128,256]{1,0:T(8,128)(2,1)S(1)} %get-tuple-element.28), channel_id=1, source_target_pairs={{0,504},{8,16},{16,8},{24,32},{32,24},{40,48},{48,40},{56,64},{64,... | collective-permute-start | bytes 196616 | tf_op jit(solution)/shard_map/ppermute | solution.py:317
  39.5 11.5 %collective-permute-start.7 = (bf16[8,128,128]{2,1,0:T(8,128)(2,1)S(1)}, bf16[8,128,128]{2,1,0:T(8,128)(2,1)S(1)}, u32[]{:S(2)}, u32[]{:S(2)}) collective-permute-start(bf16[8,128,128]{2,1,0:T(8,128)(2,1)S(1)} %get-tuple-element.30.z_ref), channel_id=1, source_target_pairs={{0,1},{1,0},{2,3},{3,2},{4,5},{5,4},{6,7},{7,6},{8,9},{9,8},{10,11... | collective-permute-start | bytes 786440 | tf_op jit(solution)/shard_map/ppermute | solution.py:320
  43.1 8.0 %collective-permute-start.6 = (bf16[128,256]{1,0:T(8,128)(2,1)S(1)}, bf16[128,256]{1,0:T(8,128)(2,1)S(1)}, u32[]{:S(2)}, u32[]{:S(2)}) collective-permute-start(bf16[128,256]{1,0:T(8,128)(2,1)S(1)} %get-tuple-element.33), channel_id=1, source_target_pairs={{0,504},{8,0},{16,8},{24,16},{32,24},{40,32},{48,40},{56,48},{64,5... | collective-permute-start | bytes 196616 | tf_op jit(solution)/shard_map/ppermute | solution.py:317

commit v4 on v3

--- a/solution.py
+++ b/solution.py
@@ -13,9 +13,9 @@
 ALONG_X = 4
 SUBLANES = 8
 TILE_ROWS = 16
+WIDE = 256
 PANEL = 8
 BOTH = ("blk", "scale")
-FULL = lax.Precision.HIGHEST
 F32 = jnp.float32
 BF16 = jnp.bfloat16
 
@@ -81,7 +81,7 @@
     copies = [pltpu.make_async_copy(src, dst, sems.at[i]) for i, (src, dst) in enumerate(moves)]
     for copy in copies:
         copy.start()
-    for copy in copies[:5]:
+    for copy in copies[:2]:
         copy.wait()
     dinv = 1.0 / jnp.sqrt(degree_ref[...].astype(F32))
     dinv_ref[...] = dinv
@@ -89,6 +89,8 @@
         scaled_ref[j] = (x_ref[:, lanes(j)] * dinv[:, lanes(j)]).astype(BF16)
     rows, picks, places = payload_rows(k)
     ahead_ref[...] = jnp.zeros_like(ahead_ref)
+    for copy in copies[2:5]:
+        copy.wait()
     for c in range(CROSS):
         ahead_ref[rows[c]] = blocks_ref[c]
         ahead_ref[picks[c]] = scaled_ref[col_ref[c]]
@@ -109,18 +111,45 @@
     return spans[:CROSS], spans[CROSS : 2 * CROSS], spans[2 * CROSS :]
 
 
+def diagonal(z_ref, place_ref, slots):
+    first, second = z_ref[place_ref[slots[0]]], z_ref[place_ref[slots[1]]]
+    zero = jnp.zeros_like(first)
+    return jnp.concatenate(
+        [jnp.concatenate([first, zero], axis=1), jnp.concatenate([zero, second], axis=1)], axis=0
+    )
+
+
+def across(blocks_ref, slots):
+    return jnp.concatenate([blocks_ref[c] for c in slots], axis=1)
+
+
+def down(blocks_ref, slots):
+    return jnp.concatenate([blocks_ref[c] for c in slots], axis=0)
+
+
 def near_kernel(z_ref, blocks_ref, col_ref, tgt_ref, count_ref, out_ref, acc):
     rb, k, _ = out_ref.shape
     acc[...] = jnp.zeros_like(acc)
     count = count_ref[0]
-    for c in range(CROSS, blocks_ref.shape[0]):
+    slots = range(CROSS, blocks_ref.shape[0])
+
+    def add(c, forward, backward):
         live = c < count
-        column, target = col_ref[c], tgt_ref[c]
-        weights = blocks_ref[c]
-        forward = fold(times_t(z_ref[column], weights), k)
-        backward = fold(times(z_ref[target], weights), k)
-        acc[jnp.where(live, target, rb)] += forward
-        acc[jnp.where(live, column, rb)] += backward
+        acc[jnp.where(live, tgt_ref[c], rb)] += forward
+        acc[jnp.where(live, col_ref[c], rb)] += backward
+
+    if z_ref.shape[1] == k:
+        for c in slots[::2]:
+            pair = (c, c + 1)
+            forward = times_t(diagonal(z_ref, col_ref, pair), across(blocks_ref, pair))
+            backward = times(diagonal(z_ref, tgt_ref, pair), down(blocks_ref, pair))
+            add(c, forward[:k], backward[:k])
+            add(c + 1, forward[k:], backward[k:])
+    else:
+        for c in slots:
+            weights = blocks_ref[c]
+            forward = fold(times_t(z_ref[col_ref[c]], weights), k)
+            add(c, forward, fold(times(z_ref[tgt_ref[c]], weights), k))
     for j in range(rb):
         out_ref[j] = acc[j]
 
@@ -129,10 +158,10 @@
     return jnp.concatenate([ref[j] for j in range(ref.shape[0])], axis=1)
 
 
-def crossed_block(part_ref, partner_ref, j, k):
+def crossed_blocks(part_ref, partner_ref, at, k):
     nodes = partner_ref.shape[1]
-    ids = lax.broadcasted_iota(jnp.int32, (nodes, BLOCK), 0)
-    onehot = jnp.where(ids == partner_ref[:, lanes(j)], 1.0, 0.0).astype(BF16)
+    ids = lax.broadcasted_iota(jnp.int32, (nodes, WIDE), 0)
+    onehot = jnp.where(ids == partner_ref[:, at : at + WIDE], 1.0, 0.0).astype(BF16)
     return fold(times(side_by_side(part_ref), onehot), k)
 
 
@@ -154,12 +183,15 @@
     z_ref,
     *rest,
 ):
-    sends, (tot,) = rest[:-1], rest[-1:]
+    *sends, tot = rest
     k = v_ref.shape[0]
     rb = v_ref.shape[1] // BLOCK
     even = even_group()
-    for j in range(rb):
-        tot[j] = near_ref[j] + crossed_block(part_ref, partner_ref, j, k)
+    for at in range(0, rb * BLOCK, WIDE):
+        crossed = crossed_blocks(part_ref, partner_ref, at, k)
+        for i in range(WIDE // BLOCK):
+            j = at // BLOCK + i
+            tot[j] = near_ref[j] + crossed[:, lanes(i)]
     rows, picks, spots = payload_rows(k)
     places = []
     for c in range(CROSS):
@@ -182,6 +214,8 @@
         y = v_ref[:, lanes(j)] + dinv * tot[j]
         y_ref[:, lanes(j)] = y
         z_ref[j] = split(y * dinv)
+        if not first:
+            sends[1][j] = z_ref[j, :k]
     for c in range(CROSS):
         wanted = jnp.zeros(z_ref.shape[1:], F32)
         for j in range(rb):
@@ -192,7 +226,7 @@
             sends[0][:, lanes(c)] = jnp.where(even, ahead, back)
             sends[1][:, lanes(c)] = jnp.where(even, back, ahead)
         else:
-            sends[0][:, lanes(c)] = back
+            sends[0][:, lanes(c)] = back[:k]
 
 
 def form_kernel(
@@ -205,7 +239,8 @@
     tgt_ref,
     count_ref,
     right_ref,
-    out_ref,
+    sums_ref,
+    parts_ref,
     acc,
 ):
     rb = z_ref.shape[0]
@@ -215,25 +250,36 @@
     for c in range(blocks_ref.shape[0]):
         forward = fold(times_t(z_ref[col_ref[c]], blocks_ref[c]), k)
         if c < CROSS:
-            right_ref[:, lanes(rb + c)] = forward
+            right_ref[:, lanes(rb + c)] = split(forward)
         else:
             acc[jnp.where(c < count, tgt_ref[c], rb)] += forward
     mine = side_by_side(z_ref)
+    for at in range(0, nodes, WIDE):
+        ids = lax.broadcasted_iota(jnp.int32, (WIDE, nodes), 0) + at
+        onehot = jnp.where(ids == partner_ref[...], 0.5, 0.0).astype(BF16)
+        right_ref[:, at : at + WIDE] = times_t(mine, onehot).astype(BF16)
     for j in range(rb):
-        ids = lax.broadcasted_iota(jnp.int32, (BLOCK, nodes), 0) + j * BLOCK
-        onehot = jnp.where(ids == partner_ref[...], 0.5, 0.0).astype(BF16)
-        right_ref[:, lanes(j)] = fold(times_t(mine, onehot), k)
-    y = y_ref[...]
-    z = y * dinv_ref[...]
-    near = jnp.concatenate([acc[j] for j in range(rb)], axis=1)
-    out_ref[:, :k] = times_t(y, y, FULL)
-    out_ref[:, k:] = times_t(near, z, FULL)
+        parts_ref[:, lanes(j)] = split(y_ref[:, lanes(j)])
+    near = [split(acc[j] * dinv_ref[:, lanes(j)]) for j in range(rb)]
+    parts = parts_ref[...]
+    left = jnp.concatenate([parts, jnp.concatenate(near, axis=1)], axis=0)
+    both = halves_added(times_t(left, parts))
+    sums_ref[:, :k] = both[:k]
+    sums_ref[:, k:] = both[k:]
+
+
+def halves_added(product):
+    k = product.shape[1] // 2
+    wide = product[:, :k] + product[:, k:]
+    pairs = range(0, product.shape[0], 2 * k)
+    return jnp.concatenate([wide[at : at + k] + wide[at + k : at + 2 * k] for at in pairs], axis=0)
 
 
 def pair_kernel(right_ref, sums_ref, next_ref, part_ref, out_ref):
-    k = right_ref.shape[0]
-    theirs = jnp.concatenate([side_by_side(part_ref), next_ref[...]], axis=1).astype(F32)
-    form = times_t(theirs[:k] + theirs[k:], right_ref[...], FULL)
+    k = sums_ref.shape[0]
+    theirs = jnp.concatenate([side_by_side(part_ref), next_ref[...]], axis=1)
+    product = times_t(theirs, right_ref[...])
+    form = product[:, :k] + product[:, k:]
     both = sums_ref[...] + jnp.concatenate([jnp.zeros((k, k), F32), form], axis=1)
     rows = out_ref.shape[1]
     for g in range(out_ref.shape[0]):
@@ -281,17 +327,18 @@
     return jnp.concatenate([tile[:, k:] for tile in tiles], axis=0)
 
 
-def solve_kernel(nodes, both_ref, y_ref, sub_ref, ray_ref):
-    k = y_ref.shape[0]
+def solve_kernel(nodes, both_ref, parts_ref, sub_ref, ray_ref):
+    k = sub_ref.shape[0]
     pieces, _, _ = both_ref.shape
     both = jnp.concatenate([both_ref[g] for g in range(pieces)], axis=0) * (1.0 / nodes)
     gram = both[:, :k]
     form = both[:, k:]
     projected = gram + form + form.T
     inverse = inverse_factor(gram)
-    sub_ref[...] = jnp.dot(inverse, y_ref[...], precision=FULL, preferred_element_type=F32)
-    half = jnp.dot(inverse, projected, precision=FULL, preferred_element_type=F32)
-    ray_ref[...] = times_t(half, inverse, FULL)
+    left = split(inverse)
+    sub_ref[...] = fold(times(jnp.concatenate([left, left], axis=1), parts_ref[...]), k)
+    half = fold(times(jnp.concatenate([left, left], axis=1), split(projected)), k)
+    ray_ref[...] = halves_added(times_t(split(half), left))
 
 
 def call(kernel, ins, outs, scratch, *args, out_specs=None):
@@ -365,7 +412,10 @@
 
     def finish(first, near_sum, v, from_inner, from_outer, part):
         outs = [((k, nodes), F32), ((rb, 2 * k, BLOCK), BF16)]
-        outs += [((2 * k, CROSS * BLOCK), BF16)] * (2 if first else 1)
+        if first:
+            outs += [((2 * k, CROSS * BLOCK), BF16)] * 2
+        else:
+            outs += [((k, CROSS * BLOCK), BF16), ((rb, k, BLOCK), BF16)]
         return call(
             functools.partial(finish_kernel, first),
             [VMEM] * 10 + [SMEM, SMEM],
@@ -395,14 +445,14 @@
     from_outer = moved(to_outer, outer)
     from_inner = moved(to_inner, inner)
     part = swapped(z)
-    images, z, back = finish(False, near(z), first_image, from_inner, from_outer, part)
+    images, z, back, high = finish(False, near(z), first_image, from_inner, from_outer, part)
 
     from_next = moved(back, lambda i: i - 1)
-    part = swapped(z)
-    right, sums = call(
+    part = swapped(high)
+    right, sums, parts = call(
         form_kernel,
         [VMEM] * 5 + [SMEM] * 3,
-        [((k, nodes + CROSS * BLOCK), F32), ((k, 2 * k), F32)],
+        [((2 * k, nodes + CROSS * BLOCK), BF16), ((k, 2 * k), F32), ((2 * k, nodes), BF16)],
         [pltpu.VMEM((rb + 1, k, BLOCK), F32)],
         images,
         z,
@@ -441,7 +491,7 @@
         [((k, nodes), F32), ((k, k), F32)],
         [],
         both,
-        images,
+        parts,
     )
 
 

time: 99.8 us -> 98.7 us (0.989)
  transfers between devices with their start and end apart: 8 -> 8, of which waited for: 1 -> 1; matrix products, arithmetic and copies ran while one was open for 0% -> 0% of each run, Pallas kernels for 6% -> 5%
where the time goes in v4:
time: 98.7 us; the launch traced here: 98.2 us
  blocking collectives  44.3 us (45%)
  starting transfers between devices  38.9 us (39%)
  Pallas kernels  12.7 us (13%)
  between operations  1.47 us (1%)
    ppermute x5, starting transfers between devices, moved(): lax.ppermute(array, 'blk', [(i, target(i) % blk) for i in range(blk)])  30.2 us
    all_to_all x1, blocking collectives, shards(): piece = lax.all_to_all(piece, 'blk', 0, 0, axis_index_groups=columns).sum(0)  20.1 us
    pallas_call x8, Pallas kernels, call(): pl.pallas_call(kernel, out_shape=[jax.ShapeDtypeStruct(shape, dtype) for...  12.7 us
    all_to_all x1, blocking collectives, shards(): both = lax.all_to_all(piece, BOTH, 0, 0, axis_index_groups=planes)  12.1 us
    all_to_all x1, blocking collectives, shards(): piece = lax.all_to_all(mine, BOTH, 0, 0, axis_index_groups=planes).sum(0)  12 us
    ppermute x3, starting transfers between devices, swapped(): return lax.ppermute(array, 'scale', [(i, i ^ 1) for i in range(scale)])  8.61 us
  transfers between devices with their start and end apart: 8, of which 1 were waited for; matrix products, arithmetic and copies ran while one was open for 0% of the time, Pallas kernels for 5%

profile of v4, /device:TPU:1, one launch (start us, length us, event | category | flops | bytes accessed | tf_op | source)
XLA Modules:
  0.0 98.2 jit_solution(2439134475004585052)
XLA Ops:
  0.6 2.0 %shard_map.86 = (f32[1,1024]{1,0:T(1,128)S(1)}, bf16[8,64,128]{2,1,0:T(8,128)(2,1)S(1)}, bf16[512,128]{1,0:T(8,128)(2,1)S(1)}, bf16[512,128]{1,0:T(8,128)(2,1)S(...) custom-call(f32[64,1024]{1,0:T(8,128)} %v_ref.1, s32[1,1024]{1,0:T(1,128)} %bitcast.5, ...), custom_call_target="tpu_custom_call" | custom-call | tf_op jit(solution)/shard_map/pallas_call | solution.py:345
  2.6 3.9 %collective-permute-start = (bf16[512,128]{1,0:T(8,128)(2,1)S(1)}, bf16[512,128]{1,0:T(8,128)(2,1)S(1)}, u32[]{:S(2)}, u32[]{:S(2)}) collective-permute-start(bf16[512,128]{1,0:T(8,128)(2,1)S(1)} %get-tuple-element.25), channel_id=1, source_target_pairs={{0,8},{8,0},{16,24},{24,16},{32,40},{40,32},{48,56},{56,48},{64,72... | collective-permute-start | bytes 393224 | tf_op jit(solution)/shard_map/ppermute | solution.py:364
  6.6 12.7 %collective-permute-start.1 = (bf16[512,128]{1,0:T(8,128)(2,1)S(1)}, bf16[512,128]{1,0:T(8,128)(2,1)S(1)}, u32[]{:S(2)}, u32[]{:S(2)}) collective-permute-start(bf16[512,128]{1,0:T(8,128)(2,1)S(1)} %get-tuple-element.26), channel_id=1, source_target_pairs={{0,504},{8,16},{16,8},{24,32},{32,24},{40,48},{48,40},{56,64},{64,... | collective-permute-start | bytes 393224 | tf_op jit(solution)/shard_map/ppermute | solution.py:364
  19.2 3.1 %collective-permute-start.2 = (bf16[8,64,128]{2,1,0:T(8,128)(2,1)S(1)}, bf16[8,64,128]{2,1,0:T(8,128)(2,1)S(1)}, u32[]{:S(2)}, u32[]{:S(2)}) collective-permute-start(bf16[8,64,128]{2,1,0:T(8,128)(2,1)S(1)} %get-tuple-element.20.z_ref), channel_id=1, source_target_pairs={{0,1},{1,0},{2,3},{3,2},{4,5},{5,4},{6,7},{7,6},{8,9},{9,8},{10,11... | collective-permute-start | bytes 393224 | tf_op jit(solution)/shard_map/ppermute | solution.py:367
  23.0 0.0 copy-start
  23.0 0.0 copy-start.1
  23.1 1.2 %shard_map.87.near_ref = f32[8,64,128]{2,1,0:T(8,128)S(1)} custom-call(bf16[8,64,128]{2,1,0:T(8,128)(2,1)S(1)} %get-tuple-element.20.z_ref, bf16[32,128,128]{2,1,0:T(8,128)(2,1)S(1)} %get-tuple-element.21.blocks_ref, s32[32]{0:T(128)S(1)} %get-tuple-element.22.col_ref, s32[32]{0:T(128)S(1)} %get-tuple-element.23.tgt_ref, s32[1]{0:T(128)S(6)} %copy.11.count_ref), custom_call_target="tpu_custom_call" | custom-call | tf_op jit(solution)/shard_map/pallas_call | solution.py:345
  24.3 0.0 collective-permute-done.inner_ref.pay_inner_ref
  24.3 0.0 collective-permute-done.1.outer_ref.pay_outer_ref
  24.3 0.0 collective-permute-done.2.part_ref
  24.3 0.0 copy-done
  24.4 0.0 copy-done.1
  24.4 1.3 %shard_map.88 = (f32[64,1024]{1,0:T(8,128)S(1)}, bf16[8,128,128]{2,1,0:T(8,128)(2,1)S(1)}, bf16[128,256]{1,0:T(8,128)(2,1)S(1)}, bf16[128,256]{1,0:T(8,128)(2,1)S(1)}) custom-call(f32[8,64,128]{2,1,0:T(8,128)S(1)} %shard_map.87.near_ref, f32[64,1024]{1,0:T(8,128)S(1)} %copy-done, f32[1,1024]{1,0:T(1,128)S(1)} %get-tuple-element.24.dinv_ref, ...), custom_call_target="tpu_custom_call" | custom-call | tf_op jit(solution)/shard_map/pallas_call | solution.py:345
  25.6 1.9 %collective-permute-start.5 = (bf16[8,128,128]{2,1,0:T(8,128)(2,1)S(1)}, bf16[8,128,128]{2,1,0:T(8,128)(2,1)S(1)}, u32[]{:S(2)}, u32[]{:S(2)}) collective-permute-start(bf16[8,128,128]{2,1,0:T(8,128)(2,1)S(1)} %get-tuple-element.27.z_ref), channel_id=1, source_target_pairs={{0,1},{1,0},{2,3},{3,2},{4,5},{5,4},{6,7},{7,6},{8,9},{9,8},{10,11... | collective-permute-start | bytes 786440 | tf_op jit(solution)/shard_map/ppermute | solution.py:367
  27.6 1.9 %collective-permute-start.3 = (bf16[128,256]{1,0:T(8,128)(2,1)S(1)}, bf16[128,256]{1,0:T(8,128)(2,1)S(1)}, u32[]{:S(2)}, u32[]{:S(2)}) collective-permute-start(bf16[128,256]{1,0:T(8,128)(2,1)S(1)} %get-tuple-element.29), channel_id=1, source_target_pairs={{0,8},{8,0},{16,24},{24,16},{32,40},{40,32},{48,56},{56,48},{64,72... | collective-permute-start | bytes 196616 | tf_op jit(solution)/shard_map/ppermute | solution.py:364
  29.5 6.0 %collective-permute-start.4 = (bf16[128,256]{1,0:T(8,128)(2,1)S(1)}, bf16[128,256]{1,0:T(8,128)(2,1)S(1)}, u32[]{:S(2)}, u32[]{:S(2)}) collective-permute-start(bf16[128,256]{1,0:T(8,128)(2,1)S(1)} %get-tuple-element.30), channel_id=1, source_target_pairs={{0,504},{8,16},{16,8},{24,32},{32,24},{40,48},{48,40},{56,64},{64,... | collective-permute-start | bytes 196616 | tf_op jit(solution)/shard_map/ppermute | solution.py:364
  35.5 1.5 %shard_map.89.near_ref = f32[8,64,128]{2,1,0:T(8,128)S(1)} custom-call(bf16[8,128,128]{2,1,0:T(8,128)(2,1)S(1)} %get-tuple-element.27.z_ref, bf16[32,128,128]{2,1,0:T(8,128)(2,1)S(1)} %get-tuple-element.21.blocks_ref, s32[32]{0:T(128)S(1)} %get-tuple-element.22.col_ref, s32[32]{0:T(128)S(1)} %get-tuple-element.23.tgt_ref, s32[1]{0:T(128)S(6)} %copy.11.count_ref), custom_call_target="tpu_custom_call" | custom-call | tf_op jit(solution)/shard_map/pallas_call | solution.py:345
  37.0 0.0 collective-permute-done.3.inner_ref
  37.1 0.8 collective-permute-done.4.outer_ref
  37.8 0.0 collective-permute-done.5.part_ref
  37.8 1.2 %shard_map.90 = (f32[64,1024]{1,0:T(8,128)S(1)}, bf16[8,128,128]{2,1,0:T(8,128)(2,1)S(1)}, bf16[64,256]{1,0:T(8,128)(2,1)S(1)}, bf16[8,64,128]{2,1,0:T(8,128)(2,1)S(1)}) custom-call(f32[8,64,128]{2,1,0:T(8,128)S(1)} %shard_map.89.near_ref, f32[64,1024]{1,0:T(8,128)S(1)} %get-tuple-element.28.v_ref, f32[1,1024]{1,0:T(1,128)S(1)} %get-tuple-element.24.dinv_ref, ...), custom_call_target="tpu_custom_call" | custom-call | tf_op jit(solution)/shard_map/pallas_call | solution.py:345
  39.0 3.5 %collective-permute-start.7 = (bf16[8,64,128]{2,1,0:T(8,128)(2,1)S(1)}, bf16[8,64,128]{2,1,0:T(8,128)(2,1)S(1)}, u32[]{:S(2)}, u32[]{:S(2)}) collective-permute-start(bf16[8,64,128]{2,1,0:T(8,128)(2,1)S(1)} %get-tuple-element.36), channel_id=1, source_target_pairs={{0,1},{1,0},{2,3},{3,2},{4,5},{5,4},{6,7},{7,6},{8,9},{9,8},{10,11... | collective-permute-start | bytes 393224 | tf_op jit(solution)/shard_map/ppermute | solution.py:367
  42.6 5.7 %collective-permute-start.6 = (bf16[64,256]{1,0:T(8,128)(2,1)S(1)}, bf16[64,256]{1,0:T(8,128)(2,1)S(1)}, u32[]{:S(2)}, u32[]{:S(2)}) collective-permute-start(bf16[64,256]{1,0:T(8,128)(2,1)S(1)} %get-tuple-element.35), channel_id=1, source_target_pairs={{0,504},{8,0},{16,8},{24,16},{32,24},{40,32},{48,40},{56,48},{64,5... | collective-permute-start | bytes 98312 | tf_op jit(solution)/shard_map/ppermute | solution.py:364
  48.3 2.3 %shard_map.91 = (bf16[128,1280]{1,0:T(8,128)(2,1)S(1)}, f32[64,128]{1,0:T(8,128)S(1)}, bf16[128,1024]{1,0:T(8,128)(2,1)S(1)}) custom-call(f32[64,1024]{1,0:T(8,128)S(1)} %get-tuple-element.31.y_ref, bf16[8,128,128]{2,1,0:T(8,128)(2,1)S(1)} %get-tuple-element.32.z_ref, f32[1,1024]{1,0:T(1,128)S(1)} %get-tuple-element.24.dinv_ref, ...), custom_call_target="tpu_custom_call" | custom-call | tf_op jit(solution)/shard_map/pallas_call | solution.py:345
  50.7 0.0 collective-permute-done.6.next_ref
  50.7 0.0 collective-permute-done.7.part_ref
  50.7 0.4 shard_map.92
  51.1 12.0 %all_to_all.15 = f32[32,2,128]{2,1,0:T(2,128)S(1)} all-to-all(f32[32,2,128]{2,1,0:T(2,128)S(1)} %shard_map.92), channel_id=1, replica_groups={{0,1,2,3,4,5,6,7,8,9,10,11,12,13,14,15,16,17,18,19,20,21,22,23,24,25,26..., dimensions={0} | all-to-all | bytes 65536 | tf_op jit(solution)/shard_map/all_to_all | solution.py:482
  63.1 20.1 %all_to_all.16 = f32[16,2,128]{2,1,0:T(2,128)S(1)} all-to-all(f32[16,2,128]{2,1,0:T(2,128)S(1)} %broadcast_in_dim.4), channel_id=1, replica_groups={{0,32,64,96,128,160,192,224,256,288,320,352,384,416,448,480},{8,40,72,1..., dimensions={0} | all-to-all | bytes 32768 | tf_op jit(solution)/shard_map/all_to_all | solution.py:484
  83.3 12.1 %all_to_all.17.both_ref = f32[32,2,128]{2,1,0:T(2,128)S(1)} all-to-all(f32[32,2,128]{2,1,0:T(2,128)S(1)} %broadcast_in_dim.5), channel_id=1, replica_groups={{0,1,2,3,4,5,6,7,8,9,10,11,12,13,14,15,16,17,18,19,20,21,22,23,24,25,26..., dimensions={0} | all-to-all | bytes 65536 | tf_op jit(solution)/shard_map/all_to_all | solution.py:486
  95.4 2.8 %shard_map.93 = (f32[64,1024]{1,0:T(8,128)}, f32[64,64]{1,0:T(8,128)}) custom-call(f32[32,2,128]{2,1,0:T(2,128)S(1)} %all_to_all.17.both_ref, bf16[128,1024]{1,0:T(8,128)(2,1)S(1)} %get-tuple-element.37.parts_ref), custom_call_target="tpu_custom_call" | custom-call | tf_op jit(solution)/shard_map/pallas_call | solution.py:345
  (4 shorter events, 0.1 us)
Async XLA Ops:
  2.6 21.7 %collective-permute-start = (bf16[512,128]{1,0:T(8,128)(2,1)S(1)}, bf16[512,128]{1,0:T(8,128)(2,1)S(1)}, u32[]{:S(2)}, u32[]{:S(2)}) collective-permute-start(bf16[512,128]{1,0:T(8,128)(2,1)S(1)} %get-tuple-element.25), channel_id=1, source_target_pairs={{0,8},{8,0},{16,24},{24,16},{32,40},{40,32},{48,56},{56,48},{64,72... | collective-permute-start | bytes 393224 | tf_op jit(solution)/shard_map/ppermute | solution.py:364
  6.6 17.8 %collective-permute-start.1 = (bf16[512,128]{1,0:T(8,128)(2,1)S(1)}, bf16[512,128]{1,0:T(8,128)(2,1)S(1)}, u32[]{:S(2)}, u32[]{:S(2)}) collective-permute-start(bf16[512,128]{1,0:T(8,128)(2,1)S(1)} %get-tuple-element.26), channel_id=1, source_target_pairs={{0,504},{8,16},{16,8},{24,32},{32,24},{40,48},{48,40},{56,64},{64,... | collective-permute-start | bytes 393224 | tf_op jit(solution)/shard_map/ppermute | solution.py:364
  19.2 5.1 %collective-permute-start.2 = (bf16[8,64,128]{2,1,0:T(8,128)(2,1)S(1)}, bf16[8,64,128]{2,1,0:T(8,128)(2,1)S(1)}, u32[]{:S(2)}, u32[]{:S(2)}) collective-permute-start(bf16[8,64,128]{2,1,0:T(8,128)(2,1)S(1)} %get-tuple-element.20.z_ref), channel_id=1, source_target_pairs={{0,1},{1,0},{2,3},{3,2},{4,5},{5,4},{6,7},{7,6},{8,9},{9,8},{10,11... | collective-permute-start | bytes 393224 | tf_op jit(solution)/shard_map/ppermute | solution.py:367
  23.0 1.3 %copy-start = (f32[64,1024]{1,0:T(8,128)S(1)}, f32[64,1024]{1,0:T(8,128)}, u32[]{:S(2)}) copy-start(f32[64,1024]{1,0:T(8,128)} %v_ref.1) | copy-start | bytes 786436
  23.0 1.3 %copy-start.1 = (s32[1024]{0:T(1024)S(1)}, s32[1024]{0:T(1024)}, u32[]{:S(2)}) copy-start(s32[1024]{0:T(1024)} %param.12) | copy-start | bytes 12292
  25.6 12.2 %collective-permute-start.5 = (bf16[8,128,128]{2,1,0:T(8,128)(2,1)S(1)}, bf16[8,128,128]{2,1,0:T(8,128)(2,1)S(1)}, u32[]{:S(2)}, u32[]{:S(2)}) collective-permute-start(bf16[8,128,128]{2,1,0:T(8,128)(2,1)S(1)} %get-tuple-element.27.z_ref), channel_id=1, source_target_pairs={{0,1},{1,0},{2,3},{3,2},{4,5},{5,4},{6,7},{7,6},{8,9},{9,8},{10,11... | collective-permute-start | bytes 786440 | tf_op jit(solution)/shard_map/ppermute | solution.py:367
  27.6 9.5 %collective-permute-start.3 = (bf16[128,256]{1,0:T(8,128)(2,1)S(1)}, bf16[128,256]{1,0:T(8,128)(2,1)S(1)}, u32[]{:S(2)}, u32[]{:S(2)}) collective-permute-start(bf16[128,256]{1,0:T(8,128)(2,1)S(1)} %get-tuple-element.29), channel_id=1, source_target_pairs={{0,8},{8,0},{16,24},{24,16},{32,40},{40,32},{48,56},{56,48},{64,72... | collective-permute-start | bytes 196616 | tf_op jit(solution)/shard_map/ppermute | solution.py:364
  29.5 8.3 %collective-permute-start.4 = (bf16[128,256]{1,0:T(8,128)(2,1)S(1)}, bf16[128,256]{1,0:T(8,128)(2,1)S(1)}, u32[]{:S(2)}, u32[]{:S(2)}) collective-permute-start(bf16[128,256]{1,0:T(8,128)(2,1)S(1)} %get-tuple-element.30), channel_id=1, source_target_pairs={{0,504},{8,16},{16,8},{24,32},{32,24},{40,48},{48,40},{56,64},{64,... | collective-permute-start | bytes 196616 | tf_op jit(solution)/shard_map/ppermute | solution.py:364
  39.0 11.6 %collective-permute-start.7 = (bf16[8,64,128]{2,1,0:T(8,128)(2,1)S(1)}, bf16[8,64,128]{2,1,0:T(8,128)(2,1)S(1)}, u32[]{:S(2)}, u32[]{:S(2)}) collective-permute-start(bf16[8,64,128]{2,1,0:T(8,128)(2,1)S(1)} %get-tuple-element.36), channel_id=1, source_target_pairs={{0,1},{1,0},{2,3},{3,2},{4,5},{5,4},{6,7},{7,6},{8,9},{9,8},{10,11... | collective-permute-start | bytes 393224 | tf_op jit(solution)/shard_map/ppermute | solution.py:367
  42.6 8.1 %collective-permute-start.6 = (bf16[64,256]{1,0:T(8,128)(2,1)S(1)}, bf16[64,256]{1,0:T(8,128)(2,1)S(1)}, u32[]{:S(2)}, u32[]{:S(2)}) collective-permute-start(bf16[64,256]{1,0:T(8,128)(2,1)S(1)} %get-tuple-element.35), channel_id=1, source_target_pairs={{0,504},{8,0},{16,8},{24,16},{32,24},{40,32},{48,40},{56,48},{64,5... | collective-permute-start | bytes 98312 | tf_op jit(solution)/shard_map/ppermute | solution.py:364

commit v5 on v4

--- a/solution.py
+++ b/solution.py
@@ -60,7 +60,6 @@
     scaled_ref,
     inner_ref,
     outer_ref,
-    blocks_ref,
     col_ref,
     tgt_ref,
     x_ref,
@@ -69,15 +68,14 @@
     sems,
 ):
     rb, k, _ = scaled_ref.shape
-    far, near = pl.ds(0, CROSS), pl.ds(CROSS, blocks_ref.shape[0] - CROSS)
+    rows, picks, places = payload_rows(k)
     moves = [
         (degree_hbm, degree_ref),
         (x_hbm, x_ref),
         (col_hbm, col_ref),
         (tgt_hbm, tgt_ref),
-        (blocks_hbm.at[far], blocks_ref.at[far]),
-        (blocks_hbm.at[near], blocks_ref.at[near]),
     ]
+    moves += [(blocks_hbm.at[c], ahead_ref.at[rows[c]]) for c in range(CROSS)]
     copies = [pltpu.make_async_copy(src, dst, sems.at[i]) for i, (src, dst) in enumerate(moves)]
     for copy in copies:
         copy.start()
@@ -87,12 +85,11 @@
     dinv_ref[...] = dinv
     for j in range(rb):
         scaled_ref[j] = (x_ref[:, lanes(j)] * dinv[:, lanes(j)]).astype(BF16)
-    rows, picks, places = payload_rows(k)
-    ahead_ref[...] = jnp.zeros_like(ahead_ref)
-    for copy in copies[2:5]:
+    tail = places[-1].stop
+    ahead_ref[tail:] = jnp.zeros_like(ahead_ref[tail:])
+    for copy in copies[2:]:
         copy.wait()
     for c in range(CROSS):
-        ahead_ref[rows[c]] = blocks_ref[c]
         ahead_ref[picks[c]] = scaled_ref[col_ref[c]]
         place = jnp.full((TILE_ROWS, BLOCK), tgt_ref[c] - rb, jnp.int32)
         ahead_ref[places[c]] = place.astype(F32).astype(BF16)
@@ -101,7 +98,6 @@
     back = jnp.concatenate([scaled_ref[j] for j in range(rb)], axis=0)
     inner_ref[...] = jnp.where(even, ahead, back)
     outer_ref[...] = jnp.where(even, back, ahead)
-    copies[5].wait()
 
 
 def payload_rows(k):
@@ -221,12 +217,13 @@
         for j in range(rb):
             wanted = jnp.where(places[c] == j, z_ref[j].astype(F32), wanted)
         back = wanted.astype(BF16)
+        ahead = z_ref[col_ref[c]]
         if first:
-            ahead = z_ref[col_ref[c]]
             sends[0][:, lanes(c)] = jnp.where(even, ahead, back)
             sends[1][:, lanes(c)] = jnp.where(even, back, ahead)
         else:
-            sends[0][:, lanes(c)] = back[:k]
+            sends[0][:, lanes(c)] = ahead[:k]
+            sends[2][:, lanes(c)] = back
 
 
 def form_kernel(
@@ -235,6 +232,9 @@
     dinv_ref,
     blocks_ref,
     partner_ref,
+    landing_ref,
+    pay_inner_ref,
+    pay_outer_ref,
     col_ref,
     tgt_ref,
     count_ref,
@@ -247,12 +247,13 @@
     k, nodes = y_ref.shape
     acc[...] = jnp.zeros_like(acc)
     count = count_ref[0]
-    for c in range(blocks_ref.shape[0]):
+    rows, _, _ = payload_rows(k)
+    for c in range(CROSS):
+        weights = jnp.where(even_group(), pay_outer_ref[rows[c]], pay_inner_ref[rows[c]])
+        right_ref[:, lanes(rb + c)] = split(fold(times(landing_ref[:, lanes(c)], weights), k))
+    for c in range(CROSS, blocks_ref.shape[0]):
         forward = fold(times_t(z_ref[col_ref[c]], blocks_ref[c]), k)
-        if c < CROSS:
-            right_ref[:, lanes(rb + c)] = split(forward)
-        else:
-            acc[jnp.where(c < count, tgt_ref[c], rb)] += forward
+        acc[jnp.where(c < count, tgt_ref[c], rb)] += forward
     mine = side_by_side(z_ref)
     for at in range(0, nodes, WIDE):
         ids = lax.broadcasted_iota(jnp.int32, (WIDE, nodes), 0) + at
@@ -275,9 +276,9 @@
     return jnp.concatenate([wide[at : at + k] + wide[at + k : at + 2 * k] for at in pairs], axis=0)
 
 
-def pair_kernel(right_ref, sums_ref, next_ref, part_ref, out_ref):
+def pair_kernel(right_ref, sums_ref, prev_ref, part_ref, out_ref):
     k = sums_ref.shape[0]
-    theirs = jnp.concatenate([side_by_side(part_ref), next_ref[...]], axis=1)
+    theirs = jnp.concatenate([side_by_side(part_ref), prev_ref[...]], axis=1)
     product = times_t(theirs, right_ref[...])
     form = product[:, :k] + product[:, k:]
     both = sums_ref[...] + jnp.concatenate([jnp.zeros((k, k), F32), form], axis=1)
@@ -341,13 +342,14 @@
     ray_ref[...] = halves_added(times_t(split(half), left))
 
 
-def call(kernel, ins, outs, scratch, *args, out_specs=None):
+def call(kernel, ins, outs, scratch, *args, out_specs=None, cost=None):
     return pl.pallas_call(
         kernel,
         out_shape=[jax.ShapeDtypeStruct(shape, dtype) for shape, dtype in outs],
         in_specs=ins,
         out_specs=[VMEM] * len(outs) if out_specs is None else out_specs,
         scratch_shapes=scratch,
+        cost_estimate=cost,
         compiler_params=pltpu.CompilerParams(vmem_limit_bytes=24 * 1024 * 1024),
     )(*args)
 
@@ -372,7 +374,7 @@
     def outer(i):
         return i - 1 + 2 * (i % 2)
 
-    dinv, scaled, to_inner, to_outer, blocks, column, target = call(
+    dinv, scaled, to_inner, to_outer, column, target = call(
         first_kernel,
         [pl.BlockSpec(memory_space=pltpu.HBM)] * 5,
         [
@@ -380,7 +382,6 @@
             ((rb, k, BLOCK), BF16),
             ((rb * k, BLOCK), BF16),
             ((rb * k, BLOCK), BF16),
-            (blocks.shape, BF16),
             (block_column.shape, jnp.int32),
             (block_target.shape, jnp.int32),
         ],
@@ -394,7 +395,8 @@
             pltpu.with_memory_space_constraint(array, pltpu.HBM)
             for array in (start_block, degree, blocks, block_column, block_target)
         ],
-        out_specs=[VMEM] * 5 + [SMEM] * 2,
+        out_specs=[VMEM] * 4 + [SMEM] * 2,
+        cost=pl.CostEstimate(flops=0, transcendentals=0, bytes_accessed=1 << 26),
     )
 
     def near(z):
@@ -416,6 +418,7 @@
             outs += [((2 * k, CROSS * BLOCK), BF16)] * 2
         else:
             outs += [((k, CROSS * BLOCK), BF16), ((rb, k, BLOCK), BF16)]
+            outs += [((2 * k, CROSS * BLOCK), BF16)]
         return call(
             functools.partial(finish_kernel, first),
             [VMEM] * 10 + [SMEM, SMEM],
@@ -445,13 +448,13 @@
     from_outer = moved(to_outer, outer)
     from_inner = moved(to_inner, inner)
     part = swapped(z)
-    images, z, back, high = finish(False, near(z), first_image, from_inner, from_outer, part)
-
-    from_next = moved(back, lambda i: i - 1)
+    images, z, ahead, high, landing = finish(False, near(z), first_image, from_inner, from_outer, part)
+
+    from_prev = moved(ahead, lambda i: i + 1)
     part = swapped(high)
     right, sums, parts = call(
         form_kernel,
-        [VMEM] * 5 + [SMEM] * 3,
+        [VMEM] * 8 + [SMEM] * 3,
         [((2 * k, nodes + CROSS * BLOCK), BF16), ((k, 2 * k), F32), ((2 * k, nodes), BF16)],
         [pltpu.VMEM((rb + 1, k, BLOCK), F32)],
         images,
@@ -459,6 +462,9 @@
         dinv,
         blocks,
         partner,
+        landing,
+        pay_inner,
+        pay_outer,
         column,
         target,
         block_count,
@@ -473,7 +479,7 @@
         [],
         right,
         sums,
-        from_next,
+        from_prev,
         part,
     )
 

time: 98.7 us -> 98.3 us (level)
  starting transfers between devices: 38.9 us -> 35 us
  waiting for transfers between devices: 0.81 us -> 4.51 us
    ppermute x5, starting transfers between devices: 30.2 us -> 26.4 us  [moved(): lax.ppermute(array, 'blk', [(i, target(i) % blk) for i in range(blk)])]
    ppermute x5, waiting for transfers between devices: 0.8 us -> 4.5 us  [moved(): lax.ppermute(array, 'blk', [(i, target(i) % blk) for i in range(blk)])]
  transfers between devices with their start and end apart: 8 -> 8, of which waited for: 1 -> 2; matrix products, arithmetic and copies ran while one was open for 0% -> 0% of each run, Pallas kernels for 5% -> 5%
where the time goes in v5:
time: 98.3 us; the launch traced here: 97.8 us
  blocking collectives  44.2 us (45%)
  starting transfers between devices  35 us (36%)
  Pallas kernels  12.5 us (13%)
  waiting for transfers between devices  4.51 us (5%)
  between operations  1.47 us (1%)
    ppermute x5, starting transfers between devices, moved(): lax.ppermute(array, 'blk', [(i, target(i) % blk) for i in range(blk)])  26.4 us
    all_to_all x1, blocking collectives, shards(): piece = lax.all_to_all(piece, 'blk', 0, 0, axis_index_groups=columns).sum(0)  19.2 us
    all_to_all x1, blocking collectives, shards(): piece = lax.all_to_all(mine, BOTH, 0, 0, axis_index_groups=planes).sum(0)  12.9 us
    pallas_call x8, Pallas kernels, call(): pl.pallas_call(kernel, out_shape=[jax.ShapeDtypeStruct(shape, dtype) for...  12.5 us
    all_to_all x1, blocking collectives, shards(): both = lax.all_to_all(piece, BOTH, 0, 0, axis_index_groups=planes)  12.1 us
    ppermute x3, starting transfers between devices, swapped(): return lax.ppermute(array, 'scale', [(i, i ^ 1) for i in range(scale)])  8.62 us
    ppermute x5, waiting for transfers between devices, moved(): lax.ppermute(array, 'blk', [(i, target(i) % blk) for i in range(blk)])  4.5 us
  transfers between devices with their start and end apart: 8, of which 2 were waited for; matrix products, arithmetic and copies ran while one was open for 0% of the time, Pallas kernels for 5%

profile of v5, /device:TPU:1, one launch (start us, length us, event | category | flops | bytes accessed | tf_op | source)
XLA Modules:
  0.0 97.8 jit_solution(11718231677385082777)
XLA Ops:
  0.6 0.0 copy-start
  0.6 1.8 %shard_map.86 = (f32[1,1024]{1,0:T(1,128)S(1)}, bf16[8,64,128]{2,1,0:T(8,128)(2,1)S(1)}, bf16[512,128]{1,0:T(8,128)(2,1)S(1)}, bf16[512,128]{1,0:T(8,128)(2,1)S(1)}, s32[32]{0:T(128)S(1)}, /*index=5*/s32[32]{0:T(128)S(1)}) custom-call(f32[64,1024]{1,0:T(8,128)} %v_ref.1, s32[1,1024]{1,0:T(1,128)} %bitcast.5, bf16[32,128,128]{2,1,0:T(8,128)(2,1)} %blocks_ref.9, ...), custom_call_target="tpu_custom_call" | custom-call | bytes 67108864 | tf_op jit(solution)/shard_map/pallas_call | solution.py:346
  2.4 3.9 %collective-permute-start = (bf16[512,128]{1,0:T(8,128)(2,1)S(1)}, bf16[512,128]{1,0:T(8,128)(2,1)S(1)}, u32[]{:S(2)}, u32[]{:S(2)}) collective-permute-start(bf16[512,128]{1,0:T(8,128)(2,1)S(1)} %get-tuple-element.24), channel_id=1, source_target_pairs={{0,8},{8,0},{16,24},{24,16},{32,40},{40,32},{48,56},{56,48},{64,72... | collective-permute-start | bytes 393224 | tf_op jit(solution)/shard_map/ppermute | solution.py:366
  6.4 12.7 %collective-permute-start.1 = (bf16[512,128]{1,0:T(8,128)(2,1)S(1)}, bf16[512,128]{1,0:T(8,128)(2,1)S(1)}, u32[]{:S(2)}, u32[]{:S(2)}) collective-permute-start(bf16[512,128]{1,0:T(8,128)(2,1)S(1)} %get-tuple-element.25), channel_id=1, source_target_pairs={{0,504},{8,16},{16,8},{24,32},{32,24},{40,48},{48,40},{56,64},{64,... | collective-permute-start | bytes 393224 | tf_op jit(solution)/shard_map/ppermute | solution.py:366
  19.0 3.1 %collective-permute-start.2 = (bf16[8,64,128]{2,1,0:T(8,128)(2,1)S(1)}, bf16[8,64,128]{2,1,0:T(8,128)(2,1)S(1)}, u32[]{:S(2)}, u32[]{:S(2)}) collective-permute-start(bf16[8,64,128]{2,1,0:T(8,128)(2,1)S(1)} %get-tuple-element.20.z_ref), channel_id=1, source_target_pairs={{0,1},{1,0},{2,3},{3,2},{4,5},{5,4},{6,7},{7,6},{8,9},{9,8},{10,11... | collective-permute-start | bytes 393224 | tf_op jit(solution)/shard_map/ppermute | solution.py:369
  22.8 0.0 copy-done
  22.8 0.0 copy-start.1
  22.8 0.0 copy-start.2
  22.9 1.2 %shard_map.87.near_ref = f32[8,64,128]{2,1,0:T(8,128)S(1)} custom-call(bf16[8,64,128]{2,1,0:T(8,128)(2,1)S(1)} %get-tuple-element.20.z_ref, bf16[32,128,128]{2,1,0:T(8,128)(2,1)S(1)} %copy-done, s32[32]{0:T(128)S(1)} %get-tuple-element.21.col_ref, s32[32]{0:T(128)S(1)} %get-tuple-element.22.tgt_ref, s32[1]{0:T(128)S(6)} %copy.11.count_ref), custom_call_target="tpu_custom_call" | custom-call | tf_op jit(solution)/shard_map/pallas_call | solution.py:346
  24.1 0.0 collective-permute-done.inner_ref.pay_inner_ref
  24.1 0.0 collective-permute-done.1.outer_ref.pay_outer_ref
  24.1 0.0 collective-permute-done.2.part_ref
  24.1 0.0 copy-done.1
  24.1 0.0 copy-done.2
  24.1 1.3 %shard_map.88 = (f32[64,1024]{1,0:T(8,128)S(1)}, bf16[8,128,128]{2,1,0:T(8,128)(2,1)S(1)}, bf16[128,256]{1,0:T(8,128)(2,1)S(1)}, bf16[128,256]{1,0:T(8,128)(2,1)S(1)}) custom-call(f32[8,64,128]{2,1,0:T(8,128)S(1)} %shard_map.87.near_ref, f32[64,1024]{1,0:T(8,128)S(1)} %copy-done.1, f32[1,1024]{1,0:T(1,128)S(1)} %get-tuple-element.23.dinv_ref, ...), custom_call_target="tpu_custom_call" | custom-call | tf_op jit(solution)/shard_map/pallas_call | solution.py:346
  25.4 1.9 %collective-permute-start.5 = (bf16[8,128,128]{2,1,0:T(8,128)(2,1)S(1)}, bf16[8,128,128]{2,1,0:T(8,128)(2,1)S(1)}, u32[]{:S(2)}, u32[]{:S(2)}) collective-permute-start(bf16[8,128,128]{2,1,0:T(8,128)(2,1)S(1)} %get-tuple-element.26.z_ref), channel_id=1, source_target_pairs={{0,1},{1,0},{2,3},{3,2},{4,5},{5,4},{6,7},{7,6},{8,9},{9,8},{10,11... | collective-permute-start | bytes 786440 | tf_op jit(solution)/shard_map/ppermute | solution.py:369
  27.3 1.9 %collective-permute-start.3 = (bf16[128,256]{1,0:T(8,128)(2,1)S(1)}, bf16[128,256]{1,0:T(8,128)(2,1)S(1)}, u32[]{:S(2)}, u32[]{:S(2)}) collective-permute-start(bf16[128,256]{1,0:T(8,128)(2,1)S(1)} %get-tuple-element.28), channel_id=1, source_target_pairs={{0,8},{8,0},{16,24},{24,16},{32,40},{40,32},{48,56},{56,48},{64,72... | collective-permute-start | bytes 196616 | tf_op jit(solution)/shard_map/ppermute | solution.py:366
  29.3 6.0 %collective-permute-start.4 = (bf16[128,256]{1,0:T(8,128)(2,1)S(1)}, bf16[128,256]{1,0:T(8,128)(2,1)S(1)}, u32[]{:S(2)}, u32[]{:S(2)}) collective-permute-start(bf16[128,256]{1,0:T(8,128)(2,1)S(1)} %get-tuple-element.29), channel_id=1, source_target_pairs={{0,504},{8,16},{16,8},{24,32},{32,24},{40,48},{48,40},{56,64},{64,... | collective-permute-start | bytes 196616 | tf_op jit(solution)/shard_map/ppermute | solution.py:366
  35.3 1.5 %shard_map.89.near_ref = f32[8,64,128]{2,1,0:T(8,128)S(1)} custom-call(bf16[8,128,128]{2,1,0:T(8,128)(2,1)S(1)} %get-tuple-element.26.z_ref, bf16[32,128,128]{2,1,0:T(8,128)(2,1)S(1)} %copy-done, s32[32]{0:T(128)S(1)} %get-tuple-element.21.col_ref, s32[32]{0:T(128)S(1)} %get-tuple-element.22.tgt_ref, s32[1]{0:T(128)S(6)} %copy.11.count_ref), custom_call_target="tpu_custom_call" | custom-call | tf_op jit(solution)/shard_map/pallas_call | solution.py:346
  36.8 0.0 collective-permute-done.3.inner_ref
  36.8 0.8 collective-permute-done.4.outer_ref
  37.6 0.0 collective-permute-done.5.part_ref
  37.6 1.2 %shard_map.90 = (f32[64,1024]{1,0:T(8,128)S(1)}, bf16[8,128,128]{2,1,0:T(8,128)(2,1)S(1)}, bf16[64,256]{1,0:T(8,128)(2,1)S(1)}, bf16[8,64,128]{2,1,0:T(8,128)(2,1)S(1)}, bf16[128,256]{1,0:T(8,128)(2,1)S(1)}) custom-call(f32[8,64,128]{2,1,0:T(8,128)S(1)} %shard_map.89.near_ref, f32[64,1024]{1,0:T(8,128)S(1)} %get-tuple-element.27.v_ref, ...), custom_call_target="tpu_custom_call" | custom-call | tf_op jit(solution)/shard_map/pallas_call | solution.py:346
  38.8 3.5 %collective-permute-start.7 = (bf16[8,64,128]{2,1,0:T(8,128)(2,1)S(1)}, bf16[8,64,128]{2,1,0:T(8,128)(2,1)S(1)}, u32[]{:S(2)}, u32[]{:S(2)}) collective-permute-start(bf16[8,64,128]{2,1,0:T(8,128)(2,1)S(1)} %get-tuple-element.36), channel_id=1, source_target_pairs={{0,1},{1,0},{2,3},{3,2},{4,5},{5,4},{6,7},{7,6},{8,9},{9,8},{10,11... | collective-permute-start | bytes 393224 | tf_op jit(solution)/shard_map/ppermute | solution.py:369
  42.4 1.9 %collective-permute-start.6 = (bf16[64,256]{1,0:T(8,128)(2,1)S(1)}, bf16[64,256]{1,0:T(8,128)(2,1)S(1)}, u32[]{:S(2)}, u32[]{:S(2)}) collective-permute-start(bf16[64,256]{1,0:T(8,128)(2,1)S(1)} %get-tuple-element.35), channel_id=1, source_target_pairs={{0,8},{8,16},{16,24},{24,32},{32,40},{40,48},{48,56},{56,64},{64,7... | collective-permute-start | bytes 98312 | tf_op jit(solution)/shard_map/ppermute | solution.py:366
  44.3 2.3 %shard_map.91 = (bf16[128,1280]{1,0:T(8,128)(2,1)S(1)}, f32[64,128]{1,0:T(8,128)S(1)}, bf16[128,1024]{1,0:T(8,128)(2,1)S(1)}) custom-call(f32[64,1024]{1,0:T(8,128)S(1)} %get-tuple-element.30.y_ref, bf16[8,128,128]{2,1,0:T(8,128)(2,1)S(1)} %get-tuple-element.31.z_ref, f32[1,1024]{1,0:T(1,128)S(1)} %get-tuple-element.23.dinv_ref, ...), custom_call_target="tpu_custom_call" | custom-call | tf_op jit(solution)/shard_map/pallas_call | solution.py:346
  46.6 3.7 %collective-permute-done.6.prev_ref = bf16[64,256]{1,0:T(8,128)(2,1)S(1)} collective-permute-done((bf16[64,256]{1,0:T(8,128)(2,1)S(1)}, bf16[64,256]{1,0:T(8,128)(2,1)S(1)}, u32[]{:S(2)}, u32[]{:S(2)}) %collective-permute-start.6) | collective-permute-done | bytes 32800 | tf_op jit(solution)/shard_map/ppermute | solution.py:366
  50.4 0.0 collective-permute-done.7.part_ref
  50.4 0.4 shard_map.92
  50.7 12.9 %all_to_all.15 = f32[32,2,128]{2,1,0:T(2,128)S(1)} all-to-all(f32[32,2,128]{2,1,0:T(2,128)S(1)} %shard_map.92), channel_id=1, replica_groups={{0,1,2,3,4,5,6,7,8,9,10,11,12,13,14,15,16,17,18,19,20,21,22,23,24,25,26..., dimensions={0} | all-to-all | bytes 65536 | tf_op jit(solution)/shard_map/all_to_all | solution.py:488
  63.7 19.2 %all_to_all.16 = f32[16,2,128]{2,1,0:T(2,128)S(1)} all-to-all(f32[16,2,128]{2,1,0:T(2,128)S(1)} %broadcast_in_dim.4), channel_id=1, replica_groups={{0,32,64,96,128,160,192,224,256,288,320,352,384,416,448,480},{8,40,72,1..., dimensions={0} | all-to-all | bytes 32768 | tf_op jit(solution)/shard_map/all_to_all | solution.py:490
  82.9 12.1 %all_to_all.17.both_ref = f32[32,2,128]{2,1,0:T(2,128)S(1)} all-to-all(f32[32,2,128]{2,1,0:T(2,128)S(1)} %broadcast_in_dim.5), channel_id=1, replica_groups={{0,1,2,3,4,5,6,7,8,9,10,11,12,13,14,15,16,17,18,19,20,21,22,23,24,25,26..., dimensions={0} | all-to-all | bytes 65536 | tf_op jit(solution)/shard_map/all_to_all | solution.py:492
  95.1 2.8 %shard_map.93 = (f32[64,1024]{1,0:T(8,128)}, f32[64,64]{1,0:T(8,128)}) custom-call(f32[32,2,128]{2,1,0:T(2,128)S(1)} %all_to_all.17.both_ref, bf16[128,1024]{1,0:T(8,128)(2,1)S(1)} %get-tuple-element.37.parts_ref), custom_call_target="tpu_custom_call" | custom-call | tf_op jit(solution)/shard_map/pallas_call | solution.py:346
  (4 shorter events, 0.1 us)
Async XLA Ops:
  0.6 22.2 %copy-start = (bf16[32,128,128]{2,1,0:T(8,128)(2,1)S(1)}, bf16[32,128,128]{2,1,0:T(8,128)(2,1)}, u32[]{:S(2)}) copy-start(bf16[32,128,128]{2,1,0:T(8,128)(2,1)} %blocks_ref.9) | copy-start | bytes 3145732
  2.4 21.7 %collective-permute-start = (bf16[512,128]{1,0:T(8,128)(2,1)S(1)}, bf16[512,128]{1,0:T(8,128)(2,1)S(1)}, u32[]{:S(2)}, u32[]{:S(2)}) collective-permute-start(bf16[512,128]{1,0:T(8,128)(2,1)S(1)} %get-tuple-element.24), channel_id=1, source_target_pairs={{0,8},{8,0},{16,24},{24,16},{32,40},{40,32},{48,56},{56,48},{64,72... | collective-permute-start | bytes 393224 | tf_op jit(solution)/shard_map/ppermute | solution.py:366
  6.4 17.7 %collective-permute-start.1 = (bf16[512,128]{1,0:T(8,128)(2,1)S(1)}, bf16[512,128]{1,0:T(8,128)(2,1)S(1)}, u32[]{:S(2)}, u32[]{:S(2)}) collective-permute-start(bf16[512,128]{1,0:T(8,128)(2,1)S(1)} %get-tuple-element.25), channel_id=1, source_target_pairs={{0,504},{8,16},{16,8},{24,32},{32,24},{40,48},{48,40},{56,64},{64,... | collective-permute-start | bytes 393224 | tf_op jit(solution)/shard_map/ppermute | solution.py:366
  19.0 5.1 %collective-permute-start.2 = (bf16[8,64,128]{2,1,0:T(8,128)(2,1)S(1)}, bf16[8,64,128]{2,1,0:T(8,128)(2,1)S(1)}, u32[]{:S(2)}, u32[]{:S(2)}) collective-permute-start(bf16[8,64,128]{2,1,0:T(8,128)(2,1)S(1)} %get-tuple-element.20.z_ref), channel_id=1, source_target_pairs={{0,1},{1,0},{2,3},{3,2},{4,5},{5,4},{6,7},{7,6},{8,9},{9,8},{10,11... | collective-permute-start | bytes 393224 | tf_op jit(solution)/shard_map/ppermute | solution.py:369
  22.8 1.3 %copy-start.1 = (f32[64,1024]{1,0:T(8,128)S(1)}, f32[64,1024]{1,0:T(8,128)}, u32[]{:S(2)}) copy-start(f32[64,1024]{1,0:T(8,128)} %v_ref.1) | copy-start | bytes 786436
  22.8 1.3 %copy-start.2 = (s32[1024]{0:T(1024)S(1)}, s32[1024]{0:T(1024)}, u32[]{:S(2)}) copy-start(s32[1024]{0:T(1024)} %param.12) | copy-start | bytes 12292
  25.4 12.2 %collective-permute-start.5 = (bf16[8,128,128]{2,1,0:T(8,128)(2,1)S(1)}, bf16[8,128,128]{2,1,0:T(8,128)(2,1)S(1)}, u32[]{:S(2)}, u32[]{:S(2)}) collective-permute-start(bf16[8,128,128]{2,1,0:T(8,128)(2,1)S(1)} %get-tuple-element.26.z_ref), channel_id=1, source_target_pairs={{0,1},{1,0},{2,3},{3,2},{4,5},{5,4},{6,7},{7,6},{8,9},{9,8},{10,11... | collective-permute-start | bytes 786440 | tf_op jit(solution)/shard_map/ppermute | solution.py:369
  27.3 9.5 %collective-permute-start.3 = (bf16[128,256]{1,0:T(8,128)(2,1)S(1)}, bf16[128,256]{1,0:T(8,128)(2,1)S(1)}, u32[]{:S(2)}, u32[]{:S(2)}) collective-permute-start(bf16[128,256]{1,0:T(8,128)(2,1)S(1)} %get-tuple-element.28), channel_id=1, source_target_pairs={{0,8},{8,0},{16,24},{24,16},{32,40},{40,32},{48,56},{56,48},{64,72... | collective-permute-start | bytes 196616 | tf_op jit(solution)/shard_map/ppermute | solution.py:366
  29.3 8.3 %collective-permute-start.4 = (bf16[128,256]{1,0:T(8,128)(2,1)S(1)}, bf16[128,256]{1,0:T(8,128)(2,1)S(1)}, u32[]{:S(2)}, u32[]{:S(2)}) collective-permute-start(bf16[128,256]{1,0:T(8,128)(2,1)S(1)} %get-tuple-element.29), channel_id=1, source_target_pairs={{0,504},{8,16},{16,8},{24,32},{32,24},{40,48},{48,40},{56,64},{64,... | collective-permute-start | bytes 196616 | tf_op jit(solution)/shard_map/ppermute | solution.py:366
  38.8 11.5 %collective-permute-start.7 = (bf16[8,64,128]{2,1,0:T(8,128)(2,1)S(1)}, bf16[8,64,128]{2,1,0:T(8,128)(2,1)S(1)}, u32[]{:S(2)}, u32[]{:S(2)}) collective-permute-start(bf16[8,64,128]{2,1,0:T(8,128)(2,1)S(1)} %get-tuple-element.36), channel_id=1, source_target_pairs={{0,1},{1,0},{2,3},{3,2},{4,5},{5,4},{6,7},{7,6},{8,9},{9,8},{10,11... | collective-permute-start | bytes 393224 | tf_op jit(solution)/shard_map/ppermute | solution.py:369
  42.4 8.0 %collective-permute-start.6 = (bf16[64,256]{1,0:T(8,128)(2,1)S(1)}, bf16[64,256]{1,0:T(8,128)(2,1)S(1)}, u32[]{:S(2)}, u32[]{:S(2)}) collective-permute-start(bf16[64,256]{1,0:T(8,128)(2,1)S(1)} %get-tuple-element.35), channel_id=1, source_target_pairs={{0,8},{8,16},{16,24},{24,32},{32,40},{40,48},{48,56},{56,64},{64,7... | collective-permute-start | bytes 98312 | tf_op jit(solution)/shard_map/ppermute | solution.py:366

commit v6 on v5

--- a/solution.py
+++ b/solution.py
@@ -161,6 +161,15 @@
     return fold(times(side_by_side(part_ref), onehot), k)
 
 
+def cross_kernel(near_ref, part_ref, partner_ref, out_ref):
+    rb, k, _ = near_ref.shape
+    for at in range(0, rb * BLOCK, WIDE):
+        crossed = crossed_blocks(part_ref, partner_ref, at, k)
+        for i in range(WIDE // BLOCK):
+            j = at // BLOCK + i
+            out_ref[j] = near_ref[j] + crossed[:, lanes(i)]
+
+
 def finish_kernel(
     first,
     near_ref,
@@ -170,8 +179,6 @@
     outer_ref,
     pay_inner_ref,
     pay_outer_ref,
-    part_ref,
-    partner_ref,
     blocks_ref,
     col_ref,
     tgt_ref,
@@ -183,16 +190,13 @@
     k = v_ref.shape[0]
     rb = v_ref.shape[1] // BLOCK
     even = even_group()
-    for at in range(0, rb * BLOCK, WIDE):
-        crossed = crossed_blocks(part_ref, partner_ref, at, k)
-        for i in range(WIDE // BLOCK):
-            j = at // BLOCK + i
-            tot[j] = near_ref[j] + crossed[:, lanes(i)]
+    for j in range(rb):
+        tot[j] = near_ref[j]
     rows, picks, spots = payload_rows(k)
     places = []
     for c in range(CROSS):
         sent = jnp.where(even, pay_outer_ref[spots[c]], pay_inner_ref[spots[c]])
-        places.append(sent.astype(F32)[0:1])
+        places.append(jnp.max(sent.astype(F32)).astype(jnp.int32))
         if first:
             at = pl.ds(pl.multiple_of((tgt_ref[c] - rb) * k, k), k)
             theirs = jnp.where(even, inner_ref[at], outer_ref[at])
@@ -203,8 +207,7 @@
         weights = jnp.where(even, pay_outer_ref[rows[c]], pay_inner_ref[rows[c]])
         tot[col_ref[c]] += fold(times(theirs, blocks_ref[c]), k)
         landed = fold(times_t(behind, weights), k)
-        for j in range(rb):
-            tot[j] += jnp.where(places[c] == j, landed, 0.0)
+        tot[places[c]] += landed
     for j in range(rb):
         dinv = dinv_ref[:, lanes(j)]
         y = v_ref[:, lanes(j)] + dinv * tot[j]
@@ -213,14 +216,11 @@
         if not first:
             sends[1][j] = z_ref[j, :k]
     for c in range(CROSS):
-        wanted = jnp.zeros(z_ref.shape[1:], F32)
-        for j in range(rb):
-            wanted = jnp.where(places[c] == j, z_ref[j].astype(F32), wanted)
-        back = wanted.astype(BF16)
+        back = z_ref[places[c]]
         ahead = z_ref[col_ref[c]]
         if first:
-            sends[0][:, lanes(c)] = jnp.where(even, ahead, back)
-            sends[1][:, lanes(c)] = jnp.where(even, back, ahead)
+            sends[0][:, lanes(c)] = jnp.where(even, ahead[:k], back[:k])
+            sends[1][:, lanes(c)] = jnp.where(even, back[:k], ahead[:k])
         else:
             sends[0][:, lanes(c)] = ahead[:k]
             sends[2][:, lanes(c)] = back
@@ -413,15 +413,24 @@
         )[0]
 
     def finish(first, near_sum, v, from_inner, from_outer, part):
+        (near_sum,) = call(
+            cross_kernel,
+            [VMEM] * 3,
+            [((rb, k, BLOCK), F32)],
+            [],
+            near_sum,
+            part,
+            partner,
+        )
         outs = [((k, nodes), F32), ((rb, 2 * k, BLOCK), BF16)]
         if first:
-            outs += [((2 * k, CROSS * BLOCK), BF16)] * 2
+            outs += [((k, CROSS * BLOCK), BF16)] * 2
         else:
             outs += [((k, CROSS * BLOCK), BF16), ((rb, k, BLOCK), BF16)]
             outs += [((2 * k, CROSS * BLOCK), BF16)]
         return call(
             functools.partial(finish_kernel, first),
-            [VMEM] * 10 + [SMEM, SMEM],
+            [VMEM] * 8 + [SMEM, SMEM],
             outs,
             [pltpu.VMEM((rb, k, BLOCK), F32)],
             near_sum,
@@ -431,8 +440,6 @@
             from_outer,
             pay_inner,
             pay_outer,
-            part,
-            partner,
             blocks,
             column,
             target,

time: 98.3 us -> 99.5 us (1.012)
    ppermute x5, starting transfers between devices: 26.4 us -> 20.9 us  [moved(): lax.ppermute(array, 'blk', [(i, target(i) % blk) for i in range(blk)])]
    ppermute x3, starting transfers between devices: 8.62 us -> 13.9 us  [swapped(): return lax.ppermute(array, 'scale', [(i, i ^ 1) for i in range(scale)])]
    pallas_call x8 -> x10, Pallas kernels: 12.5 us -> 12.7 us  [call(): pl.pallas_call(kernel, out_shape=[jax.ShapeDtypeStruct(shape, dtype) for...]
  transfers between devices with their start and end apart: 8 -> 8, of which waited for: 2 -> 2; matrix products, arithmetic and copies ran while one was open for 0% -> 0% of each run, Pallas kernels for 5% -> 6%
where the time goes in v6:
time: 99.5 us; the launch traced here: 99 us
  blocking collectives  45.1 us (45%)
  starting transfers between devices  34.8 us (35%)
  Pallas kernels  12.7 us (13%)
  waiting for transfers between devices  4.82 us (5%)
  between operations  1.49 us (1%)
    ppermute x5, starting transfers between devices, moved(): lax.ppermute(array, 'blk', [(i, target(i) % blk) for i in range(blk)])  20.9 us
    all_to_all x1, blocking collectives, shards(): piece = lax.all_to_all(piece, 'blk', 0, 0, axis_index_groups=columns).sum(0)  20 us
    ppermute x3, starting transfers between devices, swapped(): return lax.ppermute(array, 'scale', [(i, i ^ 1) for i in range(scale)])  13.9 us
    all_to_all x1, blocking collectives, shards(): piece = lax.all_to_all(mine, BOTH, 0, 0, axis_index_groups=planes).sum(0)  13 us
    pallas_call x10, Pallas kernels, call(): pl.pallas_call(kernel, out_shape=[jax.ShapeDtypeStruct(shape, dtype) for...  12.7 us
    all_to_all x1, blocking collectives, shards(): both = lax.all_to_all(piece, BOTH, 0, 0, axis_index_groups=planes)  12.1 us
    ppermute x5, waiting for transfers between devices, moved(): lax.ppermute(array, 'blk', [(i, target(i) % blk) for i in range(blk)])  4.81 us
  transfers between devices with their start and end apart: 8, of which 2 were waited for; matrix products, arithmetic and copies ran while one was open for 0% of the time, Pallas kernels for 6%

profile of v6, /device:TPU:1, one launch (start us, length us, event | category | flops | bytes accessed | tf_op | source)
XLA Modules:
  0.0 99.0 jit_solution(14295608564059075888)
XLA Ops:
  0.6 0.0 copy-start
  0.6 1.8 %shard_map.86 = (f32[1,1024]{1,0:T(1,128)S(1)}, bf16[8,64,128]{2,1,0:T(8,128)(2,1)S(1)}, bf16[512,128]{1,0:T(8,128)(2,1)S(1)}, bf16[512,128]{1,0:T(8,128)(2,1)S(1)}, s32[32]{0:T(128)S(1)}, /*index=5*/s32[32]{0:T(128)S(1)}) custom-call(f32[64,1024]{1,0:T(8,128)} %v_ref.1, s32[1,1024]{1,0:T(1,128)} %bitcast.5, bf16[32,128,128]{2,1,0:T(8,128)(2,1)} %blocks_ref.9, ...), custom_call_target="tpu_custom_call" | custom-call | bytes 67108864 | tf_op jit(solution)/shard_map/pallas_call | solution.py:346
  2.4 8.7 %collective-permute-start = (bf16[8,64,128]{2,1,0:T(8,128)(2,1)S(1)}, bf16[8,64,128]{2,1,0:T(8,128)(2,1)S(1)}, u32[]{:S(2)}, u32[]{:S(2)}) collective-permute-start(bf16[8,64,128]{2,1,0:T(8,128)(2,1)S(1)} %get-tuple-element.20.z_ref), channel_id=1, source_target_pairs={{0,1},{1,0},{2,3},{3,2},{4,5},{5,4},{6,7},{7,6},{8,9},{9,8},{10,11... | collective-permute-start | bytes 393224 | tf_op jit(solution)/shard_map/ppermute | solution.py:369
  11.2 1.9 %collective-permute-start.1 = (bf16[512,128]{1,0:T(8,128)(2,1)S(1)}, bf16[512,128]{1,0:T(8,128)(2,1)S(1)}, u32[]{:S(2)}, u32[]{:S(2)}) collective-permute-start(bf16[512,128]{1,0:T(8,128)(2,1)S(1)} %get-tuple-element.24), channel_id=1, source_target_pairs={{0,8},{8,0},{16,24},{24,16},{32,40},{40,32},{48,56},{56,48},{64,72... | collective-permute-start | bytes 393224 | tf_op jit(solution)/shard_map/ppermute | solution.py:366
  13.1 8.5 %collective-permute-start.2 = (bf16[512,128]{1,0:T(8,128)(2,1)S(1)}, bf16[512,128]{1,0:T(8,128)(2,1)S(1)}, u32[]{:S(2)}, u32[]{:S(2)}) collective-permute-start(bf16[512,128]{1,0:T(8,128)(2,1)S(1)} %get-tuple-element.25), channel_id=1, source_target_pairs={{0,504},{8,16},{16,8},{24,32},{32,24},{40,48},{48,40},{56,64},{64,... | collective-permute-start | bytes 393224 | tf_op jit(solution)/shard_map/ppermute | solution.py:366
  22.3 0.0 copy-done
  22.3 0.0 copy-start.2
  22.3 1.2 %shard_map.87.near_ref = f32[8,64,128]{2,1,0:T(8,128)S(1)} custom-call(bf16[8,64,128]{2,1,0:T(8,128)(2,1)S(1)} %get-tuple-element.20.z_ref, bf16[32,128,128]{2,1,0:T(8,128)(2,1)S(1)} %copy-done, s32[32]{0:T(128)S(1)} %get-tuple-element.21.col_ref, s32[32]{0:T(128)S(1)} %get-tuple-element.22.tgt_ref, s32[1]{0:T(128)S(6)} %copy.11.count_ref), custom_call_target="tpu_custom_call" | custom-call | tf_op jit(solution)/shard_map/pallas_call | solution.py:346
  23.5 0.0 collective-permute-done.part_ref
  23.5 0.0 copy-done.2
  23.5 0.0 copy-start.1
  23.6 0.5 shard_map.88.near_ref
  24.1 0.0 collective-permute-done.1.inner_ref.pay_inner_ref
  24.1 1.1 %collective-permute-done.2.outer_ref.pay_outer_ref = bf16[512,128]{1,0:T(8,128)(2,1)S(1)} collective-permute-done((bf16[512,128]{1,0:T(8,128)(2,1)S(1)}, bf16[512,128]{1,0:T(8,128)(2,1)S(1)}, u32[]{:S(2)}, u32[]{:S(2)}) %collective-permute-start.2) | collective-permute-done | bytes 131104 | tf_op jit(solution)/shard_map/ppermute | solution.py:366
  25.2 0.0 copy-done.1
  25.2 0.8 shard_map.89
  26.0 2.8 %collective-permute-start.3 = (bf16[8,128,128]{2,1,0:T(8,128)(2,1)S(1)}, bf16[8,128,128]{2,1,0:T(8,128)(2,1)S(1)}, u32[]{:S(2)}, u32[]{:S(2)}) collective-permute-start(bf16[8,128,128]{2,1,0:T(8,128)(2,1)S(1)} %get-tuple-element.26.z_ref), channel_id=1, source_target_pairs={{0,1},{1,0},{2,3},{3,2},{4,5},{5,4},{6,7},{7,6},{8,9},{9,8},{10,11... | collective-permute-start | bytes 786440 | tf_op jit(solution)/shard_map/ppermute | solution.py:369
  28.8 1.9 %collective-permute-start.4 = (bf16[64,256]{1,0:T(8,128)(2,1)S(1)}, bf16[64,256]{1,0:T(8,128)(2,1)S(1)}, u32[]{:S(2)}, u32[]{:S(2)}) collective-permute-start(bf16[64,256]{1,0:T(8,128)(2,1)S(1)} %get-tuple-element.28), channel_id=1, source_target_pairs={{0,8},{8,0},{16,24},{24,16},{32,40},{40,32},{48,56},{56,48},{64,72... | collective-permute-start | bytes 98312 | tf_op jit(solution)/shard_map/ppermute | solution.py:366
  30.7 6.7 %collective-permute-start.5 = (bf16[64,256]{1,0:T(8,128)(2,1)S(1)}, bf16[64,256]{1,0:T(8,128)(2,1)S(1)}, u32[]{:S(2)}, u32[]{:S(2)}) collective-permute-start(bf16[64,256]{1,0:T(8,128)(2,1)S(1)} %get-tuple-element.29), channel_id=1, source_target_pairs={{0,504},{8,16},{16,8},{24,32},{32,24},{40,48},{48,40},{56,64},{64,... | collective-permute-start | bytes 98312 | tf_op jit(solution)/shard_map/ppermute | solution.py:366
  37.4 1.5 %shard_map.90.near_ref = f32[8,64,128]{2,1,0:T(8,128)S(1)} custom-call(bf16[8,128,128]{2,1,0:T(8,128)(2,1)S(1)} %get-tuple-element.26.z_ref, bf16[32,128,128]{2,1,0:T(8,128)(2,1)S(1)} %copy-done, s32[32]{0:T(128)S(1)} %get-tuple-element.21.col_ref, s32[32]{0:T(128)S(1)} %get-tuple-element.22.tgt_ref, s32[1]{0:T(128)S(6)} %copy.11.count_ref), custom_call_target="tpu_custom_call" | custom-call | tf_op jit(solution)/shard_map/pallas_call | solution.py:346
  38.9 0.0 collective-permute-done.3.part_ref
  39.0 0.5 shard_map.91.near_ref
  39.4 0.0 collective-permute-done.4.inner_ref
  39.4 0.0 collective-permute-done.5.outer_ref
  39.4 0.8 shard_map.92
  40.3 2.3 %collective-permute-start.7 = (bf16[8,64,128]{2,1,0:T(8,128)(2,1)S(1)}, bf16[8,64,128]{2,1,0:T(8,128)(2,1)S(1)}, u32[]{:S(2)}, u32[]{:S(2)}) collective-permute-start(bf16[8,64,128]{2,1,0:T(8,128)(2,1)S(1)} %get-tuple-element.36), channel_id=1, source_target_pairs={{0,1},{1,0},{2,3},{3,2},{4,5},{5,4},{6,7},{7,6},{8,9},{9,8},{10,11... | collective-permute-start | bytes 393224 | tf_op jit(solution)/shard_map/ppermute | solution.py:369
  42.6 1.9 %collective-permute-start.6 = (bf16[64,256]{1,0:T(8,128)(2,1)S(1)}, bf16[64,256]{1,0:T(8,128)(2,1)S(1)}, u32[]{:S(2)}, u32[]{:S(2)}) collective-permute-start(bf16[64,256]{1,0:T(8,128)(2,1)S(1)} %get-tuple-element.35), channel_id=1, source_target_pairs={{0,8},{8,16},{16,24},{24,32},{32,40},{40,48},{48,56},{56,64},{64,7... | collective-permute-start | bytes 98312 | tf_op jit(solution)/shard_map/ppermute | solution.py:366
  44.5 2.4 %shard_map.93 = (bf16[128,1280]{1,0:T(8,128)(2,1)S(1)}, f32[64,128]{1,0:T(8,128)S(1)}, bf16[128,1024]{1,0:T(8,128)(2,1)S(1)}) custom-call(f32[64,1024]{1,0:T(8,128)S(1)} %get-tuple-element.30.y_ref, bf16[8,128,128]{2,1,0:T(8,128)(2,1)S(1)} %get-tuple-element.31.z_ref, f32[1,1024]{1,0:T(1,128)S(1)} %get-tuple-element.23.dinv_ref, ...), custom_call_target="tpu_custom_call" | custom-call | tf_op jit(solution)/shard_map/pallas_call | solution.py:346
  46.9 3.7 %collective-permute-done.6.prev_ref = bf16[64,256]{1,0:T(8,128)(2,1)S(1)} collective-permute-done((bf16[64,256]{1,0:T(8,128)(2,1)S(1)}, bf16[64,256]{1,0:T(8,128)(2,1)S(1)}, u32[]{:S(2)}, u32[]{:S(2)}) %collective-permute-start.6) | collective-permute-done | bytes 32800 | tf_op jit(solution)/shard_map/ppermute | solution.py:366
  50.6 0.0 collective-permute-done.7.part_ref
  50.6 0.4 shard_map.94
  51.0 13.0 %all_to_all.15 = f32[32,2,128]{2,1,0:T(2,128)S(1)} all-to-all(f32[32,2,128]{2,1,0:T(2,128)S(1)} %shard_map.94), channel_id=1, replica_groups={{0,1,2,3,4,5,6,7,8,9,10,11,12,13,14,15,16,17,18,19,20,21,22,23,24,25,26..., dimensions={0} | all-to-all | bytes 65536 | tf_op jit(solution)/shard_map/all_to_all | solution.py:495
  64.0 20.0 %all_to_all.16 = f32[16,2,128]{2,1,0:T(2,128)S(1)} all-to-all(f32[16,2,128]{2,1,0:T(2,128)S(1)} %broadcast_in_dim.4), channel_id=1, replica_groups={{0,32,64,96,128,160,192,224,256,288,320,352,384,416,448,480},{8,40,72,1..., dimensions={0} | all-to-all | bytes 32768 | tf_op jit(solution)/shard_map/all_to_all | solution.py:497
  84.1 12.1 %all_to_all.17.both_ref = f32[32,2,128]{2,1,0:T(2,128)S(1)} all-to-all(f32[32,2,128]{2,1,0:T(2,128)S(1)} %broadcast_in_dim.5), channel_id=1, replica_groups={{0,1,2,3,4,5,6,7,8,9,10,11,12,13,14,15,16,17,18,19,20,21,22,23,24,25,26..., dimensions={0} | all-to-all | bytes 65536 | tf_op jit(solution)/shard_map/all_to_all | solution.py:499
  96.2 2.8 %shard_map.95 = (f32[64,1024]{1,0:T(8,128)}, f32[64,64]{1,0:T(8,128)}) custom-call(f32[32,2,128]{2,1,0:T(2,128)S(1)} %all_to_all.17.both_ref, bf16[128,1024]{1,0:T(8,128)(2,1)S(1)} %get-tuple-element.37.parts_ref), custom_call_target="tpu_custom_call" | custom-call | tf_op jit(solution)/shard_map/pallas_call | solution.py:346
  (4 shorter events, 0.1 us)
Async XLA Ops:
  0.6 21.6 %copy-start = (bf16[32,128,128]{2,1,0:T(8,128)(2,1)S(1)}, bf16[32,128,128]{2,1,0:T(8,128)(2,1)}, u32[]{:S(2)}) copy-start(bf16[32,128,128]{2,1,0:T(8,128)(2,1)} %blocks_ref.9) | copy-start | bytes 3145732
  2.4 21.1 %collective-permute-start = (bf16[8,64,128]{2,1,0:T(8,128)(2,1)S(1)}, bf16[8,64,128]{2,1,0:T(8,128)(2,1)S(1)}, u32[]{:S(2)}, u32[]{:S(2)}) collective-permute-start(bf16[8,64,128]{2,1,0:T(8,128)(2,1)S(1)} %get-tuple-element.20.z_ref), channel_id=1, source_target_pairs={{0,1},{1,0},{2,3},{3,2},{4,5},{5,4},{6,7},{7,6},{8,9},{9,8},{10,11... | collective-permute-start | bytes 393224 | tf_op jit(solution)/shard_map/ppermute | solution.py:369
  11.2 12.9 %collective-permute-start.1 = (bf16[512,128]{1,0:T(8,128)(2,1)S(1)}, bf16[512,128]{1,0:T(8,128)(2,1)S(1)}, u32[]{:S(2)}, u32[]{:S(2)}) collective-permute-start(bf16[512,128]{1,0:T(8,128)(2,1)S(1)} %get-tuple-element.24), channel_id=1, source_target_pairs={{0,8},{8,0},{16,24},{24,16},{32,40},{40,32},{48,56},{56,48},{64,72... | collective-permute-start | bytes 393224 | tf_op jit(solution)/shard_map/ppermute | solution.py:366
  13.1 12.1 %collective-permute-start.2 = (bf16[512,128]{1,0:T(8,128)(2,1)S(1)}, bf16[512,128]{1,0:T(8,128)(2,1)S(1)}, u32[]{:S(2)}, u32[]{:S(2)}) collective-permute-start(bf16[512,128]{1,0:T(8,128)(2,1)S(1)} %get-tuple-element.25), channel_id=1, source_target_pairs={{0,504},{8,16},{16,8},{24,32},{32,24},{40,48},{48,40},{56,64},{64,... | collective-permute-start | bytes 393224 | tf_op jit(solution)/shard_map/ppermute | solution.py:366
  22.3 1.3 %copy-start.2 = (s32[1024]{0:T(1024)S(1)}, s32[1024]{0:T(1024)}, u32[]{:S(2)}) copy-start(s32[1024]{0:T(1024)} %param.12) | copy-start | bytes 12292
  23.5 1.6 %copy-start.1 = (f32[64,1024]{1,0:T(8,128)S(1)}, f32[64,1024]{1,0:T(8,128)}, u32[]{:S(2)}) copy-start(f32[64,1024]{1,0:T(8,128)} %v_ref.1) | copy-start | bytes 786436
  26.0 12.9 %collective-permute-start.3 = (bf16[8,128,128]{2,1,0:T(8,128)(2,1)S(1)}, bf16[8,128,128]{2,1,0:T(8,128)(2,1)S(1)}, u32[]{:S(2)}, u32[]{:S(2)}) collective-permute-start(bf16[8,128,128]{2,1,0:T(8,128)(2,1)S(1)} %get-tuple-element.26.z_ref), channel_id=1, source_target_pairs={{0,1},{1,0},{2,3},{3,2},{4,5},{5,4},{6,7},{7,6},{8,9},{9,8},{10,11... | collective-permute-start | bytes 786440 | tf_op jit(solution)/shard_map/ppermute | solution.py:369
  28.8 10.6 %collective-permute-start.4 = (bf16[64,256]{1,0:T(8,128)(2,1)S(1)}, bf16[64,256]{1,0:T(8,128)(2,1)S(1)}, u32[]{:S(2)}, u32[]{:S(2)}) collective-permute-start(bf16[64,256]{1,0:T(8,128)(2,1)S(1)} %get-tuple-element.28), channel_id=1, source_target_pairs={{0,8},{8,0},{16,24},{24,16},{32,40},{40,32},{48,56},{56,48},{64,72... | collective-permute-start | bytes 98312 | tf_op jit(solution)/shard_map/ppermute | solution.py:366
  30.7 8.7 %collective-permute-start.5 = (bf16[64,256]{1,0:T(8,128)(2,1)S(1)}, bf16[64,256]{1,0:T(8,128)(2,1)S(1)}, u32[]{:S(2)}, u32[]{:S(2)}) collective-permute-start(bf16[64,256]{1,0:T(8,128)(2,1)S(1)} %get-tuple-element.29), channel_id=1, source_target_pairs={{0,504},{8,16},{16,8},{24,32},{32,24},{40,48},{48,40},{56,64},{64,... | collective-permute-start | bytes 98312 | tf_op jit(solution)/shard_map/ppermute | solution.py:366
  40.3 10.3 %collective-permute-start.7 = (bf16[8,64,128]{2,1,0:T(8,128)(2,1)S(1)}, bf16[8,64,128]{2,1,0:T(8,128)(2,1)S(1)}, u32[]{:S(2)}, u32[]{:S(2)}) collective-permute-start(bf16[8,64,128]{2,1,0:T(8,128)(2,1)S(1)} %get-tuple-element.36), channel_id=1, source_target_pairs={{0,1},{1,0},{2,3},{3,2},{4,5},{5,4},{6,7},{7,6},{8,9},{9,8},{10,11... | collective-permute-start | bytes 393224 | tf_op jit(solution)/shard_map/ppermute | solution.py:369
  42.6 8.0 %collective-permute-start.6 = (bf16[64,256]{1,0:T(8,128)(2,1)S(1)}, bf16[64,256]{1,0:T(8,128)(2,1)S(1)}, u32[]{:S(2)}, u32[]{:S(2)}) collective-permute-start(bf16[64,256]{1,0:T(8,128)(2,1)S(1)} %get-tuple-element.35), channel_id=1, source_target_pairs={{0,8},{8,16},{16,24},{24,32},{32,40},{40,48},{48,56},{56,64},{64,7... | collective-permute-start | bytes 98312 | tf_op jit(solution)/shard_map/ppermute | solution.py:366

commit v7 on v6

--- a/solution.py
+++ b/solution.py
@@ -231,7 +231,6 @@
     z_ref,
     dinv_ref,
     blocks_ref,
-    partner_ref,
     landing_ref,
     pay_inner_ref,
     pay_outer_ref,
@@ -244,21 +243,16 @@
     acc,
 ):
     rb = z_ref.shape[0]
-    k, nodes = y_ref.shape
+    k = y_ref.shape[0]
     acc[...] = jnp.zeros_like(acc)
     count = count_ref[0]
     rows, _, _ = payload_rows(k)
     for c in range(CROSS):
         weights = jnp.where(even_group(), pay_outer_ref[rows[c]], pay_inner_ref[rows[c]])
-        right_ref[:, lanes(rb + c)] = split(fold(times(landing_ref[:, lanes(c)], weights), k))
+        right_ref[:, lanes(c)] = split(fold(times(landing_ref[:, lanes(c)], weights), k))
     for c in range(CROSS, blocks_ref.shape[0]):
         forward = fold(times_t(z_ref[col_ref[c]], blocks_ref[c]), k)
         acc[jnp.where(c < count, tgt_ref[c], rb)] += forward
-    mine = side_by_side(z_ref)
-    for at in range(0, nodes, WIDE):
-        ids = lax.broadcasted_iota(jnp.int32, (WIDE, nodes), 0) + at
-        onehot = jnp.where(ids == partner_ref[...], 0.5, 0.0).astype(BF16)
-        right_ref[:, at : at + WIDE] = times_t(mine, onehot).astype(BF16)
     for j in range(rb):
         parts_ref[:, lanes(j)] = split(y_ref[:, lanes(j)])
     near = [split(acc[j] * dinv_ref[:, lanes(j)]) for j in range(rb)]
@@ -276,10 +270,18 @@
     return jnp.concatenate([wide[at : at + k] + wide[at + k : at + 2 * k] for at in pairs], axis=0)
 
 
-def pair_kernel(right_ref, sums_ref, prev_ref, part_ref, out_ref):
+def pairs_kernel(sums_ref, z_ref, part_ref, partner_ref, out_ref):
     k = sums_ref.shape[0]
-    theirs = jnp.concatenate([side_by_side(part_ref), prev_ref[...]], axis=1)
-    product = times_t(theirs, right_ref[...])
+    ats = range(0, partner_ref.shape[1], WIDE)
+    crossed = [crossed_blocks(part_ref, partner_ref, at, k).astype(BF16) for at in ats]
+    product = times_t(jnp.concatenate(crossed, axis=1), side_by_side(z_ref))
+    out_ref[:, :k] = sums_ref[:, :k]
+    out_ref[:, k:] = sums_ref[:, k:] + 0.5 * (product[:, :k] + product[:, k:])
+
+
+def pair_kernel(right_ref, sums_ref, prev_ref, out_ref):
+    k = sums_ref.shape[0]
+    product = times_t(prev_ref[...], right_ref[...])
     form = product[:, :k] + product[:, k:]
     both = sums_ref[...] + jnp.concatenate([jnp.zeros((k, k), F32), form], axis=1)
     rows = out_ref.shape[1]
@@ -461,14 +463,13 @@
     part = swapped(high)
     right, sums, parts = call(
         form_kernel,
-        [VMEM] * 8 + [SMEM] * 3,
-        [((2 * k, nodes + CROSS * BLOCK), BF16), ((k, 2 * k), F32), ((2 * k, nodes), BF16)],
+        [VMEM] * 7 + [SMEM] * 3,
+        [((2 * k, CROSS * BLOCK), BF16), ((k, 2 * k), F32), ((2 * k, nodes), BF16)],
         [pltpu.VMEM((rb + 1, k, BLOCK), F32)],
         images,
         z,
         dinv,
         blocks,
-        partner,
         landing,
         pay_inner,
         pay_outer,
@@ -479,15 +480,15 @@
     plane = ALONG_X * scale
     depth = blk // ALONG_X
     rows = k // plane
+    (sums,) = call(pairs_kernel, [VMEM] * 4, [((k, 2 * k), F32)], [], sums, z, part, partner)
     (mine,) = call(
         pair_kernel,
-        [VMEM] * 4,
+        [VMEM] * 3,
         [((plane, rows, 2 * k), F32)],
         [],
         right,
         sums,
         from_prev,
-        part,
     )
 
     planes = [[z_at * plane + i for i in range(plane)] for z_at in range(depth)]

time: 99.5 us -> 99.4 us (level)
    pallas_call x10 -> x11, Pallas kernels: 12.7 us -> 12.8 us  [call(): pl.pallas_call(kernel, out_shape=[jax.ShapeDtypeStruct(shape, dtype) for...]
where the time goes in v7:
time: 99.4 us; the launch traced here: 98.9 us
  blocking collectives  45.1 us (45%)
  starting transfers between devices  34.8 us (35%)
  Pallas kernels  12.8 us (13%)
  waiting for transfers between devices  4.55 us (5%)
  between operations  1.5 us (2%)
    ppermute x5, starting transfers between devices, moved(): lax.ppermute(array, 'blk', [(i, target(i) % blk) for i in range(blk)])  20.9 us
    all_to_all x1, blocking collectives, shards(): piece = lax.all_to_all(piece, 'blk', 0, 0, axis_index_groups=columns).sum(0)  20 us
    ppermute x3, starting transfers between devices, swapped(): return lax.ppermute(array, 'scale', [(i, i ^ 1) for i in range(scale)])  13.9 us
    all_to_all x1, blocking collectives, shards(): piece = lax.all_to_all(mine, BOTH, 0, 0, axis_index_groups=planes).sum(0)  13 us
    pallas_call x11, Pallas kernels, call(): pl.pallas_call(kernel, out_shape=[jax.ShapeDtypeStruct(shape, dtype) for...  12.8 us
    all_to_all x1, blocking collectives, shards(): both = lax.all_to_all(piece, BOTH, 0, 0, axis_index_groups=planes)  12.1 us
    ppermute x5, waiting for transfers between devices, moved(): lax.ppermute(array, 'blk', [(i, target(i) % blk) for i in range(blk)])  4.54 us
  transfers between devices with their start and end apart: 8, of which 2 were waited for; matrix products, arithmetic and copies ran while one was open for 0% of the time, Pallas kernels for 6%

profile of v7, /device:TPU:1, one launch (start us, length us, event | category | flops | bytes accessed | tf_op | source)
XLA Modules:
  0.0 98.9 jit_solution(17410784993966120985)
XLA Ops:
  0.6 0.0 copy-start
  0.6 1.8 %shard_map.86 = (f32[1,1024]{1,0:T(1,128)S(1)}, bf16[8,64,128]{2,1,0:T(8,128)(2,1)S(1)}, bf16[512,128]{1,0:T(8,128)(2,1)S(1)}, bf16[512,128]{1,0:T(8,128)(2,1)S(1)}, s32[32]{0:T(128)S(1)}, /*index=5*/s32[32]{0:T(128)S(1)}) custom-call(f32[64,1024]{1,0:T(8,128)} %v_ref.1, s32[1,1024]{1,0:T(1,128)} %bitcast.5, bf16[32,128,128]{2,1,0:T(8,128)(2,1)} %blocks_ref.9, ...), custom_call_target="tpu_custom_call" | custom-call | bytes 67108864 | tf_op jit(solution)/shard_map/pallas_call | solution.py:348
  2.4 8.7 %collective-permute-start = (bf16[8,64,128]{2,1,0:T(8,128)(2,1)S(1)}, bf16[8,64,128]{2,1,0:T(8,128)(2,1)S(1)}, u32[]{:S(2)}, u32[]{:S(2)}) collective-permute-start(bf16[8,64,128]{2,1,0:T(8,128)(2,1)S(1)} %get-tuple-element.20.z_ref), channel_id=1, source_target_pairs={{0,1},{1,0},{2,3},{3,2},{4,5},{5,4},{6,7},{7,6},{8,9},{9,8},{10,11... | collective-permute-start | bytes 393224 | tf_op jit(solution)/shard_map/ppermute | solution.py:371
  11.2 1.9 %collective-permute-start.1 = (bf16[512,128]{1,0:T(8,128)(2,1)S(1)}, bf16[512,128]{1,0:T(8,128)(2,1)S(1)}, u32[]{:S(2)}, u32[]{:S(2)}) collective-permute-start(bf16[512,128]{1,0:T(8,128)(2,1)S(1)} %get-tuple-element.24), channel_id=1, source_target_pairs={{0,8},{8,0},{16,24},{24,16},{32,40},{40,32},{48,56},{56,48},{64,72... | collective-permute-start | bytes 393224 | tf_op jit(solution)/shard_map/ppermute | solution.py:368
  13.1 8.5 %collective-permute-start.2 = (bf16[512,128]{1,0:T(8,128)(2,1)S(1)}, bf16[512,128]{1,0:T(8,128)(2,1)S(1)}, u32[]{:S(2)}, u32[]{:S(2)}) collective-permute-start(bf16[512,128]{1,0:T(8,128)(2,1)S(1)} %get-tuple-element.25), channel_id=1, source_target_pairs={{0,504},{8,16},{16,8},{24,32},{32,24},{40,48},{48,40},{56,64},{64,... | collective-permute-start | bytes 393224 | tf_op jit(solution)/shard_map/ppermute | solution.py:368
  22.3 0.0 copy-done
  22.3 0.0 copy-start.2
  22.3 1.2 %shard_map.87.near_ref = f32[8,64,128]{2,1,0:T(8,128)S(1)} custom-call(bf16[8,64,128]{2,1,0:T(8,128)(2,1)S(1)} %get-tuple-element.20.z_ref, bf16[32,128,128]{2,1,0:T(8,128)(2,1)S(1)} %copy-done, s32[32]{0:T(128)S(1)} %get-tuple-element.21.col_ref, s32[32]{0:T(128)S(1)} %get-tuple-element.22.tgt_ref, s32[1]{0:T(128)S(6)} %copy.11.count_ref), custom_call_target="tpu_custom_call" | custom-call | tf_op jit(solution)/shard_map/pallas_call | solution.py:348
  23.5 0.0 collective-permute-done.part_ref
  23.5 0.0 copy-done.2
  23.5 0.0 copy-start.1
  23.6 0.5 shard_map.88.near_ref
  24.1 0.0 collective-permute-done.1.inner_ref.pay_inner_ref
  24.1 1.1 %collective-permute-done.2.outer_ref.pay_outer_ref = bf16[512,128]{1,0:T(8,128)(2,1)S(1)} collective-permute-done((bf16[512,128]{1,0:T(8,128)(2,1)S(1)}, bf16[512,128]{1,0:T(8,128)(2,1)S(1)}, u32[]{:S(2)}, u32[]{:S(2)}) %collective-permute-start.2) | collective-permute-done | bytes 131104 | tf_op jit(solution)/shard_map/ppermute | solution.py:368
  25.2 0.0 copy-done.1
  25.2 0.8 shard_map.89
  26.0 2.8 %collective-permute-start.3 = (bf16[8,128,128]{2,1,0:T(8,128)(2,1)S(1)}, bf16[8,128,128]{2,1,0:T(8,128)(2,1)S(1)}, u32[]{:S(2)}, u32[]{:S(2)}) collective-permute-start(bf16[8,128,128]{2,1,0:T(8,128)(2,1)S(1)} %get-tuple-element.26.z_ref), channel_id=1, source_target_pairs={{0,1},{1,0},{2,3},{3,2},{4,5},{5,4},{6,7},{7,6},{8,9},{9,8},{10,11... | collective-permute-start | bytes 786440 | tf_op jit(solution)/shard_map/ppermute | solution.py:371
  28.8 1.9 %collective-permute-start.4 = (bf16[64,256]{1,0:T(8,128)(2,1)S(1)}, bf16[64,256]{1,0:T(8,128)(2,1)S(1)}, u32[]{:S(2)}, u32[]{:S(2)}) collective-permute-start(bf16[64,256]{1,0:T(8,128)(2,1)S(1)} %get-tuple-element.28), channel_id=1, source_target_pairs={{0,8},{8,0},{16,24},{24,16},{32,40},{40,32},{48,56},{56,48},{64,72... | collective-permute-start | bytes 98312 | tf_op jit(solution)/shard_map/ppermute | solution.py:368
  30.7 6.7 %collective-permute-start.5 = (bf16[64,256]{1,0:T(8,128)(2,1)S(1)}, bf16[64,256]{1,0:T(8,128)(2,1)S(1)}, u32[]{:S(2)}, u32[]{:S(2)}) collective-permute-start(bf16[64,256]{1,0:T(8,128)(2,1)S(1)} %get-tuple-element.29), channel_id=1, source_target_pairs={{0,504},{8,16},{16,8},{24,32},{32,24},{40,48},{48,40},{56,64},{64,... | collective-permute-start | bytes 98312 | tf_op jit(solution)/shard_map/ppermute | solution.py:368
  37.4 1.5 %shard_map.90.near_ref = f32[8,64,128]{2,1,0:T(8,128)S(1)} custom-call(bf16[8,128,128]{2,1,0:T(8,128)(2,1)S(1)} %get-tuple-element.26.z_ref, bf16[32,128,128]{2,1,0:T(8,128)(2,1)S(1)} %copy-done, s32[32]{0:T(128)S(1)} %get-tuple-element.21.col_ref, s32[32]{0:T(128)S(1)} %get-tuple-element.22.tgt_ref, s32[1]{0:T(128)S(6)} %copy.11.count_ref), custom_call_target="tpu_custom_call" | custom-call | tf_op jit(solution)/shard_map/pallas_call | solution.py:348
  38.9 0.0 collective-permute-done.3.part_ref
  39.0 0.5 shard_map.91.near_ref
  39.4 0.0 collective-permute-done.4.inner_ref
  39.4 0.0 collective-permute-done.5.outer_ref
  39.4 0.8 shard_map.92
  40.3 2.3 %collective-permute-start.6 = (bf16[8,64,128]{2,1,0:T(8,128)(2,1)S(1)}, bf16[8,64,128]{2,1,0:T(8,128)(2,1)S(1)}, u32[]{:S(2)}, u32[]{:S(2)}) collective-permute-start(bf16[8,64,128]{2,1,0:T(8,128)(2,1)S(1)} %get-tuple-element.35), channel_id=1, source_target_pairs={{0,1},{1,0},{2,3},{3,2},{4,5},{5,4},{6,7},{7,6},{8,9},{9,8},{10,11... | collective-permute-start | bytes 393224 | tf_op jit(solution)/shard_map/ppermute | solution.py:371
  42.6 1.9 %collective-permute-start.7 = (bf16[64,256]{1,0:T(8,128)(2,1)S(1)}, bf16[64,256]{1,0:T(8,128)(2,1)S(1)}, u32[]{:S(2)}, u32[]{:S(2)}) collective-permute-start(bf16[64,256]{1,0:T(8,128)(2,1)S(1)} %get-tuple-element.36), channel_id=1, source_target_pairs={{0,8},{8,16},{16,24},{24,32},{32,40},{40,48},{48,56},{56,64},{64,7... | collective-permute-start | bytes 98312 | tf_op jit(solution)/shard_map/ppermute | solution.py:368
  44.5 1.8 %shard_map.93 = (bf16[128,256]{1,0:T(8,128)(2,1)S(1)}, f32[64,128]{1,0:T(8,128)S(1)}, bf16[128,1024]{1,0:T(8,128)(2,1)S(1)}) custom-call(f32[64,1024]{1,0:T(8,128)S(1)} %get-tuple-element.30.y_ref, bf16[8,128,128]{2,1,0:T(8,128)(2,1)S(1)} %get-tuple-element.31.z_ref, f32[1,1024]{1,0:T(1,128)S(1)} %get-tuple-element.23.dinv_ref, ...), custom_call_target="tpu_custom_call" | custom-call | tf_op jit(solution)/shard_map/pallas_call | solution.py:348
  46.3 0.0 collective-permute-done.6.part_ref
  46.4 0.8 shard_map.94.sums_ref
  47.2 3.4 %collective-permute-done.7.prev_ref = bf16[64,256]{1,0:T(8,128)(2,1)S(1)} collective-permute-done((bf16[64,256]{1,0:T(8,128)(2,1)S(1)}, bf16[64,256]{1,0:T(8,128)(2,1)S(1)}, u32[]{:S(2)}, u32[]{:S(2)}) %collective-permute-start.7) | collective-permute-done | bytes 32800 | tf_op jit(solution)/shard_map/ppermute | solution.py:368
  50.6 0.3 shard_map.95
  50.9 13.0 %all_to_all.15 = f32[32,2,128]{2,1,0:T(2,128)S(1)} all-to-all(f32[32,2,128]{2,1,0:T(2,128)S(1)} %shard_map.95), channel_id=1, replica_groups={{0,1,2,3,4,5,6,7,8,9,10,11,12,13,14,15,16,17,18,19,20,21,22,23,24,25,26..., dimensions={0} | all-to-all | bytes 65536 | tf_op jit(solution)/shard_map/all_to_all | solution.py:496
  63.9 20.0 %all_to_all.16 = f32[16,2,128]{2,1,0:T(2,128)S(1)} all-to-all(f32[16,2,128]{2,1,0:T(2,128)S(1)} %broadcast_in_dim.4), channel_id=1, replica_groups={{0,32,64,96,128,160,192,224,256,288,320,352,384,416,448,480},{8,40,72,1..., dimensions={0} | all-to-all | bytes 32768 | tf_op jit(solution)/shard_map/all_to_all | solution.py:498
  84.0 12.1 %all_to_all.17.both_ref = f32[32,2,128]{2,1,0:T(2,128)S(1)} all-to-all(f32[32,2,128]{2,1,0:T(2,128)S(1)} %broadcast_in_dim.5), channel_id=1, replica_groups={{0,1,2,3,4,5,6,7,8,9,10,11,12,13,14,15,16,17,18,19,20,21,22,23,24,25,26..., dimensions={0} | all-to-all | bytes 65536 | tf_op jit(solution)/shard_map/all_to_all | solution.py:500
  96.1 2.8 %shard_map.96 = (f32[64,1024]{1,0:T(8,128)}, f32[64,64]{1,0:T(8,128)}) custom-call(f32[32,2,128]{2,1,0:T(2,128)S(1)} %all_to_all.17.both_ref, bf16[128,1024]{1,0:T(8,128)(2,1)S(1)} %get-tuple-element.37.parts_ref), custom_call_target="tpu_custom_call" | custom-call | tf_op jit(solution)/shard_map/pallas_call | solution.py:348
  (4 shorter events, 0.1 us)
Async XLA Ops:
  0.6 21.6 %copy-start = (bf16[32,128,128]{2,1,0:T(8,128)(2,1)S(1)}, bf16[32,128,128]{2,1,0:T(8,128)(2,1)}, u32[]{:S(2)}) copy-start(bf16[32,128,128]{2,1,0:T(8,128)(2,1)} %blocks_ref.9) | copy-start | bytes 3145732
  2.4 21.1 %collective-permute-start = (bf16[8,64,128]{2,1,0:T(8,128)(2,1)S(1)}, bf16[8,64,128]{2,1,0:T(8,128)(2,1)S(1)}, u32[]{:S(2)}, u32[]{:S(2)}) collective-permute-start(bf16[8,64,128]{2,1,0:T(8,128)(2,1)S(1)} %get-tuple-element.20.z_ref), channel_id=1, source_target_pairs={{0,1},{1,0},{2,3},{3,2},{4,5},{5,4},{6,7},{7,6},{8,9},{9,8},{10,11... | collective-permute-start | bytes 393224 | tf_op jit(solution)/shard_map/ppermute | solution.py:371
  11.2 12.9 %collective-permute-start.1 = (bf16[512,128]{1,0:T(8,128)(2,1)S(1)}, bf16[512,128]{1,0:T(8,128)(2,1)S(1)}, u32[]{:S(2)}, u32[]{:S(2)}) collective-permute-start(bf16[512,128]{1,0:T(8,128)(2,1)S(1)} %get-tuple-element.24), channel_id=1, source_target_pairs={{0,8},{8,0},{16,24},{24,16},{32,40},{40,32},{48,56},{56,48},{64,72... | collective-permute-start | bytes 393224 | tf_op jit(solution)/shard_map/ppermute | solution.py:368
  13.1 12.1 %collective-permute-start.2 = (bf16[512,128]{1,0:T(8,128)(2,1)S(1)}, bf16[512,128]{1,0:T(8,128)(2,1)S(1)}, u32[]{:S(2)}, u32[]{:S(2)}) collective-permute-start(bf16[512,128]{1,0:T(8,128)(2,1)S(1)} %get-tuple-element.25), channel_id=1, source_target_pairs={{0,504},{8,16},{16,8},{24,32},{32,24},{40,48},{48,40},{56,64},{64,... | collective-permute-start | bytes 393224 | tf_op jit(solution)/shard_map/ppermute | solution.py:368
  22.3 1.3 %copy-start.2 = (s32[1024]{0:T(1024)S(1)}, s32[1024]{0:T(1024)}, u32[]{:S(2)}) copy-start(s32[1024]{0:T(1024)} %param.12) | copy-start | bytes 12292
  23.5 1.6 %copy-start.1 = (f32[64,1024]{1,0:T(8,128)S(1)}, f32[64,1024]{1,0:T(8,128)}, u32[]{:S(2)}) copy-start(f32[64,1024]{1,0:T(8,128)} %v_ref.1) | copy-start | bytes 786436
  26.0 12.9 %collective-permute-start.3 = (bf16[8,128,128]{2,1,0:T(8,128)(2,1)S(1)}, bf16[8,128,128]{2,1,0:T(8,128)(2,1)S(1)}, u32[]{:S(2)}, u32[]{:S(2)}) collective-permute-start(bf16[8,128,128]{2,1,0:T(8,128)(2,1)S(1)} %get-tuple-element.26.z_ref), channel_id=1, source_target_pairs={{0,1},{1,0},{2,3},{3,2},{4,5},{5,4},{6,7},{7,6},{8,9},{9,8},{10,11... | collective-permute-start | bytes 786440 | tf_op jit(solution)/shard_map/ppermute | solution.py:371
  28.8 10.6 %collective-permute-start.4 = (bf16[64,256]{1,0:T(8,128)(2,1)S(1)}, bf16[64,256]{1,0:T(8,128)(2,1)S(1)}, u32[]{:S(2)}, u32[]{:S(2)}) collective-permute-start(bf16[64,256]{1,0:T(8,128)(2,1)S(1)} %get-tuple-element.28), channel_id=1, source_target_pairs={{0,8},{8,0},{16,24},{24,16},{32,40},{40,32},{48,56},{56,48},{64,72... | collective-permute-start | bytes 98312 | tf_op jit(solution)/shard_map/ppermute | solution.py:368
  30.7 8.7 %collective-permute-start.5 = (bf16[64,256]{1,0:T(8,128)(2,1)S(1)}, bf16[64,256]{1,0:T(8,128)(2,1)S(1)}, u32[]{:S(2)}, u32[]{:S(2)}) collective-permute-start(bf16[64,256]{1,0:T(8,128)(2,1)S(1)} %get-tuple-element.29), channel_id=1, source_target_pairs={{0,504},{8,16},{16,8},{24,32},{32,24},{40,48},{48,40},{56,64},{64,... | collective-permute-start | bytes 98312 | tf_op jit(solution)/shard_map/ppermute | solution.py:368
  40.3 6.1 %collective-permute-start.6 = (bf16[8,64,128]{2,1,0:T(8,128)(2,1)S(1)}, bf16[8,64,128]{2,1,0:T(8,128)(2,1)S(1)}, u32[]{:S(2)}, u32[]{:S(2)}) collective-permute-start(bf16[8,64,128]{2,1,0:T(8,128)(2,1)S(1)} %get-tuple-element.35), channel_id=1, source_target_pairs={{0,1},{1,0},{2,3},{3,2},{4,5},{5,4},{6,7},{7,6},{8,9},{9,8},{10,11... | collective-permute-start | bytes 393224 | tf_op jit(solution)/shard_map/ppermute | solution.py:371
  42.6 8.0 %collective-permute-start.7 = (bf16[64,256]{1,0:T(8,128)(2,1)S(1)}, bf16[64,256]{1,0:T(8,128)(2,1)S(1)}, u32[]{:S(2)}, u32[]{:S(2)}) collective-permute-start(bf16[64,256]{1,0:T(8,128)(2,1)S(1)} %get-tuple-element.36), channel_id=1, source_target_pairs={{0,8},{8,16},{16,24},{24,32},{32,40},{40,48},{48,56},{56,64},{64,7... | collective-permute-start | bytes 98312 | tf_op jit(solution)/shard_map/ppermute | solution.py:368
